TPU v7x, 32 devices: a whole 2x2x4 slice. The times are simulated.
32 devices in a mesh: member: 8 (over z, core), band: 4 (over y, x).
Axes of the slice: x: 2, y: 2, z: 4, core: 2. Of those that a mesh axis runs over, the one named last changes fastest.
Arguments:
- states: bfloat16 [16, 84, 64, 128], P('member', None, 'band'), may hold values from -6 to 6
- noise_field: float32 [16, 84, 64, 128], P('member', None, 'band'), may hold values from -3 to 3
- target: bfloat16 [84, 64, 128], P(None, 'band'), may hold values from -6 to 6
- w_conv: bfloat16 [512, 756], replicated, may hold values from -0.21875 to 0.21875
- w_proj: bfloat16 [84, 512], replicated, may hold values from -0.25 to 0.25
- matchings: int32 [4, 16], replicated, may hold values from 0 to 15, each once within a row
Outputs:
- grad_states: bfloat16 [16, 84, 64, 128], P('member', None, 'band')
- grad_conv: float32 [512, 756], P(('member', 'band'))
- grad_proj: float32 [84, 512], P(None, ('member', 'band'))
Inputs may be any that keep to these rules, and one draw needn't show every extreme that they name: `matchings`: each row is a permutation of the 16 member numbers.
All inputs are finite; a program needn't handle non-finite values.
Results may differ from a plain program's by a relative error of at most 0.0075.
Values may be sent and summed in bfloat16 or wider, within the bound.
No kernel may reach another device: no remote copies, remote signals or barrier semaphores. Data moves between devices by JAX's collectives and lax.ppermute only.
A program may use at most 128 MiB of HBM per device.

v0:
```python
import jax
import jax.numpy as jnp
from jax import lax
from jax.sharding import PartitionSpec as P

SQRT_HALF = 0.7071067811865476
INV_ROOT_TWO_PI = 0.3989422804014327


def extended_2(block, sides, width):
    for axis, dim in sides:
        count = lax.axis_size(axis)
        forward = [(i, i + 1) for i in range(count - 1)]
        backward = [(target, source) for source, target in forward]
        low = lax.ppermute(
            lax.slice_in_dim(block, block.shape[dim] - width, None, axis=dim), axis, forward
        )
        high = lax.ppermute(lax.slice_in_dim(block, 0, width, axis=dim), axis, backward)
        block = jnp.concatenate([low, block, high], axis=dim)
    return block


def gelu_slope(preact):
    return (
        0.5 * (1.0 + lax.erf(preact * SQRT_HALF))
        + preact * jnp.exp(-0.5 * preact * preact) * INV_ROOT_TWO_PI
    )


def group_table(lon_cols):
    col_ids = jnp.arange(lon_cols, dtype=jnp.int32)[:, None] // 4
    grp_ids = jnp.arange(lon_cols // 4, dtype=jnp.int32)[None, :]
    return (col_ids == grp_ids).astype(jnp.float32)


def native_grad(differ, table):
    mem_dev, channels, lat_rows, lon_cols = differ.shape
    blocks = differ.reshape(mem_dev, channels, lat_rows // 8, 8, lon_cols)
    row_sums = jnp.sum(blocks * blocks, axis=(1, 3))
    patch_sums = jnp.einsum("mrc,cg->mrg", row_sums, table, precision=lax.Precision.HIGHEST)
    scales = lax.rsqrt(patch_sums / (32.0 * channels) + 1e-06)
    spread = jnp.einsum("mrg,cg->mrc", scales, table, precision=lax.Precision.HIGHEST)
    return (blocks * spread[:, None, :, None, :]).reshape(mem_dev, channels, lat_rows, lon_cols)


def on_device(states, noise_field, target, w_conv, w_proj, matchings):
    mem_dev, channels, lat_rows, lon_cols = states.shape
    hid_width = w_conv.shape[0]
    count = matchings.shape[0]
    inputs_bf = (states.astype(jnp.float32) + noise_field).astype(jnp.bfloat16)
    extended = extended_2(inputs_bf, (("band", 2),), 1)
    extended = jnp.pad(extended, ((0, 0), (0, 0), (0, 0), (1, 1)))
    pieces = [
        extended[:, :, row_off : row_off + lat_rows, col_off : col_off + lon_cols]
        for row_off in range(3)
        for col_off in range(3)
    ]
    columns = jnp.stack(pieces, axis=1).reshape(mem_dev, 9 * channels, lat_rows * lon_cols)
    preact = jnp.einsum("hk,mkp->mhp", w_conv, columns, preferred_element_type=jnp.float32)
    hidden = jax.nn.gelu(preact, approximate=False).astype(jnp.bfloat16)
    outputs = inputs_bf.astype(jnp.float32).reshape(mem_dev, channels, -1) + jnp.einsum(
        "vh,mhp->mvp", w_proj, hidden, preferred_element_type=jnp.float32
    )
    predicted = outputs.astype(jnp.bfloat16).reshape(mem_dev, channels, lat_rows, lon_cols)
    own_native = predicted.astype(jnp.float32)
    table = group_table(lon_cols)
    truth_term = native_grad(own_native - target.astype(jnp.float32)[None], table)
    member_count = lax.axis_size("member")
    total_members = mem_dev * member_count
    numbers = jnp.broadcast_to(jnp.arange(total_members, dtype=jnp.int32)[None, :], matchings.shape)
    inverse = (
        jnp.zeros_like(matchings)
        .at[jnp.arange(count, dtype=jnp.int32)[:, None], matchings]
        .set(numbers)
    )
    everyone = lax.all_gather(predicted, "member", axis=0, tiled=True)
    member_ids = lax.axis_index("member") * mem_dev + jnp.arange(mem_dev, dtype=jnp.int32)
    pair_sum = jnp.zeros_like(own_native)
    for match in range(count):
        for lookup in (matchings, inverse):
            wanted = lookup[match][member_ids]
            partner = jnp.stack(
                [
                    lax.dynamic_index_in_dim(everyone, wanted[slot], 0, keepdims=False)
                    for slot in range(mem_dev)
                ],
                axis=0,
            ).astype(jnp.float32)
            pair_sum = pair_sum + native_grad(own_native - partner, table)
    grad_native = (truth_term - pair_sum / (2.0 * count)).astype(jnp.bfloat16)
    grad_pred = grad_native.reshape(mem_dev, channels, -1)
    dhidden = jnp.einsum("vh,mvp->mhp", w_proj, grad_pred, preferred_element_type=jnp.float32)
    grad_pre = (dhidden * gelu_slope(preact)).astype(jnp.bfloat16)
    conv_term = jnp.einsum("mhp,mkp->hk", grad_pre, columns, preferred_element_type=jnp.float32)
    proj_term = jnp.einsum("mvp,mhp->vh", grad_pred, hidden, preferred_element_type=jnp.float32)
    grad_ext = extended_2(
        grad_pre.reshape(mem_dev, hid_width, lat_rows, lon_cols), (("band", 2),), 1
    )
    dcolumns = jnp.einsum("hk,mhrc->mkrc", w_conv, grad_ext, preferred_element_type=jnp.float32)
    dcolumns = dcolumns.reshape(mem_dev, 9, channels, lat_rows + 2, lon_cols)
    dpadded = jnp.pad(dcolumns, ((0, 0), (0, 0), (0, 0), (0, 0), (1, 1)))
    dinput = jnp.zeros((mem_dev, channels, lat_rows, lon_cols), jnp.float32)
    for row_off in range(3):
        for col_off in range(3):
            dinput = (
                dinput
                + dpadded[
                    :,
                    row_off * 3 + col_off,
                    :,
                    2 - row_off : 2 - row_off + lat_rows,
                    2 - col_off : 2 - col_off + lon_cols,
                ]
            )
    grad_states = (grad_native.astype(jnp.float32) + dinput).astype(jnp.bfloat16)
    weight_sums = (
        lax.psum_scatter(conv_term, ("member", "band"), scatter_dimension=0, tiled=True),
        lax.psum_scatter(proj_term, ("member", "band"), scatter_dimension=1, tiled=True),
    )
    positions = mem_dev * lat_rows * lon_cols * lax.axis_size("member") * lax.axis_size("band")
    factor = 1.0 / positions**0.5
    return (grad_states, weight_sums[0] * factor, weight_sums[1] * factor)


def solution(mesh):
    return jax.shard_map(
        on_device,
        mesh=mesh,
        in_specs=(
            P("member", None, "band", None),
            P("member", None, "band", None),
            P(None, "band", None),
            P(),
            P(),
            P(),
        ),
        out_specs=(
            P("member", None, "band", None),
            P(("member", "band"), None),
            P(None, ("member", "band")),
        ),
        check_vma=False,
    )
```

profile of v0, /device:TPU:0, one launch (start us, length us, event | category | flops | bytes accessed | tf_op | source)
XLA Modules:
  0.0 410.4 jit_solution(5981249292538346972)
XLA Ops:
  7.2 1.7 add_convert_fusion
  9.1 4.9 %collective-permute-start = (bf16[2,84,1,128]{3,2,1,0:T(2,128)(2,1)S(1)}, bf16[2,84,1,128]{3,2,1,0:T(2,128)(2,1)S(1)}, u32[]{:S(2)}, u32[]{:S(2)}) collective-permute-start(bf16[2,84,1,128]{3,2,1,0:T(2,128)(2,1)S(1)} %get-tuple-element.30), channel_id=1, source_target_pairs={{0,1},{1,2},{2,3},{4,5},{5,6},{6,7},{8,9},{9,10},{10,11},{12,13},{... | collective-permute-start | bytes 129032 | tf_op jit(solution)/shard_map/ppermute | solution.py:15
  14.0 1.3 collective-permute-start.1
  16.0 4.3 %collective-permute-done.1 = bf16[2,84,1,128]{3,2,1,0:T(2,128)(2,1)S(1)} collective-permute-done((bf16[2,84,1,128]{3,2,1,0:T(2,128)(2,1)S(1)}, bf16[2,84,1,128]{3,2,1,0:T(2,128)(2,1)S(1)}, u32[]{:S(2)}, u32[]{:S(2)}) %collective-permute-start.1) | collective-permute-done | bytes 43040 | tf_op jit(solution)/shard_map/ppermute | solution.py:18
  20.4 1.8 fusion.35
  23.4 0.8 fusion.94
  25.0 0.8 fusion.90
  25.8 3.7 copy.42
  29.5 6.4 %reshape.271 = bf16[2,756,2048]{2,1,0:T(8,128)(2,1)} reshape(bf16[2,9,84,16,128]{4,3,2,1,0:T(8,128)(2,1)} %copy.42) | data formatting | bytes 12386304 | tf_op jit(solution)/shard_map/reshape | solution.py:58
  35.9 23.9 %fusion.2 = (bf16[2,512,2048]{1,2,0:T(8,128)(2,1)S(1)}, f32[2,2048,512]{2,1,0:T(8,128)}) fusion(bf16[2,756,2048]{2,1,0:T(8,128)(2,1)} %reshape.271, bf16[512,756]{0,1:T(8,128)(2,1)S(1)} %copy-done), kind=kOutput, calls=%fused_computation.19 | convolution fusion | flops 3307208704 | bytes 19550208 | tf_op jit(solution)/shard_map/hk,mkp->mhp/dot_general | solution.py:59
  59.8 2.0 copy-done.1
  61.8 1.4 fusion.30
  63.2 1.2 reshape.272
  64.6 3.7 scatter_fusion
  68.4 0.6 gather_fusion.1
  69.0 0.6 fusion.163
  72.2 0.6 gather_fusion.3
  72.8 0.7 fusion.161
  76.1 0.6 gather_fusion.5
  76.7 0.6 fusion.159
  79.8 0.6 gather_fusion.7
  80.5 0.6 fusion.157
  83.7 0.6 gather_fusion
  84.3 0.7 fusion.164
  87.5 0.6 gather_fusion.2
  91.2 0.6 gather_fusion.4
  91.8 0.7 fusion.160
  95.1 0.6 gather_fusion.6
  95.8 0.6 fusion.158
  109.4 14.5 %all-gather.2.cloned.1.call-done = bf16[16,84,16,128]{3,2,1,0:T(8,128)(2,1)} async-done(((bf16[2,84,16,128]{3,2,1,0:T(8,128)(2,1)}), bf16[16,84,16,128]{3,2,1,0:T(8,128)(2,1)}) %all-gather.2.cloned.1.call-update) | async-done | bytes 5505040 | tf_op jit(solution)/shard_map/all_gather | solution.py:76
  123.9 4.9 %constant_dynamic-slice_fusion.1 = (bf16[1,84,16,128]{3,2,1,0:T(8,128)(2,1)}, bf16[1,84,16,128]{3,2,1,0:T(8,128)(2,1)}, bf16[1,84,16,128]{3,2,1,0:T(8,128)(2,1)}...) fusion(bf16[16,84,16,128]{3,2,1,0:T(8,128)(2,1)} %all-gather.2., ...), kind=kLoop, calls=%fused_computation.258 | loop fusion | bytes 11010112 | tf_op jit(solution)/shard_map/jit(dynamic_index_in_dim)/dynamic_slice | solution.py:84
  129.7 1.2 stack.133
  130.9 1.9 stack.134
  132.8 1.9 stack.137
  134.7 1.9 stack.138
  136.6 1.9 stack.141
  138.5 1.9 stack.142
  140.4 1.9 stack.145
  142.3 1.9 stack.146
  144.2 1.9 stack.149
  146.0 1.9 stack.150
  147.9 1.9 stack.153
  149.8 1.9 stack.154
  151.7 1.9 stack.157
  153.6 1.9 stack.158
  155.6 4.1 %fusion.38 = (f32[2,2048]{1,0:T(2,128)S(1)}, f32[2,2048]{1,0:T(2,128)S(1)}, f32[2,2048]{1,0:T(2,128)S(1)}, f32[2,2048]{1,0:T(2,128)S(1)}, f32[2,2048]{1,0:T(2,12...) fusion(bf16[2,84,2048]{2,1,0:T(8,128)(2,1)S(1)} %fusion.30, ...), kind=kLoop, calls=%fused_computation.87 | loop fusion | flops 15101952 | bytes 7028736 | tf_op jit(solution)/shard_map/reduce_sum | solution.py:39
  163.0 1.9 fusion.40
  164.9 0.9 copy-done.35
  165.8 2.5 convolution_bitcast_fusion.3
  168.3 8.2 %fusion.8 = bf16[2,512,2048]{1,2,0:T(8,128)(2,1)} fusion(f32[2,2048,512]{2,1,0:T(8,128)} %get-tuple-element.75, bf16[2,84,2048]{2,1,0:T(8,128)(2,1)} %copy-done.35, bf16[84,512]{1,0:T(8,128)(2,1)S(1)} %copy-done.38), kind=kOutput, calls=%fused_computation.25 | convolution fusion | flops 373293056 | bytes 13357056 | tf_op jit(solution)/shard_map/vh,mvp->mhp/dot_general | solution.py:92
  176.5 6.2 %copy.44 = bf16[2,512,16,128]{3,1,2,0:T(8,128)(2,1)} copy(bf16[2,512,16,128]{1,3,2,0:T(8,128)(2,1)} %bitcast.343) | data formatting | bytes 8388608 | tf_op jit(solution)/shard_map/reshape | solution.py:97
  182.7 1.1 fusion.155
  183.7 3.4 collective-permute-start.2
  187.1 1.7 collective-permute-start.3
  188.8 8.7 %convolution_bitcast_fusion.2 = f32[512,756]{1,0:T(8,128)} fusion(bf16[2,512,2048]{1,2,0:T(8,128)(2,1)} %fusion.8, bf16[2,756,2048]{2,1,0:T(8,128)(2,1)} %reshape.271), kind=kOutput, calls=%fused_computation.86 | convolution fusion | flops 3170893824 | bytes 11935744 | tf_op jit(solution)/shard_map/mhp,mkp->hk/dot_general | solution.py:94
  197.7 3.3 collective-permute-done.3
  201.0 11.0 %convolution_bitcast_fusion = f32[2,756,18,128]{3,1,2,0:T(8,128)} fusion(bf16[2,512,1,128]{3,1,2,0:T(8,128)(2,1)S(1)} %collective-permute-done.3, bf16[2,512,16,128]{3,1,2,0:T(8,128)(2,1)} %copy.44, bf16[2,512,1,128]{3,1,2,0:T(8,128)(2,1)S(1)} %collective-permute-done.2, bf16[512,756]{0,1:T(8,128)(2,1)S(1)} %copy-done), kind=kOutput, calls=%fused_computation.51 | convolution fusion | flops 3571974144 | bytes 19427328 | tf_op jit(solution)/shard_map/hk,mhrc->mkrc/dot_general | solution.py:99
  212.0 14.2 %reshape.274 = f32[2,9,84,18,128]{4,2,1,3,0:T(8,128)} reshape(f32[2,756,18,128]{3,1,2,0:T(8,128)} %convolution_bitcast_fusion) | data formatting | bytes 27869184 | tf_op jit(solution)/shard_map/reshape | solution.py:100
  226.4 9.5 %copy.47 = f32[2,9,84,18,128]{4,3,2,0,1:T(8,128)S(1)} copy(f32[2,9,84,18,128]{4,2,1,3,0:T(8,128)} %reshape.274) | data formatting | bytes 27869184 | tf_op jit(solution)/shard_map/reshape | solution.py:100
  236.0 4.1 %fusion.68 = bf16[2,84,16,128]{3,2,1,0:T(8,128)(2,1)} fusion(f32[2,9,84,18,128]{4,3,2,0,1:T(8,128)S(1)} %copy.47, bf16[2,84,16,128]{3,2,1,0:T(8,128)(2,1)S(1)} %copy-done.3, bf16[1,84,16,128]{3,2,1,0:T(8,128)(2,1)S(1)} %copy-done.32, bf16[1,84,16,128]{3,2,1,0:T(8,128)(2,1)S(1)} %copy-done.34, bf16[1,84,16,128]{3,2,1,0:T(8,128)(2,1)S(1)} %copy-done.29, ...), kind=kLoop, calls=%fused_computation.126 | loop fusion | flops 19267584 | bytes 30425088 | tf_op jit(solution)/shard_map/convert_element_type | solution.py:115
  240.1 62.6 %reduce-scatter.5.cloned.1.call-done = f32[84,16]{0,1:T(8,128)} async-done(((f32[84,512]{0,1:T(8,128)}), f32[84,16]{0,1:T(8,128)}) %reduce-scatter.5.cloned.1.call-update) | async-done | bytes 5392 | tf_op jit(solution)/shard_map/reduce_scatter | solution.py:118
  302.7 1.3 broadcast_multiply_fusion.1
  304.0 98.0 %reduce-scatter.3.cloned.1.call-done = f32[16,756]{1,0:T(8,128)} async-done(((f32[512,756]{1,0:T(8,128)}), f32[16,756]{1,0:T(8,128)}) %reduce-scatter.3.cloned.1.call-update) | async-done | bytes 48400 | tf_op jit(solution)/shard_map/reduce_scatter | solution.py:117
  402.0 1.4 broadcast_multiply_fusion
  (152 shorter events, 8.2 us)
Async XLA Ops:
  7.2 28.7 %copy-start = (bf16[512,756]{0,1:T(8,128)(2,1)S(1)}, bf16[512,756]{0,1:T(8,128)(2,1)}, u32[]{:S(2)}) copy-start(bf16[512,756]{0,1:T(8,128)(2,1)} %param.9) | copy-start | bytes 2322436
  7.2 116.7 %all-gather.2.cloned.1.call-start = ((), (), s32[]{:S(2)}) async-start(), calls=%async_computation.2 | async-start | bytes 6193152 | tf_op jit(solution)/shard_map/all_gather | solution.py:76
  9.1 7.0 %collective-permute-start = (bf16[2,84,1,128]{3,2,1,0:T(2,128)(2,1)S(1)}, bf16[2,84,1,128]{3,2,1,0:T(2,128)(2,1)S(1)}, u32[]{:S(2)}, u32[]{:S(2)}) collective-permute-start(bf16[2,84,1,128]{3,2,1,0:T(2,128)(2,1)S(1)} %get-tuple-element.30), channel_id=1, source_target_pairs={{0,1},{1,2},{2,3},{4,5},{5,6},{6,7},{8,9},{9,10},{10,11},{12,13},{... | collective-permute-start | bytes 129032 | tf_op jit(solution)/shard_map/ppermute | solution.py:15
  14.0 6.4 %collective-permute-start.1 = (bf16[2,84,1,128]{3,2,1,0:T(2,128)(2,1)S(1)}, bf16[2,84,1,128]{3,2,1,0:T(2,128)(2,1)S(1)}, u32[]{:S(2)}, u32[]{:S(2)}) collective-permute-start(bf16[2,84,1,128]{3,2,1,0:T(2,128)(2,1)S(1)} %get-tuple-element.31), channel_id=1, source_target_pairs={{1,0},{2,1},{3,2},{5,4},{6,5},{7,6},{9,8},{10,9},{11,10},{13,12},{... | collective-permute-start | bytes 129032 | tf_op jit(solution)/shard_map/ppermute | solution.py:18
  35.9 25.9 %copy-start.38 = (bf16[84,512]{1,0:T(8,128)(2,1)S(1)}, bf16[84,512]{1,0:T(8,128)(2,1)}, u32[]{:S(2)}) copy-start(bf16[84,512]{1,0:T(8,128)(2,1)} %param.10) | copy-start | bytes 258052
  59.8 2.0 copy-start.1
  61.8 2.7 copy-start.39
  64.4 238.4 %reduce-scatter.5.cloned.1.call-start = ((), (), s32[]{:S(2)}) async-start(), calls=%async_computation.4 | async-start | bytes 270336 | tf_op jit(solution)/shard_map/reduce_scatter | solution.py:118
  64.6 34.3 %copy-start.36 = (bf16[84,16,128]{2,1,0:T(8,128)(2,1)S(1)}, bf16[84,16,128]{2,1,0:T(8,128)(2,1)}, u32[]{:S(2)}) copy-start(bf16[84,16,128]{2,1,0:T(8,128)(2,1)} %param.8) | copy-start | bytes 1032196
  128.8 0.7 copy-start.33
  128.8 0.9 copy-start.31
  155.5 7.3 %copy-start.4 = (bf16[1,84,2048]{2,1,0:T(8,128)(2,1)S(1)}, bf16[1,84,2048]{2,1,0:T(8,128)(2,1)}, u32[]{:S(2)}) copy-start(bf16[1,84,2048]{2,1,0:T(8,128)(2,1)} %stack.134) | copy-start | bytes 1032196
  155.5 7.3 %copy-start.5 = (bf16[1,84,2048]{2,1,0:T(8,128)(2,1)S(1)}, bf16[1,84,2048]{2,1,0:T(8,128)(2,1)}, u32[]{:S(2)}) copy-start(bf16[1,84,2048]{2,1,0:T(8,128)(2,1)} %stack.137) | copy-start | bytes 1032196
  155.5 7.4 %copy-start.6 = (bf16[1,84,2048]{2,1,0:T(8,128)(2,1)S(1)}, bf16[1,84,2048]{2,1,0:T(8,128)(2,1)}, u32[]{:S(2)}) copy-start(bf16[1,84,2048]{2,1,0:T(8,128)(2,1)} %stack.138) | copy-start | bytes 1032196
  155.5 7.4 %copy-start.7 = (bf16[1,84,2048]{2,1,0:T(8,128)(2,1)S(1)}, bf16[1,84,2048]{2,1,0:T(8,128)(2,1)}, u32[]{:S(2)}) copy-start(bf16[1,84,2048]{2,1,0:T(8,128)(2,1)} %stack.141) | copy-start | bytes 1032196
  155.5 7.4 %copy-start.8 = (bf16[1,84,2048]{2,1,0:T(8,128)(2,1)S(1)}, bf16[1,84,2048]{2,1,0:T(8,128)(2,1)}, u32[]{:S(2)}) copy-start(bf16[1,84,2048]{2,1,0:T(8,128)(2,1)} %stack.142) | copy-start | bytes 1032196
  155.5 7.4 %copy-start.9 = (bf16[1,84,2048]{2,1,0:T(8,128)(2,1)S(1)}, bf16[1,84,2048]{2,1,0:T(8,128)(2,1)}, u32[]{:S(2)}) copy-start(bf16[1,84,2048]{2,1,0:T(8,128)(2,1)} %stack.145) | copy-start | bytes 1032196
  155.5 7.4 %copy-start.10 = (bf16[1,84,2048]{2,1,0:T(8,128)(2,1)S(1)}, bf16[1,84,2048]{2,1,0:T(8,128)(2,1)}, u32[]{:S(2)}) copy-start(bf16[1,84,2048]{2,1,0:T(8,128)(2,1)} %stack.146) | copy-start | bytes 1032196
  155.5 7.4 %copy-start.11 = (bf16[1,84,2048]{2,1,0:T(8,128)(2,1)S(1)}, bf16[1,84,2048]{2,1,0:T(8,128)(2,1)}, u32[]{:S(2)}) copy-start(bf16[1,84,2048]{2,1,0:T(8,128)(2,1)} %stack.149) | copy-start | bytes 1032196
  155.6 7.4 %copy-start.12 = (bf16[1,84,2048]{2,1,0:T(8,128)(2,1)S(1)}, bf16[1,84,2048]{2,1,0:T(8,128)(2,1)}, u32[]{:S(2)}) copy-start(bf16[1,84,2048]{2,1,0:T(8,128)(2,1)} %stack.150) | copy-start | bytes 1032196
  155.6 7.4 %copy-start.13 = (bf16[1,84,2048]{2,1,0:T(8,128)(2,1)S(1)}, bf16[1,84,2048]{2,1,0:T(8,128)(2,1)}, u32[]{:S(2)}) copy-start(bf16[1,84,2048]{2,1,0:T(8,128)(2,1)} %stack.153) | copy-start | bytes 1032196
  155.6 7.4 %copy-start.14 = (bf16[1,84,2048]{2,1,0:T(8,128)(2,1)S(1)}, bf16[1,84,2048]{2,1,0:T(8,128)(2,1)}, u32[]{:S(2)}) copy-start(bf16[1,84,2048]{2,1,0:T(8,128)(2,1)} %stack.154) | copy-start | bytes 1032196
  155.6 7.4 %copy-start.15 = (bf16[1,84,2048]{2,1,0:T(8,128)(2,1)S(1)}, bf16[1,84,2048]{2,1,0:T(8,128)(2,1)}, u32[]{:S(2)}) copy-start(bf16[1,84,2048]{2,1,0:T(8,128)(2,1)} %stack.157) | copy-start | bytes 1032196
  155.6 7.4 %copy-start.16 = (bf16[1,84,2048]{2,1,0:T(8,128)(2,1)S(1)}, bf16[1,84,2048]{2,1,0:T(8,128)(2,1)}, u32[]{:S(2)}) copy-start(bf16[1,84,2048]{2,1,0:T(8,128)(2,1)} %stack.158) | copy-start | bytes 1032196
  162.8 3.0 copy-start.2
  164.9 0.9 copy-start.35
  168.3 233.8 %reduce-scatter.3.cloned.1.call-start = ((), (), s32[]{:S(2)}) async-start(), calls=%async_computation.3 | async-start | bytes 1622016 | tf_op jit(solution)/shard_map/reduce_scatter | solution.py:117
  183.7 13.9 %collective-permute-start.2 = (bf16[2,512,1,128]{3,1,2,0:T(8,128)(2,1)S(1)}, bf16[2,512,1,128]{3,1,2,0:T(8,128)(2,1)S(1)}, u32[]{:S(2)}, u32[]{:S(2)}) collective-permute-start(bf16[2,512,1,128]{3,1,2,0:T(8,128)(2,1)S(1)} %get-tuple-element.28), channel_id=1, source_target_pairs={{0,1},{1,2},{2,3},{4,5},{5,6},{6,7},{8,9},{9,10},{10,11},{12,13},{... | collective-permute-start | bytes 786440 | tf_op jit(solution)/shard_map/ppermute | solution.py:15
  187.1 10.5 %copy-start.37 = (bf16[84,16,128]{2,1,0:T(8,128)(2,1)S(1)}, bf16[84,16,128]{2,1,0:T(8,128)(2,1)}, u32[]{:S(2)}) copy-start(bf16[84,16,128]{2,1,0:T(8,128)(2,1)} %param.8) | copy-start | bytes 1032196
  187.1 13.8 %collective-permute-start.3 = (bf16[2,512,1,128]{3,1,2,0:T(8,128)(2,1)S(1)}, bf16[2,512,1,128]{3,1,2,0:T(8,128)(2,1)S(1)}, u32[]{:S(2)}, u32[]{:S(2)}) collective-permute-start(bf16[2,512,1,128]{3,1,2,0:T(8,128)(2,1)S(1)} %get-tuple-element.29), channel_id=1, source_target_pairs={{1,0},{2,1},{3,2},{5,4},{6,5},{7,6},{9,8},{10,9},{11,10},{13,12},{... | collective-permute-start | bytes 786440 | tf_op jit(solution)/shard_map/ppermute | solution.py:18
  226.2 9.6 %copy-start.3 = (bf16[2,84,16,128]{3,2,1,0:T(8,128)(2,1)S(1)}, bf16[2,84,16,128]{3,2,1,0:T(8,128)(2,1)}, u32[]{:S(2)}) copy-start(bf16[2,84,16,128]{3,2,1,0:T(8,128)(2,1)} %reshape.272) | copy-start | bytes 2064388
  226.2 9.6 %copy-start.17 = (bf16[1,84,16,128]{3,2,1,0:T(8,128)(2,1)S(1)}, bf16[1,84,16,128]{3,2,1,0:T(8,128)(2,1)}, u32[]{:S(2)}) copy-start(bf16[1,84,16,128]{3,2,1,0:T(8,128)(2,1)} %get-tuple-element.12) | copy-start | bytes 1032196
  226.2 9.6 %copy-start.18 = (bf16[1,84,16,128]{3,2,1,0:T(8,128)(2,1)S(1)}, bf16[1,84,16,128]{3,2,1,0:T(8,128)(2,1)}, u32[]{:S(2)}) copy-start(bf16[1,84,16,128]{3,2,1,0:T(8,128)(2,1)} %get-tuple-element.13) | copy-start | bytes 1032196
  226.2 9.6 %copy-start.19 = (bf16[1,84,16,128]{3,2,1,0:T(8,128)(2,1)S(1)}, bf16[1,84,16,128]{3,2,1,0:T(8,128)(2,1)}, u32[]{:S(2)}) copy-start(bf16[1,84,16,128]{3,2,1,0:T(8,128)(2,1)} %get-tuple-element.14) | copy-start | bytes 1032196
  226.2 9.7 %copy-start.20 = (bf16[1,84,16,128]{3,2,1,0:T(8,128)(2,1)S(1)}, bf16[1,84,16,128]{3,2,1,0:T(8,128)(2,1)}, u32[]{:S(2)}) copy-start(bf16[1,84,16,128]{3,2,1,0:T(8,128)(2,1)} %get-tuple-element.15) | copy-start | bytes 1032196
  226.3 9.7 %copy-start.21 = (bf16[1,84,16,128]{3,2,1,0:T(8,128)(2,1)S(1)}, bf16[1,84,16,128]{3,2,1,0:T(8,128)(2,1)}, u32[]{:S(2)}) copy-start(bf16[1,84,16,128]{3,2,1,0:T(8,128)(2,1)} %get-tuple-element.16) | copy-start | bytes 1032196
  226.3 9.7 %copy-start.22 = (bf16[1,84,16,128]{3,2,1,0:T(8,128)(2,1)S(1)}, bf16[1,84,16,128]{3,2,1,0:T(8,128)(2,1)}, u32[]{:S(2)}) copy-start(bf16[1,84,16,128]{3,2,1,0:T(8,128)(2,1)} %get-tuple-element.17) | copy-start | bytes 1032196
  226.3 9.7 %copy-start.23 = (bf16[1,84,16,128]{3,2,1,0:T(8,128)(2,1)S(1)}, bf16[1,84,16,128]{3,2,1,0:T(8,128)(2,1)}, u32[]{:S(2)}) copy-start(bf16[1,84,16,128]{3,2,1,0:T(8,128)(2,1)} %get-tuple-element.18) | copy-start | bytes 1032196
  226.3 9.7 %copy-start.24 = (bf16[1,84,16,128]{3,2,1,0:T(8,128)(2,1)S(1)}, bf16[1,84,16,128]{3,2,1,0:T(8,128)(2,1)}, u32[]{:S(2)}) copy-start(bf16[1,84,16,128]{3,2,1,0:T(8,128)(2,1)} %get-tuple-element.19) | copy-start | bytes 1032196
  226.3 9.7 %copy-start.25 = (bf16[1,84,16,128]{3,2,1,0:T(8,128)(2,1)S(1)}, bf16[1,84,16,128]{3,2,1,0:T(8,128)(2,1)}, u32[]{:S(2)}) copy-start(bf16[1,84,16,128]{3,2,1,0:T(8,128)(2,1)} %get-tuple-element.20) | copy-start | bytes 1032196
  226.3 9.7 %copy-start.26 = (bf16[1,84,16,128]{3,2,1,0:T(8,128)(2,1)S(1)}, bf16[1,84,16,128]{3,2,1,0:T(8,128)(2,1)}, u32[]{:S(2)}) copy-start(bf16[1,84,16,128]{3,2,1,0:T(8,128)(2,1)} %get-tuple-element.21) | copy-start | bytes 1032196
  226.3 9.7 %copy-start.27 = (bf16[1,84,16,128]{3,2,1,0:T(8,128)(2,1)S(1)}, bf16[1,84,16,128]{3,2,1,0:T(8,128)(2,1)}, u32[]{:S(2)}) copy-start(bf16[1,84,16,128]{3,2,1,0:T(8,128)(2,1)} %get-tuple-element.22) | copy-start | bytes 1032196
  226.3 9.7 %copy-start.28 = (bf16[1,84,16,128]{3,2,1,0:T(8,128)(2,1)S(1)}, bf16[1,84,16,128]{3,2,1,0:T(8,128)(2,1)}, u32[]{:S(2)}) copy-start(bf16[1,84,16,128]{3,2,1,0:T(8,128)(2,1)} %get-tuple-element.23) | copy-start | bytes 1032196
  226.3 9.7 %copy-start.29 = (bf16[1,84,16,128]{3,2,1,0:T(8,128)(2,1)S(1)}, bf16[1,84,16,128]{3,2,1,0:T(8,128)(2,1)}, u32[]{:S(2)}) copy-start(bf16[1,84,16,128]{3,2,1,0:T(8,128)(2,1)} %get-tuple-element.24) | copy-start | bytes 1032196
  226.3 9.7 %copy-start.30 = (bf16[1,84,16,128]{3,2,1,0:T(8,128)(2,1)S(1)}, bf16[1,84,16,128]{3,2,1,0:T(8,128)(2,1)}, u32[]{:S(2)}) copy-start(bf16[1,84,16,128]{3,2,1,0:T(8,128)(2,1)} %get-tuple-element.25) | copy-start | bytes 1032196
  226.4 9.7 %copy-start.32 = (bf16[1,84,16,128]{3,2,1,0:T(8,128)(2,1)S(1)}, bf16[1,84,16,128]{3,2,1,0:T(8,128)(2,1)}, u32[]{:S(2)}) copy-start(bf16[1,84,16,128]{3,2,1,0:T(8,128)(2,1)} %copy-done.31) | copy-start | bytes 1032196
  226.4 9.7 %copy-start.34 = (bf16[1,84,16,128]{3,2,1,0:T(8,128)(2,1)S(1)}, bf16[1,84,16,128]{3,2,1,0:T(8,128)(2,1)}, u32[]{:S(2)}) copy-start(bf16[1,84,16,128]{3,2,1,0:T(8,128)(2,1)} %copy-done.33) | copy-start | bytes 1032196
Sparse Core Ops, SparseCore 0:
  64.5 59.3 all-gather.1
  168.4 134.3 reduce-scatter.4
  308.0 93.9 reduce-scatter.2
where the time goes:
time: 418 us; the launch traced here: 410 us
  waiting for transfers between devices  183 us (44%)
  local copies, waits for them, and re-layouts  94.5 us (23%)
  matrix products  58.3 us (14%)
  between operations  45.7 us (11%)
  other arithmetic  17.4 us (4%)
  starting transfers between devices  11.4 us (3%)
    reduce_scatter x1, waiting for transfers between devices, on_device(): lax.psum_scatter(conv_term, ('member', 'band'), scatter_dimension=0, tile...  98 us
    reduce_scatter x1, waiting for transfers between devices, on_device(): lax.psum_scatter(proj_term, ('member', 'band'), scatter_dimension=1, tile...  62.6 us
    another operation x16, local copies, waits for them, and re-layouts, on_device(): jnp.stack([lax.dynamic_index_in_dim(everyone, wanted[slot], 0, keepdims=F...  26.1 us
    dot_general x1, matrix products, on_device(): jnp.einsum('hk,mkp->mhp', w_conv, columns, preferred_element_type=jnp.flo...  23.9 us
    reshape x2, local copies, waits for them, and re-layouts, on_device(): dcolumns = dcolumns.reshape(mem_dev, 9, channels, lat_rows + 2, lon_cols)  23.7 us
    all_gather x1, waiting for transfers between devices, on_device(): everyone = lax.all_gather(predicted, 'member', axis=0, tiled=True)  14.5 us
    dot_general x1, matrix products, on_device(): jnp.einsum('hk,mhrc->mkrc', w_conv, grad_ext, preferred_element_type=jnp....  11 us
    dot_general x1, matrix products, on_device(): jnp.einsum('mhp,mkp->hk', grad_pre, columns, preferred_element_type=jnp.f...  8.74 us
  transfers between devices with their start and end apart: 7, of which 6 were waited for; matrix products, arithmetic and copies ran while one was open for 19% of the time, Pallas kernels for 0%

commit v1 on v0

v1 whole, which is shorter than its diff:
```python
import functools

import jax
import jax.numpy as jnp
from jax import lax
from jax.experimental import pallas as pl
from jax.experimental.pallas import tpu as pltpu
from jax.sharding import PartitionSpec as P

SQRT_HALF = 0.7071067811865476
INV_ROOT_TWO_PI = 0.3989422804014327
F32 = jnp.float32
BF16 = jnp.bfloat16
LANES = 128
TAPS = 256
VMEM_LIMIT = 60 * 1024 * 1024


def vmem_params(count):
    return pltpu.CompilerParams(
        dimension_semantics=("arbitrary",) * count, vmem_limit_bytes=VMEM_LIMIT
    )


def shift_right(vals):
    lane = lax.broadcasted_iota(jnp.int32, vals.shape, 1)
    return jnp.where(lane == 0, 0.0, pltpu.roll(vals, 1, 1))


def shift_left(vals):
    width = vals.shape[1]
    lane = lax.broadcasted_iota(jnp.int32, vals.shape, 1)
    return jnp.where(lane == width - 1, 0.0, pltpu.roll(vals, width - 1, 1))


def expand_row(vals, scratch):
    channels = vals.shape[0]
    scratch[pl.ds(0, channels), :] = shift_right(vals)
    scratch[pl.ds(channels, channels), :] = vals
    scratch[pl.ds(2 * channels, channels), :] = shift_left(vals)
    return scratch[...].astype(BF16)


def regroup(rows, parts):
    channels, width = rows[0].shape
    size = width // parts
    lane = lax.broadcasted_iota(jnp.int32, (channels, width), 1) // size
    outs = []
    for q in range(parts):
        out = None
        for i in range(parts):
            moved = rows[i]
            shift = (i - q) * size % width
            if shift:
                moved = pltpu.roll(moved, shift, 1)
            out = moved if out is None else jnp.where(lane == i, moved, out)
        outs.append(out)
    return outs


class Sizes:
    def __init__(self, states, w_conv, member_count):
        self.mem, self.ch, self.lat, self.lon = states.shape
        self.hid = w_conv.shape[0]
        self.devs = member_count
        self.prows = self.lat // 8
        self.parts = member_count // self.prows
        self.groups = 8 // self.parts
        self.sub = self.groups * self.ch
        self.subpad = (self.sub + 7) // 8 * 8
        self.pos = self.lat * self.lon


def prep_kernel(sz, states, noise, target, w_conv, e_out, x_out, t_out, w_out, xs, es, ps):
    es[...] = jnp.zeros_like(es)
    x = (states[0].astype(F32) + noise[0]).astype(BF16)
    xs[...] = x.astype(F32).reshape(sz.ch * sz.lat, sz.lon)
    for row in range(sz.lat):
        vals = xs[pl.ds(row, sz.ch, stride=sz.lat), :]
        x_out[0, :, row * sz.lon : (row + 1) * sz.lon] = vals.astype(BF16)
        e_out[0, :, row * sz.lon : (row + 1) * sz.lon] = expand_row(vals, es)

    @pl.when(pl.program_id(0) == 0)
    def _():
        xs[...] = target[...].astype(F32).reshape(sz.ch * sz.lat, sz.lon)
        if sz.subpad > sz.sub:
            ps[...] = jnp.zeros_like(ps)
        for prow in range(sz.prows):
            for group in range(sz.groups):
                first = prow * 8 + group * sz.parts
                rows = [
                    xs[pl.ds(first + i, sz.ch, stride=sz.lat), :] for i in range(sz.parts)
                ]
                for q, out in enumerate(regroup(rows, sz.parts)):
                    ps[q, pl.ds(group * sz.ch, sz.ch), :] = out
            for q in range(sz.parts):
                t_out[prow * sz.parts + q] = ps[q].astype(BF16)

    @pl.when(pl.program_id(0) == sz.mem - 1)
    def _():
        taps = 3 * sz.ch
        for part in range(3):
            w_out[:, part * TAPS : (part + 1) * TAPS] = jnp.concatenate(
                [
                    w_conv[:, part * taps : (part + 1) * taps],
                    jnp.zeros((sz.hid, TAPS - taps), BF16),
                ],
                axis=1,
            )


def forward_kernel(sz, e_in, x_in, halo_up, halo_dn, w3, w_proj, hid_out, slope_out, snd, ext, es, ps):
    width = sz.lon
    prow = pl.program_id(1)

    @pl.when(prow == 0)
    def _():
        es[...] = jnp.zeros_like(es)
        if sz.subpad > sz.sub:
            ps[...] = jnp.zeros_like(ps)
        ext[:, width : width + sz.pos] = e_in[0]
        ext[:, 0:width] = expand_row(halo_up[0, :, 0, :].astype(F32), es)
        ext[:, width + sz.pos :] = expand_row(halo_dn[0, :, 0, :].astype(F32), es)

    base = prow * (8 * width)
    rows = []
    for pair in range(4):
        start = pl.multiple_of(base + pair * 2 * width, width)
        cols = jnp.concatenate(
            [ext[:, pl.ds(pl.multiple_of(start + ro * width, width), 2 * width)] for ro in range(3)],
            axis=0,
        )
        preact = jnp.dot(w3[...], cols, preferred_element_type=F32)
        cdf = 0.5 + 0.5 * lax.erf(preact * SQRT_HALF)
        hidden = (preact * cdf).astype(BF16)
        bell = jnp.exp(preact * preact * (-0.5))
        here = slice(pair * 2 * width, (pair + 1) * 2 * width)
        hid_out[0, :, here] = hidden
        slope_out[0, :, here] = cdf + preact * (bell * INV_ROOT_TWO_PI)
        pred = x_in[0, :, here].astype(F32) + jnp.dot(
            w_proj[...], hidden, preferred_element_type=F32
        )
        pred = pred.astype(BF16).astype(F32)
        rows += [pred[:, :width], pred[:, width:]]
    for group in range(sz.groups):
        outs = regroup(rows[group * sz.parts : (group + 1) * sz.parts], sz.parts)
        for q, out in enumerate(outs):
            ps[q, pl.ds(group * sz.ch, sz.ch), :] = out
    for q in range(sz.parts):
        snd[q, 0] = ps[q].astype(BF16)


def pair_kernel(sz, count, members, match, device, preds, truth, grads, vals, tsc, sums, scale, inv):
    norm = 1.0 / (32.0 * sz.ch)
    vals[...] = preds[...].reshape(members, sz.subpad, LANES).astype(F32)
    tsc[...] = truth[0].astype(F32)
    folds = sz.subpad // 8

    def squares(diff):
        return jnp.sum((diff * diff).reshape(folds, 8, LANES), axis=0)

    def first(m, carry):
        own = vals[m]
        sums[pl.ds(pl.multiple_of((count * members + m) * 8, 8), 8), :] = squares(own - tsc[...])
        for k in range(count):
            other = match[k, m]
            inv[k, other] = m
            at = pl.multiple_of((k * members + m) * 8, 8)
            sums[pl.ds(at, 8), :] = squares(own - vals[other])
        return carry

    lax.fori_loop(0, members, first, 0)
    rows = (count + 1) * members
    total = sums[pl.ds(0, rows, stride=8), :]
    for j in range(1, 8):
        total = total + sums[pl.ds(j, rows, stride=8), :]
    size = sz.lon // sz.parts
    step = size
    while step < LANES:
        total = total + pltpu.roll(total, step, 1)
        step *= 2
    lane = lax.broadcasted_iota(jnp.int32, total.shape, 1)
    for bit in (1, 2):
        total = total + jnp.where(
            (lane & bit) == 0, pltpu.roll(total, LANES - bit, 1), pltpu.roll(total, bit, 1)
        )
    scale[...] = lax.rsqrt(total * norm + 1e-06)

    def second(m, carry):
        own = vals[m]

        def term(other, index):
            return (own - other) * scale[pl.ds(index, 1), :]

        acc = jnp.zeros_like(own)
        for k in range(count):
            acc = acc + term(vals[match[k, m]], k * members + m)
            back = inv[k, m]
            acc = acc + term(vals[back], k * members + back)
        out = term(tsc[...], count * members + m) - acc / (2.0 * count)
        grads[m // sz.mem, m % sz.mem] = out.astype(BF16)
        return carry

    lax.fori_loop(0, members, second, 0)


def weight_kernel(sz, back, hid, slope, e_in, halo_up, halo_dn, w_proj_t, wt3, gp_out, gpre_out, wg_out, edge_out, ext, es, rows_f, acc):
    width = sz.lon
    member = pl.program_id(0)
    es[...] = jnp.zeros_like(es)
    ext[:, width : width + sz.pos] = e_in[0]
    ext[:, 0:width] = expand_row(halo_up[0, :, 0, :].astype(F32), es)
    ext[:, width + sz.pos :] = expand_row(halo_dn[0, :, 0, :].astype(F32), es)
    for prow in range(sz.prows):
        for q in range(sz.parts):
            rows_f[q] = back[prow * sz.parts + q, 0].astype(F32)
        for group in range(sz.groups):
            outs = regroup(
                [rows_f[q, pl.ds(group * sz.ch, sz.ch), :] for q in range(sz.parts)], sz.parts
            )
            for i, out in enumerate(outs):
                row = prow * 8 + group * sz.parts + i
                gp_out[0, :, row * width : (row + 1) * width] = out.astype(BF16)
    zero = jnp.zeros((sz.hid, width), BF16)
    gpre_out[0, :, 0:width] = zero
    gpre_out[0, :, width + sz.pos :] = zero
    for pair in range(sz.lat // 2):
        here = slice(pair * 2 * width, (pair + 1) * 2 * width)
        dhid = jnp.dot(w_proj_t[...], gp_out[0, :, here], preferred_element_type=F32)
        there = slice((pair * 2 + 1) * width, (pair * 2 + 3) * width)
        gpre_out[0, :, there] = (dhid * slope[0, :, here]).astype(BF16)
    gpre = gpre_out[0, :, width : width + sz.pos]
    dims = (((1,), (1,)), ((), ()))
    for ro in range(4):
        if ro < 3:
            term = lax.dot_general(
                gpre, ext[:, ro * width : ro * width + sz.pos], dims, preferred_element_type=F32
            )
            at = slice(ro * TAPS, (ro + 1) * TAPS)
        else:
            term = lax.dot_general(hid[0], gp_out[0], dims, preferred_element_type=F32)
            at = slice(3 * TAPS, 3 * TAPS + sz.ch)

        @pl.when(member == 0)
        def _():
            acc[:, at] = term

        @pl.when(member > 0)
        def _():
            acc[:, at] = acc[:, at] + term

    for side in range(2):
        col = 0 if side == 0 else sz.pos - width
        part = jnp.dot(
            wt3[0 if side == 0 else 2], gpre[:, col : col + width], preferred_element_type=F32
        )
        edge_out[0, side] = fold_taps(part, sz.ch)

    @pl.when(member == sz.mem - 1)
    def _():
        wg_out[:, : 3 * TAPS + sz.ch] = acc[...].astype(BF16)
        wg_out[:, 3 * TAPS + sz.ch :] = jnp.zeros(
            (sz.hid, wg_out.shape[1] - 3 * TAPS - sz.ch), BF16
        )


def fold_taps(part, channels):
    return (
        part[channels : 2 * channels]
        + shift_left(part[0:channels])
        + shift_right(part[2 * channels : 3 * channels])
    )


def data_kernel(sz, gpre, gp, wt3, from_dn, from_up, out, gs):
    width = sz.lon
    for pair in range(sz.lat // 2):
        part = None
        for ro in range(3):
            start = (pair * 2 + 2 - ro) * width
            term = jnp.dot(
                wt3[ro], gpre[0, :, start : start + 2 * width], preferred_element_type=F32
            )
            part = term if part is None else part + term
        for i in range(2):
            row = pair * 2 + i
            total = gp[0, :, row * width : (row + 1) * width].astype(F32) + fold_taps(
                part[:, i * width : (i + 1) * width], sz.ch
            )
            if row == 0:
                total = total + from_up[0, 0]
            if row == sz.lat - 1:
                total = total + from_dn[0, 0]
            gs[pl.ds(row, sz.ch, stride=sz.lat), :] = total
    out[0] = gs[...].reshape(sz.ch, sz.lat, width).astype(BF16)


def spec(shape, index):
    return pl.BlockSpec(shape, index)


def whole(shape):
    return pl.BlockSpec(shape, lambda *_: (0,) * len(shape))


def on_device(states, noise_field, target, w_conv, w_proj, matchings):
    member_count = lax.axis_size("member")
    band_count = lax.axis_size("band")
    sz = Sizes(states, w_conv, member_count)
    mem, ch, lat, lon, hid, pos = sz.mem, sz.ch, sz.lat, sz.lon, sz.hid, sz.pos
    count = matchings.shape[0]
    members = mem * member_count
    down = [(i, i + 1) for i in range(band_count - 1)]
    up = [(i + 1, i) for i in range(band_count - 1)]

    def edge(row):
        return (
            states[:, :, row : row + 1].astype(F32) + noise_field[:, :, row : row + 1]
        ).astype(BF16)

    halo_up = lax.ppermute(edge(lat - 1), "band", down)
    halo_dn = lax.ppermute(edge(0), "band", up)

    def by_member(*shape):
        return spec((1,) + shape, lambda m, *_: (m,) + (0,) * len(shape))

    e_in, x_in, truth, w3 = pl.pallas_call(
        functools.partial(prep_kernel, sz),
        grid=(mem,),
        in_specs=[
            by_member(ch, lat, lon),
            by_member(ch, lat, lon),
            whole((ch, lat, lon)),
            whole(w_conv.shape),
        ],
        out_specs=[
            by_member(TAPS, pos),
            by_member(ch, pos),
            whole((sz.devs, sz.subpad, LANES)),
            whole((hid, 3 * TAPS)),
        ],
        out_shape=[
            jax.ShapeDtypeStruct((mem, TAPS, pos), BF16),
            jax.ShapeDtypeStruct((mem, ch, pos), BF16),
            jax.ShapeDtypeStruct((sz.devs, sz.subpad, LANES), BF16),
            jax.ShapeDtypeStruct((hid, 3 * TAPS), BF16),
        ],
        scratch_shapes=[
            pltpu.VMEM((ch * lat, lon), F32),
            pltpu.VMEM((TAPS, lon), F32),
            pltpu.VMEM((sz.parts, sz.subpad, LANES), F32),
        ],
        compiler_params=vmem_params(1),
        cost_estimate=pl.CostEstimate(flops=10_000_000, bytes_accessed=8_000_000, transcendentals=0),
        name="prep",
    )(states, noise_field, target, w_conv)

    hidden, slope, snd = pl.pallas_call(
        functools.partial(forward_kernel, sz),
        grid=(mem, sz.prows),
        in_specs=[
            spec((1, TAPS, pos), lambda m, p: (m, 0, 0)),
            spec((1, ch, 8 * lon), lambda m, p: (m, 0, p)),
            spec((1, ch, 1, lon), lambda m, p: (m, 0, 0, 0)),
            spec((1, ch, 1, lon), lambda m, p: (m, 0, 0, 0)),
            whole((hid, 3 * TAPS)),
            whole(w_proj.shape),
        ],
        out_specs=[
            spec((1, hid, 8 * lon), lambda m, p: (m, 0, p)),
            spec((1, hid, 8 * lon), lambda m, p: (m, 0, p)),
            spec((sz.parts, 1, sz.subpad, LANES), lambda m, p: (p, m, 0, 0)),
        ],
        out_shape=[
            jax.ShapeDtypeStruct((mem, hid, pos), BF16),
            jax.ShapeDtypeStruct((mem, hid, pos), F32),
            jax.ShapeDtypeStruct((sz.devs, mem, sz.subpad, LANES), BF16),
        ],
        scratch_shapes=[
            pltpu.VMEM((TAPS, pos + 2 * lon), BF16),
            pltpu.VMEM((TAPS, lon), F32),
            pltpu.VMEM((sz.parts, sz.subpad, LANES), F32),
        ],
        compiler_params=vmem_params(2),
        cost_estimate=pl.CostEstimate(flops=4_000_000_000, bytes_accessed=18_000_000, transcendentals=4_000_000),
        name="forward",
    )(e_in, x_in, halo_up, halo_dn, w3, w_proj)

    preds = lax.all_to_all(snd, "member", 0, 0, tiled=True)

    device = lax.axis_index("member").astype(jnp.int32).reshape(1)
    rows = (count + 1) * members
    grads = pl.pallas_call(
        functools.partial(pair_kernel, sz, count, members),
        grid_spec=pltpu.PrefetchScalarGridSpec(
            num_scalar_prefetch=2,
            grid=(1,),
            in_specs=[
                whole((sz.devs, mem, sz.subpad, LANES)),
                spec((1, sz.subpad, LANES), lambda i, match, device: (device[0], 0, 0)),
            ],
            out_specs=whole((sz.devs, mem, sz.subpad, LANES)),
            scratch_shapes=[
                pltpu.VMEM((members, sz.subpad, LANES), F32),
                pltpu.VMEM((sz.subpad, LANES), F32),
                pltpu.VMEM((rows * 8, LANES), F32),
                pltpu.VMEM((rows, LANES), F32),
                pltpu.SMEM((count, members), jnp.int32),
            ],
        ),
        out_shape=jax.ShapeDtypeStruct((sz.devs, mem, sz.subpad, LANES), BF16),
        compiler_params=vmem_params(1),
        name="pairs",
    )(matchings, device, preds, truth)

    back = lax.all_to_all(grads, "member", 0, 0, tiled=True)

    w_proj_t = w_proj.T
    wt3 = jnp.pad(w_conv.T.reshape(3, 3 * ch, hid), ((0, 0), (0, TAPS - 3 * ch), (0, 0)))
    cols = 4 * TAPS - LANES
    grad_pred, grad_pre, partial, edges = pl.pallas_call(
        functools.partial(weight_kernel, sz),
        grid=(mem,),
        in_specs=[
            spec((sz.devs, 1, sz.subpad, LANES), lambda m: (0, m, 0, 0)),
            by_member(hid, pos),
            by_member(hid, pos),
            by_member(TAPS, pos),
            by_member(ch, 1, lon),
            by_member(ch, 1, lon),
            whole(w_proj_t.shape),
            whole(wt3.shape),
        ],
        out_specs=[
            by_member(ch, pos),
            by_member(hid, pos + 2 * lon),
            whole((hid, cols)),
            by_member(2, ch, lon),
        ],
        out_shape=[
            jax.ShapeDtypeStruct((mem, ch, pos), BF16),
            jax.ShapeDtypeStruct((mem, hid, pos + 2 * lon), BF16),
            jax.ShapeDtypeStruct((hid, cols), BF16),
            jax.ShapeDtypeStruct((mem, 2, ch, lon), F32),
        ],
        scratch_shapes=[
            pltpu.VMEM((TAPS, pos + 2 * lon), BF16),
            pltpu.VMEM((TAPS, lon), F32),
            pltpu.VMEM((sz.parts, sz.subpad, LANES), F32),
            pltpu.VMEM((hid, 3 * TAPS + ch), F32),
        ],
        compiler_params=vmem_params(1),
        name="weights",
    )(back, hidden, slope, e_in, halo_up, halo_dn, w_proj_t, wt3)

    shards = member_count * band_count
    terms = lax.all_to_all(
        partial.reshape(shards, hid // shards, cols), ("member", "band"), 0, 0, tiled=True
    )
    from_dn = lax.ppermute(edges[:, 0:1], "band", up)
    from_up = lax.ppermute(edges[:, 1:2], "band", down)

    grad_states = pl.pallas_call(
        functools.partial(data_kernel, sz),
        grid=(mem,),
        in_specs=[
            by_member(hid, pos + 2 * lon),
            by_member(ch, pos),
            whole(wt3.shape),
            by_member(1, ch, lon),
            by_member(1, ch, lon),
        ],
        out_specs=by_member(ch, lat, lon),
        out_shape=jax.ShapeDtypeStruct((mem, ch, lat, lon), BF16),
        scratch_shapes=[pltpu.VMEM((ch * lat, lon), F32)],
        compiler_params=vmem_params(1),
        cost_estimate=pl.CostEstimate(flops=4_000_000_000, bytes_accessed=8_000_000, transcendentals=0),
        name="data",
    )(grad_pre, grad_pred, wt3, from_dn, from_up)

    factor = 1.0 / (pos * members * band_count) ** 0.5
    total = jnp.sum(terms.astype(F32), axis=0) * factor
    own = hid // shards
    grad_conv = total[:, : 3 * TAPS].reshape(own, 3, TAPS)[:, :, : 3 * ch].reshape(own, 9 * ch)
    grad_proj = total[:, 3 * TAPS : 3 * TAPS + ch].T
    return grad_states, grad_conv, grad_proj


def solution(mesh):
    return jax.shard_map(
        on_device,
        mesh=mesh,
        in_specs=(
            P("member", None, "band", None),
            P("member", None, "band", None),
            P(None, "band", None),
            P(),
            P(),
            P(),
        ),
        out_specs=(
            P("member", None, "band", None),
            P(("member", "band"), None),
            P(None, ("member", "band")),
        ),
        check_vma=False,
    )
```

time: 418 us -> 135 us (0.32); the launches traced: 410 us -> 134 us
  waiting for transfers between devices: 183 us -> 46.1 us
  local copies, waits for them, and re-layouts: 94.5 us -> 9.39 us
  matrix products: 58.3 us -> 0 us
  Pallas kernels: 0 us -> 51.5 us
  between operations: 45.7 us -> 0.76 us
  other arithmetic: 17.4 us -> 1.87 us
  starting transfers between devices: 11.4 us -> 24.3 us
    reduce_scatter x2 -> x0, waiting for transfers between devices: 161 us -> none  [the longest x1 98 us: on_device(): lax.psum_scatter(conv_term, ('member', 'band'), scatter_dimension=0, tile...]
    dot_general x24 -> x0, matrix products: 58.3 us -> none  [the longest x1 23.9 us: on_device(): jnp.einsum('hk,mkp->mhp', w_conv, columns, preferred_element_type=jnp.flo...]
    pallas_call x0 -> x5, Pallas kernels: none -> 51.5 us  [the longest x1 18 us: on_device(): pl.pallas_call(functools.partial(weight_kernel, sz), grid=(mem,), in_spec...]
    all_to_all x0 -> x3, waiting for transfers between devices: none -> 37.7 us  [the longest x1 18.8 us: on_device(): preds = lax.all_to_all(snd, 'member', 0, 0, tiled=True)]
    reshape x6 -> x3, local copies, waits for them, and re-layouts: 37.8 us -> 0.85 us  [the longest x2 0.75 us: on_device(): total[:, :3 * TAPS].reshape(own, 3, TAPS)[:, :, :3 * ch]]
    another operation x19 -> x0, local copies, waits for them, and re-layouts: 30.5 us -> none  [the longest x16 26.1 us: on_device(): jnp.stack([lax.dynamic_index_in_dim(everyone, wanted[slot], 0, keepdims=F...]
    all_gather x1 -> x0, waiting for transfers between devices: 14.5 us -> none  [on_device(): everyone = lax.all_gather(predicted, 'member', axis=0, tiled=True)]
    all_to_all x0 -> x3, starting transfers between devices: none -> 12.5 us  [the longest x1 5.54 us: on_device(): preds = lax.all_to_all(snd, 'member', 0, 0, tiled=True)]
  transfers between devices with their start and end apart: 7 -> 7, of which waited for: 6 -> 5; matrix products, arithmetic and copies ran while one was open for 19% -> 4% of each run, Pallas kernels for 0% -> 9%
where the time goes in v1:
time: 135 us; the launch traced here: 134 us
  Pallas kernels  51.5 us (38%)
  waiting for transfers between devices  46.1 us (34%)
  starting transfers between devices  24.3 us (18%)
  local copies, waits for them, and re-layouts  9.39 us (7%)
  other arithmetic  1.87 us (1%)
    all_to_all x1, waiting for transfers between devices, on_device(): preds = lax.all_to_all(snd, 'member', 0, 0, tiled=True)  18.8 us
    pallas_call x1, Pallas kernels, on_device(): pl.pallas_call(functools.partial(weight_kernel, sz), grid=(mem,), in_spec...  18 us
    all_to_all x1, waiting for transfers between devices, on_device(): back = lax.all_to_all(grads, 'member', 0, 0, tiled=True)  16.9 us
    pallas_call x1, Pallas kernels, on_device(): pl.pallas_call(functools.partial(forward_kernel, sz), grid=(mem, sz.prows...  15.3 us
    pallas_call x1, Pallas kernels, on_device(): pl.pallas_call(functools.partial(data_kernel, sz), grid=(mem,), in_specs=...  7.03 us
    unnamed x18, local copies, waits for them, and re-layouts  6.05 us
    pallas_call x1, Pallas kernels, on_device(): pl.pallas_call(functools.partial(prep_kernel, sz), grid=(mem,), in_specs=...  5.69 us
    pallas_call x1, Pallas kernels, on_device(): pl.pallas_call(functools.partial(pair_kernel, sz, count, members), grid_s...  5.57 us
  transfers between devices with their start and end apart: 7, of which 5 were waited for; matrix products, arithmetic and copies ran while one was open for 4% of the time, Pallas kernels for 9%

profile of v1, /device:TPU:0, one launch (start us, length us, event | category | flops | bytes accessed | tf_op | source)
XLA Modules:
  0.0 134.0 jit_solution(11833200608258881344)
XLA Ops:
  0.6 1.7 %add_convert_fusion = (bf16[2,84,1,128]{3,2,1,0:T(2,128)(2,1)S(1)}, bf16[2,84,1,128]{3,2,1,0:T(2,128)(2,1)S(1)}) fusion(f32[2,84,16,128]{3,2,1,0:T(8,128)} %noise.1, bf16[2,84,16,128]{3,2,1,0:T(8,128)(2,1)} %states.1), kind=kLoop, calls=%fused_computation.1 | loop fusion | flops 129024 | bytes 344064 | tf_op jit(solution)/shard_map/convert_element_type | solution.py:319
  2.4 1.3 collective-permute-start.1
  3.7 5.5 %collective-permute-start = (bf16[2,84,1,128]{3,2,1,0:T(2,128)(2,1)S(1)}, bf16[2,84,1,128]{3,2,1,0:T(2,128)(2,1)S(1)}, u32[]{:S(2)}, u32[]{:S(2)}) collective-permute-start(bf16[2,84,1,128]{3,2,1,0:T(2,128)(2,1)S(1)} %get-tuple-element.26), channel_id=1, source_target_pairs={{0,1},{1,2},{2,3},{4,5},{5,6},{6,7},{8,9},{9,10},{10,11},{12,13},{... | collective-permute-start | bytes 129032 | tf_op jit(solution)/shard_map/ppermute | solution.py:321
  9.2 2.3 %copy.11.w_conv = bf16[512,756]{1,0:T(8,128)(2,1)} copy(bf16[512,756]{0,1:T(8,128)(2,1)} %param.9) | data formatting | bytes 1548288 | tf_op args[3]
  11.5 5.7 %prep.1 = (bf16[2,256,2048]{2,1,0:T(8,128)(2,1)}, bf16[2,84,2048]{2,1,0:T(8,128)(2,1)}, bf16[8,168,128]{2,1,0:T(8,128)(2,1)}, bf16[512,768]{1,0:T(8,128)(2,1)}) custom-call(bf16[2,84,16,128]{3,2,1,0:T(8,128)(2,1)} %states.1, f32[2,84,16,128]{3,2,1,0:T(8,128)} %noise.1, bf16[84,16,128]{2,1,0:T(8,128)(2,1)} %target.1, bf16[512,756]{1,0:T(8,128)(2,1)} %copy.11.w_conv), custom_call_target="tpu_custom_call" | custom-call | flops 10000000 | bytes 8000000 | tf_op jit(solution)/shard_map/prep/pallas_call | solution.py:327
  17.1 0.0 collective-permute-done.1.halo_dn
  17.2 0.0 copy-start.4
  17.2 0.0 collective-permute-done.halo_up
  17.2 0.0 copy-start.5
  17.2 0.6 copy-done.4
  17.8 0.0 copy-done.5
  17.8 15.3 %forward.1 = (bf16[2,512,2048]{2,1,0:T(8,128)(2,1)}, f32[2,512,2048]{2,1,0:T(8,128)}, bf16[8,2,168,128]{3,2,1,0:T(8,128)(2,1)}) custom-call(bf16[2,256,2048]{2,1,0:T(8,128)(2,1)} %get-tuple-element.14.e_in, bf16[2,84,2048]{2,1,0:T(8,128)(2,1)} %get-tuple-element.15.x_in, bf16[2,84,1,128]{3,2,1,0:T(2,128)(2,1)} %copy-done.5, ...), custom_call_target="tpu_custom_call" | custom-call | flops 4000000000 | bytes 18000000 | tf_op jit(solution)/shard_map/forward/pallas_call | solution.py:358
  33.1 0.0 copy-start.3
  33.1 0.0 copy-start
  33.1 5.5 %all-to-all-start = ((bf16[8,2,168,128]{3,2,1,0:T(8,128)(2,1)}), bf16[8,2,168,128]{3,2,1,0:T(8,128)(2,1)S(1)}, u32[]{:S(2)}, u32[]{:S(2)}) async-start(bf16[8,2,168,128]{3,2,1,0:T(8,128)(2,1)} %get-tuple-element.17), calls=%async_computation | async-start | bytes 1376256 | tf_op jit(solution)/shard_map/all_to_all | solution.py:389
  38.7 18.8 %all-to-all-done.preds = bf16[8,2,168,128]{3,2,1,0:T(8,128)(2,1)S(1)} async-done(((bf16[8,2,168,128]{3,2,1,0:T(8,128)(2,1)}), bf16[8,2,168,128]{3,2,1,0:T(8,128)(2,1)S(1)}, u32[]{:S(2)}, u32[]{:S(2)}) %all-to-all-start) | async-done | bytes 688160 | tf_op jit(solution)/shard_map/all_to_all | solution.py:389
  57.5 0.0 copy-start.2
  57.5 0.8 copy-done.2
  58.4 5.6 %pairs.1 = bf16[8,2,168,128]{3,2,1,0:T(8,128)(2,1)} custom-call(s32[4,16]{1,0:T(4,128)} %match.1, s32[1]{0:T(128)} %bitcast.device, bf16[8,2,168,128]{3,2,1,0:T(8,128)(2,1)} %copy-done.2, bf16[8,168,128]{2,1,0:T(8,128)(2,1)} %get-tuple-element.18.truth), custom_call_target="tpu_custom_call" | custom-call | tf_op jit(solution)/shard_map/pairs/pallas_call | solution.py:393
  64.0 3.5 %all-to-all-start.1 = ((bf16[8,2,168,128]{3,2,1,0:T(8,128)(2,1)}), bf16[8,2,168,128]{3,2,1,0:T(8,128)(2,1)S(1)}, u32[]{:S(2)}, u32[]{:S(2)}) async-start(bf16[8,2,168,128]{3,2,1,0:T(8,128)(2,1)} %pairs.1), calls=%async_computation.1 | async-start | bytes 1376256 | tf_op jit(solution)/shard_map/all_to_all | solution.py:416
  67.5 0.0 copy-done.3
  67.5 0.8 copy.12
  68.3 0.0 copy-done
  68.3 0.1 reshape.22
  68.4 0.9 pad.4.wt3
  69.3 16.9 %all-to-all-done.1.back = bf16[8,2,168,128]{3,2,1,0:T(8,128)(2,1)S(1)} async-done(((bf16[8,2,168,128]{3,2,1,0:T(8,128)(2,1)}), bf16[8,2,168,128]{3,2,1,0:T(8,128)(2,1)S(1)}, u32[]{:S(2)}, u32[]{:S(2)}) %all-to-all-start.1) | async-done | bytes 688160 | tf_op jit(solution)/shard_map/all_to_all | solution.py:416
  86.3 0.0 copy-start.1
  86.3 0.8 copy-done.1
  87.1 18.0 %weights.1 = (bf16[2,84,2048]{2,1,0:T(8,128)(2,1)}, bf16[2,512,2304]{2,1,0:T(8,128)(2,1)}, bf16[512,896]{1,0:T(8,128)(2,1)}, f32[2,2,84,128]{3,2,1,0:T(8,128)}) custom-call(bf16[8,2,168,128]{3,2,1,0:T(8,128)(2,1)} %copy-done.1, bf16[2,512,2048]{2,1,0:T(8,128)(2,1)} %get-tuple-element.19.hid, f32[2,512,2048]{2,1,0:T(8,128)} %get-tuple-element.20.slope, ...), custom_call_target="tpu_custom_call" | custom-call | tf_op jit(solution)/shard_map/weights/pallas_call | solution.py:421
  105.1 3.5 %all-to-all-start.2 = ((bf16[32,16,896]{2,1,0:T(8,128)(2,1)}), bf16[32,16,896]{2,1,0:T(8,128)(2,1)S(1)}, u32[]{:S(2)}, u32[]{:S(2)}) async-start(bf16[32,16,896]{2,1,0:T(8,128)(2,1)} %bitcast.8), calls=%async_computation.2 | async-start | bytes 1835008 | tf_op jit(solution)/shard_map/all_to_all | solution.py:457
  108.5 1.0 fusion
  109.5 3.7 %collective-permute-start.3 = (f32[2,1,84,128]{3,2,1,0:T(8,128)S(1)}, f32[2,1,84,128]{3,2,1,0:T(8,128)S(1)}, u32[]{:S(2)}, u32[]{:S(2)}) collective-permute-start(f32[2,1,84,128]{3,2,1,0:T(8,128)S(1)} %get-tuple-element.27), channel_id=1, source_target_pairs={{0,1},{1,2},{2,3},{4,5},{5,6},{6,7},{8,9},{9,10},{10,11},{12,13},{... | collective-permute-start | bytes 258056 | tf_op jit(solution)/shard_map/ppermute | solution.py:461
  113.2 1.3 collective-permute-start.2
  114.5 3.3 %collective-permute-done.3.from_up = f32[2,1,84,128]{3,2,1,0:T(8,128)S(1)} collective-permute-done((f32[2,1,84,128]{3,2,1,0:T(8,128)S(1)}, f32[2,1,84,128]{3,2,1,0:T(8,128)S(1)}, u32[]{:S(2)}, u32[]{:S(2)}) %collective-permute-start.3) | collective-permute-done | bytes 86048 | tf_op jit(solution)/shard_map/ppermute | solution.py:461
  117.8 0.0 copy-start.6
  117.8 5.1 %collective-permute-done.2.from_dn = f32[2,1,84,128]{3,2,1,0:T(8,128)S(1)} collective-permute-done((f32[2,1,84,128]{3,2,1,0:T(8,128)S(1)}, f32[2,1,84,128]{3,2,1,0:T(8,128)S(1)}, u32[]{:S(2)}, u32[]{:S(2)}) %collective-permute-start.2) | collective-permute-done | bytes 86048 | tf_op jit(solution)/shard_map/ppermute | solution.py:460
  122.9 0.0 copy-start.7
  122.9 0.0 copy-done.6
  122.9 0.6 copy-done.7
  123.5 7.0 %data.1 = bf16[2,84,16,128]{3,2,1,0:T(8,128)(2,1)} custom-call(bf16[2,512,2304]{2,1,0:T(8,128)(2,1)} %get-tuple-element.21.gpre, bf16[2,84,2048]{2,1,0:T(8,128)(2,1)} %get-tuple-element.22.gp, bf16[3,256,512]{2,1,0:T(8,128)(2,1)} %pad.4.wt3, f32[2,1,84,128]{3,2,1,0:T(8,128)} %copy-done.7, f32[2,1,84,128]{3,2,1,0:T(8,128)} %copy-done.6), custom_call_target="tpu_custom_call" | custom-call | flops 4000000000 | bytes 8000000 | tf_op jit(solution)/shard_map/data/pallas_call | solution.py:463
  130.6 1.9 %all-to-all-done.2 = bf16[32,16,896]{2,1,0:T(8,128)(2,1)S(1)} async-done(((bf16[32,16,896]{2,1,0:T(8,128)(2,1)}), bf16[32,16,896]{2,1,0:T(8,128)(2,1)S(1)}, u32[]{:S(2)}, u32[]{:S(2)}) %all-to-all-start.2) | async-done | bytes 917536 | tf_op jit(solution)/shard_map/all_to_all | solution.py:457
  132.5 0.1 convert_reduce_fusion
  132.7 0.6 slice_bitcast_fusion
  133.3 0.7 reshape.25
  (3 shorter events, 0.0 us)
Async XLA Ops:
  2.4 14.8 %collective-permute-start.1 = (bf16[2,84,1,128]{3,2,1,0:T(2,128)(2,1)S(1)}, bf16[2,84,1,128]{3,2,1,0:T(2,128)(2,1)S(1)}, u32[]{:S(2)}, u32[]{:S(2)}) collective-permute-start(bf16[2,84,1,128]{3,2,1,0:T(2,128)(2,1)S(1)} %get-tuple-element.25), channel_id=1, source_target_pairs={{1,0},{2,1},{3,2},{5,4},{6,5},{7,6},{9,8},{10,9},{11,10},{13,12},{... | collective-permute-start | bytes 129032 | tf_op jit(solution)/shard_map/ppermute | solution.py:322
  3.7 13.5 %collective-permute-start = (bf16[2,84,1,128]{3,2,1,0:T(2,128)(2,1)S(1)}, bf16[2,84,1,128]{3,2,1,0:T(2,128)(2,1)S(1)}, u32[]{:S(2)}, u32[]{:S(2)}) collective-permute-start(bf16[2,84,1,128]{3,2,1,0:T(2,128)(2,1)S(1)} %get-tuple-element.26), channel_id=1, source_target_pairs={{0,1},{1,2},{2,3},{4,5},{5,6},{6,7},{8,9},{9,10},{10,11},{12,13},{... | collective-permute-start | bytes 129032 | tf_op jit(solution)/shard_map/ppermute | solution.py:321
  17.2 0.6 copy-start.4
  17.2 0.7 copy-start.5
  33.1 34.4 %copy-start.3 = (bf16[84,512]{1,0:T(8,128)(2,1)S(1)}, bf16[84,512]{1,0:T(8,128)(2,1)}, u32[]{:S(2)}) copy-start(bf16[84,512]{1,0:T(8,128)(2,1)} %w_proj.1) | copy-start | bytes 258052
  33.1 35.1 %copy-start = (bf16[512,756]{0,1:T(8,128)(2,1)S(1)}, bf16[512,756]{0,1:T(8,128)(2,1)}, u32[]{:S(2)}) copy-start(bf16[512,756]{0,1:T(8,128)(2,1)} %param.9) | copy-start | bytes 2322436
  33.1 24.4 %all-to-all-start = ((bf16[8,2,168,128]{3,2,1,0:T(8,128)(2,1)}), bf16[8,2,168,128]{3,2,1,0:T(8,128)(2,1)S(1)}, u32[]{:S(2)}, u32[]{:S(2)}) async-start(bf16[8,2,168,128]{3,2,1,0:T(8,128)(2,1)} %get-tuple-element.17), calls=%async_computation | async-start | bytes 1376256 | tf_op jit(solution)/shard_map/all_to_all | solution.py:389
  57.5 0.8 copy-start.2
  64.0 22.3 %all-to-all-start.1 = ((bf16[8,2,168,128]{3,2,1,0:T(8,128)(2,1)}), bf16[8,2,168,128]{3,2,1,0:T(8,128)(2,1)S(1)}, u32[]{:S(2)}, u32[]{:S(2)}) async-start(bf16[8,2,168,128]{3,2,1,0:T(8,128)(2,1)} %pairs.1), calls=%async_computation.1 | async-start | bytes 1376256 | tf_op jit(solution)/shard_map/all_to_all | solution.py:416
  86.3 0.8 copy-start.1
  105.1 27.4 %all-to-all-start.2 = ((bf16[32,16,896]{2,1,0:T(8,128)(2,1)}), bf16[32,16,896]{2,1,0:T(8,128)(2,1)S(1)}, u32[]{:S(2)}, u32[]{:S(2)}) async-start(bf16[32,16,896]{2,1,0:T(8,128)(2,1)} %bitcast.8), calls=%async_computation.2 | async-start | bytes 1835008 | tf_op jit(solution)/shard_map/all_to_all | solution.py:457
  109.5 8.3 %collective-permute-start.3 = (f32[2,1,84,128]{3,2,1,0:T(8,128)S(1)}, f32[2,1,84,128]{3,2,1,0:T(8,128)S(1)}, u32[]{:S(2)}, u32[]{:S(2)}) collective-permute-start(f32[2,1,84,128]{3,2,1,0:T(8,128)S(1)} %get-tuple-element.27), channel_id=1, source_target_pairs={{0,1},{1,2},{2,3},{4,5},{5,6},{6,7},{8,9},{9,10},{10,11},{12,13},{... | collective-permute-start | bytes 258056 | tf_op jit(solution)/shard_map/ppermute | solution.py:461
  113.2 9.7 %collective-permute-start.2 = (f32[2,1,84,128]{3,2,1,0:T(8,128)S(1)}, f32[2,1,84,128]{3,2,1,0:T(8,128)S(1)}, u32[]{:S(2)}, u32[]{:S(2)}) collective-permute-start(f32[2,1,84,128]{3,2,1,0:T(8,128)S(1)} %get-tuple-element.28), channel_id=1, source_target_pairs={{1,0},{2,1},{3,2},{5,4},{6,5},{7,6},{9,8},{10,9},{11,10},{13,12},{... | collective-permute-start | bytes 258056 | tf_op jit(solution)/shard_map/ppermute | solution.py:460
  117.8 5.1 %copy-start.6 = (f32[2,1,84,128]{3,2,1,0:T(8,128)}, f32[2,1,84,128]{3,2,1,0:T(8,128)S(1)}, u32[]{:S(2)}) copy-start(f32[2,1,84,128]{3,2,1,0:T(8,128)S(1)} %collective-permute-done.3.from_up) | copy-start | bytes 258052
  122.9 0.6 copy-start.7

commit v2 on v1

v2 whole, which is shorter than its diff:
```python
import functools

import jax
import jax.numpy as jnp
from jax import lax
from jax.experimental import pallas as pl
from jax.experimental.pallas import tpu as pltpu
from jax.sharding import PartitionSpec as P

SQRT_HALF = 0.7071067811865476
INV_ROOT_TWO_PI = 0.3989422804014327
F32 = jnp.float32
BF16 = jnp.bfloat16
LANES = 128
TAPS = 256
VMEM_LIMIT = 60 * 1024 * 1024


def vmem_params(count):
    return pltpu.CompilerParams(
        dimension_semantics=("arbitrary",) * count, vmem_limit_bytes=VMEM_LIMIT
    )


def shift_right(vals):
    lane = lax.broadcasted_iota(jnp.int32, vals.shape, 1)
    return jnp.where(lane == 0, 0.0, pltpu.roll(vals, 1, 1))


def shift_left(vals):
    width = vals.shape[1]
    lane = lax.broadcasted_iota(jnp.int32, vals.shape, 1)
    return jnp.where(lane == width - 1, 0.0, pltpu.roll(vals, width - 1, 1))


def expand_row(vals, scratch):
    channels = vals.shape[0]
    scratch[pl.ds(0, channels), :] = shift_right(vals)
    scratch[pl.ds(channels, channels), :] = vals
    scratch[pl.ds(2 * channels, channels), :] = shift_left(vals)
    return scratch[...].astype(BF16)


def swap_blocks(rows):
    parts = len(rows)
    size = rows[0].shape[1] // parts
    lane = lax.broadcasted_iota(jnp.int32, rows[0].shape, 1)
    rows = list(rows)
    bit = 1
    while bit < parts:
        low = (lane & (bit * size)) == 0
        shift = bit * size
        width = rows[0].shape[1]
        for i in range(parts):
            if i & bit:
                continue
            a, b = rows[i], rows[i | bit]
            rows[i] = jnp.where(low, a, pltpu.roll(b, shift, 1))
            rows[i | bit] = jnp.where(low, pltpu.roll(a, width - shift, 1), b)
        bit *= 2
    return rows


class Sizes:
    def __init__(self, states, w_conv, member_count):
        self.mem, self.ch, self.lat, self.lon = states.shape
        self.hid = w_conv.shape[0]
        self.devs = member_count
        prows = self.lat // 8
        self.chunks = prows if member_count <= 8 else 1
        self.crows = self.lat // self.chunks
        self.parts = self.devs * 8 // self.crows
        self.cpos = self.crows * self.lon
        self.sub = self.mem * self.ch
        self.chpad = (self.ch + 7) // 8 * 8
        self.pos = self.lat * self.lon
        assert self.parts == 8 and self.crows % 8 == 0


def prep_kernel(sz, states, noise, target, w_conv, e_out, x_out, t_out, w_out, xs, es):
    es[...] = jnp.zeros_like(es)
    x = (states[0].astype(F32) + noise[0]).astype(BF16)
    xs[...] = x.astype(F32).reshape(sz.ch * sz.lat, sz.lon)
    for row in range(sz.lat):
        vals = xs[pl.ds(row, sz.ch, stride=sz.lat), :]
        x_out[0, :, row * sz.lon : (row + 1) * sz.lon] = vals.astype(BF16)
        e_out[0, :, row * sz.lon : (row + 1) * sz.lon] = expand_row(vals, es)

    @pl.when(pl.program_id(0) == 0)
    def _():
        xs[...] = target[...].astype(F32).reshape(sz.ch * sz.lat, sz.lon)
        for chunk in range(sz.chunks):
            for prow in range(sz.crows // 8):
                first = chunk * sz.crows + prow * 8
                rows = [xs[pl.ds(first + i, sz.ch, stride=sz.lat), :] for i in range(8)]
                for q, out in enumerate(swap_blocks(rows)):
                    t_out[chunk, prow * 8 + q] = out.astype(BF16)

    @pl.when(pl.program_id(0) == sz.mem - 1)
    def _():
        taps = 3 * sz.ch
        for part in range(3):
            w_out[:, part * TAPS : (part + 1) * TAPS] = jnp.concatenate(
                [
                    w_conv[:, part * taps : (part + 1) * taps],
                    jnp.zeros((sz.hid, TAPS - taps), BF16),
                ],
                axis=1,
            )


def extend(sz, chunk, ext, es, e_in, halo_up, halo_dn):
    width = sz.lon
    first = chunk * sz.crows
    last = first + sz.crows
    es[...] = jnp.zeros_like(es)
    low = max(first - 1, 0)
    high = min(last + 1, sz.lat)
    at = (low - first + 1) * width
    ext[:, at : at + (high - low) * width] = e_in[0, :, low * width : high * width]
    if first == 0:
        ext[:, 0:width] = expand_row(halo_up[0, :, 0, :].astype(F32), es)
    if last == sz.lat:
        ext[:, width + sz.cpos :] = expand_row(halo_dn[0, :, 0, :].astype(F32), es)


def forward_kernel(sz, chunk, e_in, x_in, halo_up, halo_dn, w3, w_proj, hid_out, slope_out, snd, ext, es, ps):
    width = sz.lon
    member = pl.program_id(0)
    extend(sz, chunk, ext, es, e_in, halo_up, halo_dn)
    rows = []
    for pair in range(sz.crows // 2):
        cols = jnp.concatenate(
            [ext[:, (pair * 2 + ro) * width : (pair * 2 + ro + 2) * width] for ro in range(3)], axis=0
        )
        preact = jnp.dot(w3[...], cols, preferred_element_type=F32)
        twice = 1.0 + lax.erf(preact * SQRT_HALF)
        hidden = (preact * twice).astype(BF16)
        bell = jnp.exp(preact * preact * (-0.5)) * (2.0 * INV_ROOT_TWO_PI)
        here = slice(pair * 2 * width, (pair + 1) * 2 * width)
        hid_out[0, :, here] = hidden
        slope_out[0, :, here] = (twice + preact * bell).astype(BF16)
        pred = x_in[0, :, here].astype(F32) + jnp.dot(
            w_proj[...], hidden, preferred_element_type=F32
        )
        pred = pred.astype(BF16).astype(F32)
        rows += [pred[:, :width], pred[:, width:]]
    for prow in range(sz.crows // 8):
        for q, out in enumerate(swap_blocks(rows[prow * 8 : (prow + 1) * 8])):
            for m in range(sz.mem):

                @pl.when(member == m)
                def _():
                    ps[prow * 8 + q, pl.ds(m * sz.ch, sz.ch), :] = out

    @pl.when(member == sz.mem - 1)
    def _():
        snd[...] = ps[...].astype(BF16)


def pair_kernel(sz, count, match, device, preds, truth, grads, vals, tsc, sums, scale, gs, inv):
    norm = 1.0 / (32.0 * sz.ch)
    members = sz.devs * sz.mem
    ch, folds = sz.ch, sz.chpad // 8
    tail = folds * 8 - 8
    tsc[pl.ds(tail, 8), :] = jnp.zeros((8, LANES), F32)
    tsc[pl.ds(0, ch), :] = truth[0, 0].astype(F32)

    def unpack(src, carry):
        gs[...] = preds[src].astype(F32)
        for j in range(sz.mem):
            vals[src * sz.mem + j, pl.ds(tail, 8), :] = jnp.zeros((8, LANES), F32)
            vals[src * sz.mem + j, pl.ds(0, ch), :] = gs[pl.ds(j * ch, ch), :]
        return carry

    lax.fori_loop(0, sz.devs, unpack, 0)

    def squares(diff):
        return jnp.sum((diff * diff).reshape(folds, 8, LANES), axis=0)

    def first(m, carry):
        own = vals[m]
        sums[pl.ds(pl.multiple_of((count * members + m) * 8, 8), 8), :] = squares(own - tsc[...])
        for k in range(count):
            other = match[k, m]
            inv[k, other] = m
            at = pl.multiple_of((k * members + m) * 8, 8)
            sums[pl.ds(at, 8), :] = squares(own - vals[other])
        return carry

    lax.fori_loop(0, members, first, 0)
    rows = (count + 1) * members
    total = sums[pl.ds(0, rows, stride=8), :]
    for j in range(1, 8):
        total = total + sums[pl.ds(j, rows, stride=8), :]
    step = sz.lon // sz.parts
    while step < LANES:
        total = total + pltpu.roll(total, step, 1)
        step *= 2
    lane = lax.broadcasted_iota(jnp.int32, total.shape, 1)
    for bit in (1, 2):
        total = total + jnp.where(
            (lane & bit) == 0, pltpu.roll(total, LANES - bit, 1), pltpu.roll(total, bit, 1)
        )
    scale[...] = lax.rsqrt(total * norm + 1e-06)

    def second(src, carry):
        for j in range(sz.mem):
            m = src * sz.mem + j
            own = vals[m]

            def term(other, index):
                return (own - other) * scale[pl.ds(index, 1), :]

            acc = None
            for k in range(count):
                back = inv[k, m]
                both = term(vals[match[k, m]], k * members + m)
                both = both + term(vals[back], k * members + back)
                acc = both if acc is None else acc + both
            out = term(tsc[...], count * members + m) - acc * (0.5 / count)
            gs[pl.ds(j * ch, ch), :] = out[:ch]
        grads[src] = gs[...].astype(BF16)
        return carry

    lax.fori_loop(0, sz.devs, second, 0)


def fold_taps(part, channels):
    return (
        part[channels : 2 * channels]
        + shift_left(part[0:channels])
        + shift_right(part[2 * channels : 3 * channels])
    )


def weight_kernel(sz, chunk, *refs):
    refs = list(refs)
    back, hid, slope, e_in, halo_up, halo_dn, w_proj_t, wt3 = refs[:8]
    refs = refs[8:]
    acc_in = refs.pop(0) if chunk else None
    gp_out, gpre_out, wg_out, edge_out, ext, es, rows_f, acc = refs
    width = sz.lon
    member = pl.program_id(0)
    final = chunk == sz.chunks - 1
    extend(sz, chunk, ext, es, e_in, halo_up, halo_dn)
    for prow in range(sz.crows // 8):
        for q in range(8):
            rows_f[q] = back[prow * 8 + q].astype(F32)
        for m in range(sz.mem):

            @pl.when(member == m)
            def _():
                outs = swap_blocks([rows_f[q, pl.ds(m * sz.ch, sz.ch), :] for q in range(8)])
                for i, out in enumerate(outs):
                    row = prow * 8 + i
                    gp_out[0, :, row * width : (row + 1) * width] = out.astype(BF16)

    for pair in range(sz.crows // 2):
        here = slice(pair * 2 * width, (pair + 1) * 2 * width)
        dhid = jnp.dot(w_proj_t[...], gp_out[0, :, here], preferred_element_type=F32)
        gpre_out[0, :, here] = (dhid * slope[0, :, here].astype(F32)).astype(BF16)
    gpre = gpre_out[0]
    dims = (((1,), (1,)), ((), ()))
    for ro in range(4):
        if ro < 3:
            term = lax.dot_general(
                gpre, ext[:, ro * width : ro * width + sz.cpos], dims, preferred_element_type=F32
            )
            at = slice(ro * TAPS, (ro + 1) * TAPS)
        else:
            term = lax.dot_general(hid[0], gp_out[0], dims, preferred_element_type=F32)
            at = slice(3 * TAPS, 3 * TAPS + sz.ch)

        @pl.when(member == 0)
        def _():
            acc[:, at] = term + acc_in[:, at] if chunk else term

        @pl.when(member > 0)
        def _():
            acc[:, at] = acc[:, at] + term

    for side in range(2):
        if (side == 0 and chunk == 0) or (side == 1 and final):
            col = 0 if side == 0 else sz.cpos - width
            part = jnp.dot(
                wt3[0 if side == 0 else 2], gpre[:, col : col + width], preferred_element_type=F32
            )
            edge_out[0, side if sz.chunks == 1 else 0] = fold_taps(part, sz.ch)

    @pl.when(member == sz.mem - 1)
    def _():
        used = 3 * TAPS + sz.ch
        wg_out[:, :used] = acc[...].astype(wg_out.dtype)
        if final:
            wg_out[:, used:] = jnp.zeros((sz.hid, wg_out.shape[1] - used), wg_out.dtype)


def data_kernel(sz, *refs):
    gpres, gps = refs[: sz.chunks], refs[sz.chunks : 2 * sz.chunks]
    wt3, from_dn, from_up, out, gs = refs[2 * sz.chunks :]
    width = sz.lon

    def two_rows(first):
        cols = []
        for row in (first, first + 1):
            if row < 0 or row >= sz.lat:
                cols.append(jnp.zeros((sz.hid, width), BF16))
            else:
                at = row % sz.crows * width
                cols.append(gpres[row // sz.crows][0, :, at : at + width])
        return jnp.concatenate(cols, axis=1)

    for pair in range(sz.lat // 2):
        part = None
        for ro in range(3):
            term = jnp.dot(wt3[ro], two_rows(pair * 2 + 1 - ro), preferred_element_type=F32)
            part = term if part is None else part + term
        for i in range(2):
            row = pair * 2 + i
            at = row % sz.crows * width
            total = gps[row // sz.crows][0, :, at : at + width].astype(F32) + fold_taps(
                part[:, i * width : (i + 1) * width], sz.ch
            )
            if row == 0:
                total = total + from_up[0, 0]
            if row == sz.lat - 1:
                total = total + from_dn[0, 0]
            gs[pl.ds(row, sz.ch, stride=sz.lat), :] = total
    out[0] = gs[...].reshape(sz.ch, sz.lat, width).astype(BF16)


def whole(shape):
    return pl.BlockSpec(shape, lambda *_: (0,) * len(shape))


def by_member(*shape):
    return pl.BlockSpec((1,) + shape, lambda m, *_: (m,) + (0,) * len(shape))


def array(shape, dtype):
    return jax.ShapeDtypeStruct(shape, dtype)


def cost(flops, moved, transcendentals=0):
    return pl.CostEstimate(flops=flops, bytes_accessed=moved, transcendentals=transcendentals)


def on_device(states, noise_field, target, w_conv, w_proj, matchings):
    member_count = lax.axis_size("member")
    band_count = lax.axis_size("band")
    sz = Sizes(states, w_conv, member_count)
    mem, ch, lat, lon, hid, pos = sz.mem, sz.ch, sz.lat, sz.lon, sz.hid, sz.pos
    cpos, chunks = sz.cpos, sz.chunks
    count = matchings.shape[0]
    members = mem * member_count
    down = [(i, i + 1) for i in range(band_count - 1)]
    up = [(i + 1, i) for i in range(band_count - 1)]

    def edge(row):
        return (
            states[:, :, row : row + 1].astype(F32) + noise_field[:, :, row : row + 1]
        ).astype(BF16)

    halo_up = lax.ppermute(edge(lat - 1), "band", down)
    halo_dn = lax.ppermute(edge(0), "band", up)

    e_in, x_in, truth, w3 = pl.pallas_call(
        functools.partial(prep_kernel, sz),
        grid=(mem,),
        in_specs=[
            by_member(ch, lat, lon),
            by_member(ch, lat, lon),
            whole((ch, lat, lon)),
            whole(w_conv.shape),
        ],
        out_specs=[
            by_member(TAPS, pos),
            by_member(ch, pos),
            whole((chunks, sz.devs, ch, LANES)),
            whole((hid, 3 * TAPS)),
        ],
        out_shape=[
            array((mem, TAPS, pos), BF16),
            array((mem, ch, pos), BF16),
            array((chunks, sz.devs, ch, LANES), BF16),
            array((hid, 3 * TAPS), BF16),
        ],
        scratch_shapes=[pltpu.VMEM((ch * lat, lon), F32), pltpu.VMEM((TAPS, lon), F32)],
        compiler_params=vmem_params(1),
        cost_estimate=cost(10_000_000, 8_000_000),
        name="prep",
    )(states, noise_field, target, w_conv)

    half_proj = w_proj * jnp.asarray(0.5, BF16)
    conv_flops = 2 * mem * cpos * hid * 3 * TAPS
    hidden, slope, snd = [], [], []
    for chunk in range(chunks):
        outs = pl.pallas_call(
            functools.partial(forward_kernel, sz, chunk),
            grid=(mem,),
            in_specs=[
                by_member(TAPS, pos),
                pl.BlockSpec((1, ch, cpos), lambda m, chunk=chunk: (m, 0, chunk)),
                by_member(ch, 1, lon),
                by_member(ch, 1, lon),
                whole((hid, 3 * TAPS)),
                whole(w_proj.shape),
            ],
            out_specs=[
                by_member(hid, cpos),
                by_member(hid, cpos),
                whole((sz.devs, sz.sub, LANES)),
            ],
            out_shape=[
                array((mem, hid, cpos), BF16),
                array((mem, hid, cpos), BF16),
                array((sz.devs, sz.sub, LANES), BF16),
            ],
            scratch_shapes=[
                pltpu.VMEM((TAPS, cpos + 2 * lon), BF16),
                pltpu.VMEM((TAPS, lon), F32),
                pltpu.VMEM((sz.devs, sz.sub, LANES), F32),
            ],
            compiler_params=vmem_params(1),
            cost_estimate=cost(conv_flops, 9_000_000, 2 * mem * cpos * hid),
            name=f"forward{chunk}",
        )(e_in, x_in, halo_up, halo_dn, w3, half_proj)
        hidden.append(outs[0])
        slope.append(outs[1])
        snd.append(outs[2])

    device = lax.axis_index("member").astype(jnp.int32).reshape(1)
    rows = (count + 1) * members
    preds = [lax.all_to_all(part, "member", 0, 0, tiled=True) for part in snd]
    back = []
    for chunk in range(chunks):
        grads = pl.pallas_call(
            functools.partial(pair_kernel, sz, count),
            grid_spec=pltpu.PrefetchScalarGridSpec(
                num_scalar_prefetch=2,
                grid=(1,),
                in_specs=[
                    whole((sz.devs, sz.sub, LANES)),
                    pl.BlockSpec(
                        (1, 1, ch, LANES),
                        lambda i, match, device, chunk=chunk: (chunk, device[0], 0, 0),
                    ),
                ],
                out_specs=whole((sz.devs, sz.sub, LANES)),
                scratch_shapes=[
                    pltpu.VMEM((members, sz.chpad, LANES), F32),
                    pltpu.VMEM((sz.chpad, LANES), F32),
                    pltpu.VMEM((rows * 8, LANES), F32),
                    pltpu.VMEM((rows, LANES), F32),
                    pltpu.VMEM((sz.sub, LANES), F32),
                    pltpu.SMEM((count, members), jnp.int32),
                ],
            ),
            out_shape=array((sz.devs, sz.sub, LANES), BF16),
            compiler_params=vmem_params(1),
            cost_estimate=cost(members * 20 * sz.chpad * LANES, 2_000_000),
            name=f"pairs{chunk}",
        )(matchings, device, preds[chunk], truth)
        back.append(lax.all_to_all(grads, "member", 0, 0, tiled=True))

    late_conv, late_proj, _ = lax.optimization_barrier((w_conv, half_proj, snd[0]))
    w_proj_t = late_proj.T
    wt3 = jnp.pad(late_conv.T.reshape(3, 3 * ch, hid), ((0, 0), (0, TAPS - 3 * ch), (0, 0)))
    used = 3 * TAPS + ch
    cols = (used + LANES - 1) // LANES * LANES
    grad_pred, grad_pre, edges = [], [], []
    partial = None
    for chunk in range(chunks):
        final = chunk == chunks - 1
        wg_shape = (hid, cols) if final else (hid, used)
        sides = 2 if chunks == 1 else 1
        extra = [] if partial is None else [partial]
        outs = pl.pallas_call(
            functools.partial(weight_kernel, sz, chunk),
            grid=(mem,),
            in_specs=[
                whole((sz.devs, sz.sub, LANES)),
                by_member(hid, cpos),
                by_member(hid, cpos),
                by_member(TAPS, pos),
                by_member(ch, 1, lon),
                by_member(ch, 1, lon),
                whole(w_proj_t.shape),
                whole(wt3.shape),
            ]
            + [whole((hid, used)) for _ in extra],
            out_specs=[
                by_member(ch, cpos),
                by_member(hid, cpos),
                whole(wg_shape),
                by_member(sides, ch, lon),
            ],
            out_shape=[
                array((mem, ch, cpos), BF16),
                array((mem, hid, cpos), BF16),
                array(wg_shape, BF16 if final else F32),
                array((mem, sides, ch, lon), F32),
            ],
            scratch_shapes=[
                pltpu.VMEM((TAPS, cpos + 2 * lon), BF16),
                pltpu.VMEM((TAPS, lon), F32),
                pltpu.VMEM((8, sz.sub, LANES), F32),
                pltpu.VMEM((hid, used), F32),
            ],
            compiler_params=vmem_params(1),
            cost_estimate=cost(conv_flops, 9_000_000),
            name=f"weights{chunk}",
        )(back[chunk], hidden[chunk], slope[chunk], e_in, halo_up, halo_dn, w_proj_t, wt3, *extra)
        grad_pred.append(outs[0])
        grad_pre.append(outs[1])
        partial = outs[2]
        edges.append(outs[3])

    shards = member_count * band_count
    terms = lax.all_to_all(
        partial.reshape(shards, hid // shards, cols), ("member", "band"), 0, 0, tiled=True
    )
    from_dn = lax.ppermute(edges[0][:, 0:1], "band", up)
    from_up = lax.ppermute(edges[-1][:, -1:], "band", down)

    grad_states = pl.pallas_call(
        functools.partial(data_kernel, sz),
        grid=(mem,),
        in_specs=[by_member(hid, cpos)] * chunks
        + [by_member(ch, cpos)] * chunks
        + [whole(wt3.shape), by_member(1, ch, lon), by_member(1, ch, lon)],
        out_specs=by_member(ch, lat, lon),
        out_shape=array((mem, ch, lat, lon), BF16),
        scratch_shapes=[pltpu.VMEM((ch * lat, lon), F32)],
        compiler_params=vmem_params(1),
        cost_estimate=cost(chunks * conv_flops, 8_000_000),
        name="data",
    )(*grad_pre, *grad_pred, wt3, from_dn, from_up)

    factor = 1.0 / (pos * members * band_count) ** 0.5
    total = jnp.sum(terms.astype(F32), axis=0)
    own = hid // shards
    grad_conv = total[:, : 3 * TAPS].reshape(own, 3, TAPS)[:, :, : 3 * ch].reshape(own, 9 * ch)
    grad_proj = total[:, 3 * TAPS : 3 * TAPS + ch].T
    return grad_states, grad_conv * factor, grad_proj * (0.5 * factor)


def solution(mesh):
    return jax.shard_map(
        on_device,
        mesh=mesh,
        in_specs=(
            P("member", None, "band", None),
            P("member", None, "band", None),
            P(None, "band", None),
            P(),
            P(),
            P(),
        ),
        out_specs=(
            P("member", None, "band", None),
            P(("member", "band"), None),
            P(None, ("member", "band")),
        ),
        check_vma=False,
    )
```

time: 135 us -> 139 us (1.030)
  waiting for transfers between devices: 46.1 us -> 27.2 us
  Pallas kernels: 51.5 us -> 65.7 us
  starting transfers between devices: 24.3 us -> 33.5 us
    all_to_all x2 -> x4, waiting for transfers between devices: 35.8 us -> 16.3 us  [the longest x2 9.26 us: on_device(): preds = [lax.all_to_all(part, 'member', 0, 0, tiled=True) for part in snd]]
    pallas_call x3 -> x6, Pallas kernels: 38.8 us -> 52.6 us  [the longest x2 25.3 us: on_device(): pl.pallas_call(functools.partial(weight_kernel, sz, chunk), grid=(mem,),...]
    all_to_all x2 -> x4, starting transfers between devices: 9.09 us -> 15.4 us  [the longest x2 8.33 us: on_device(): preds = [lax.all_to_all(part, 'member', 0, 0, tiled=True) for part in snd]]
    all_to_all x1, starting transfers between devices: 3.45 us -> 6.95 us  [on_device(): lax.all_to_all(partial.reshape(shards, hid // shards, cols), ('member', '...]
    mul x0 -> x2, local copies, waits for them, and re-layouts: none -> 1.49 us  [the longest x1 0.77 us: on_device(): half_proj = w_proj * jnp.asarray(0.5, BF16)]
    unnamed x18 -> x24, local copies, waits for them, and re-layouts: 6.05 us -> 5.41 us
  transfers between devices with their start and end apart: 7 -> 9, of which waited for: 5 -> 6; matrix products, arithmetic and copies ran while one was open for 4% -> 4% of each run, Pallas kernels for 9% -> 31%
where the time goes in v2:
time: 139 us; the launch traced here: 138 us
  Pallas kernels  65.7 us (47%)
  starting transfers between devices  33.5 us (24%)
  waiting for transfers between devices  27.2 us (20%)
  local copies, waits for them, and re-layouts  8.01 us (6%)
  other arithmetic  2.49 us (2%)
    pallas_call x2, Pallas kernels, on_device(): pl.pallas_call(functools.partial(weight_kernel, sz, chunk), grid=(mem,),...  25.3 us
    pallas_call x2, Pallas kernels, on_device(): pl.pallas_call(functools.partial(forward_kernel, sz, chunk), grid=(mem,),...  18.7 us
    all_to_all x2, waiting for transfers between devices, on_device(): preds = [lax.all_to_all(part, 'member', 0, 0, tiled=True) for part in snd]  9.26 us
    pallas_call x2, Pallas kernels, on_device(): pl.pallas_call(functools.partial(pair_kernel, sz, count), grid_spec=pltpu...  8.6 us
    all_to_all x2, starting transfers between devices, on_device(): preds = [lax.all_to_all(part, 'member', 0, 0, tiled=True) for part in snd]  8.33 us
    pallas_call x1, Pallas kernels, on_device(): pl.pallas_call(functools.partial(data_kernel, sz), grid=(mem,), in_specs=...  7.54 us
    all_to_all x2, waiting for transfers between devices, on_device(): back.append(lax.all_to_all(grads, 'member', 0, 0, tiled=True))  7.08 us
    all_to_all x2, starting transfers between devices, on_device(): back.append(lax.all_to_all(grads, 'member', 0, 0, tiled=True))  7.05 us
  transfers between devices with their start and end apart: 9, of which 6 were waited for; matrix products, arithmetic and copies ran while one was open for 4% of the time, Pallas kernels for 31%

profile of v2, /device:TPU:0, one launch (start us, length us, event | category | flops | bytes accessed | tf_op | source)
XLA Modules:
  0.0 137.7 jit_solution(815947107798629457)
XLA Ops:
  0.6 1.7 %add_convert_fusion = (bf16[2,84,1,128]{3,2,1,0:T(2,128)(2,1)S(1)}, bf16[2,84,1,128]{3,2,1,0:T(2,128)(2,1)S(1)}) fusion(f32[2,84,16,128]{3,2,1,0:T(8,128)} %noise.1, bf16[2,84,16,128]{3,2,1,0:T(8,128)(2,1)} %states.1), kind=kLoop, calls=%fused_computation.1 | loop fusion | flops 129024 | bytes 344064 | tf_op jit(solution)/shard_map/convert_element_type | solution.py:363
  2.4 4.9 %collective-permute-start = (bf16[2,84,1,128]{3,2,1,0:T(2,128)(2,1)S(1)}, bf16[2,84,1,128]{3,2,1,0:T(2,128)(2,1)S(1)}, u32[]{:S(2)}, u32[]{:S(2)}) collective-permute-start(bf16[2,84,1,128]{3,2,1,0:T(2,128)(2,1)S(1)} %get-tuple-element.44), channel_id=1, source_target_pairs={{0,1},{1,2},{2,3},{4,5},{5,6},{6,7},{8,9},{9,10},{10,11},{12,13},{... | collective-permute-start | bytes 129032 | tf_op jit(solution)/shard_map/ppermute | solution.py:365
  7.2 1.3 collective-permute-start.1
  8.5 1.0 copy.14
  9.6 0.0 copy-start.1
  9.6 2.3 %copy.13.w_conv = bf16[512,756]{1,0:T(8,128)(2,1)} copy(bf16[512,756]{0,1:T(8,128)(2,1)} %param.9) | data formatting | bytes 1548288 | tf_op args[3]
  11.9 0.8 copy.15.w_proj
  12.7 5.5 %prep.1 = (bf16[2,256,2048]{2,1,0:T(8,128)(2,1)}, bf16[2,84,2048]{2,1,0:T(8,128)(2,1)}, bf16[2,8,84,128]{3,2,1,0:T(8,128)(2,1)}, bf16[512,768]{1,0:T(8,128)(2,1)}) custom-call(bf16[2,84,16,128]{3,2,1,0:T(8,128)(2,1)} %states.1, f32[2,84,16,128]{3,2,1,0:T(8,128)} %noise.1, bf16[84,16,128]{2,1,0:T(8,128)(2,1)} %target.1, bf16[512,756]{1,0:T(8,128)(2,1)} %copy.13.w_conv), custom_call_target="tpu_custom_call" | custom-call | flops 10000000 | bytes 8000000 | tf_op jit(solution)/shard_map/prep/pallas_call | solution.py:368
  18.2 0.0 copy-done.1
  18.2 0.0 collective-permute-done.halo_up.refs_4_
  18.3 0.0 copy-start.6
  18.3 0.0 collective-permute-done.1.halo_dn.refs_5_
  18.3 0.0 copy-start.7
  18.3 0.6 copy-done.6
  18.9 0.1 copy-done.7
  18.9 9.4 %forward0.1 = (bf16[2,512,1024]{2,1,0:T(8,128)(2,1)}, bf16[2,512,1024]{2,1,0:T(8,128)(2,1)}, bf16[8,168,128]{2,1,0:T(8,128)(2,1)}) custom-call(bf16[2,256,2048]{2,1,0:T(8,128)(2,1)} %get-tuple-element.23.e_in.refs_3_, bf16[2,84,2048]{2,1,0:T(8,128)(2,1)} %get-tuple-element.24.x_in, bf16[2,84,1,128]{3,2,1,0:T(2,128)(2,1)} %copy-done.6, ...), custom_call_target="tpu_custom_call" | custom-call | flops 1610612736 | bytes 9000000 | tf_op jit(solution)/shard_map/forward0/pallas_call | solution.py:399
  28.4 4.9 %all-to-all-start = ((bf16[8,168,128]{2,1,0:T(8,128)(2,1)}), bf16[8,168,128]{2,1,0:T(8,128)(2,1)S(1)}, u32[]{:S(2)}, u32[]{:S(2)}) async-start(bf16[8,168,128]{2,1,0:T(8,128)(2,1)} %get-tuple-element.26), calls=%async_computation | async-start | bytes 688128 | tf_op jit(solution)/shard_map/all_to_all | solution.py:435
  33.3 9.3 %forward1.1 = (bf16[2,512,1024]{2,1,0:T(8,128)(2,1)}, bf16[2,512,1024]{2,1,0:T(8,128)(2,1)}, bf16[8,168,128]{2,1,0:T(8,128)(2,1)}) custom-call(bf16[2,256,2048]{2,1,0:T(8,128)(2,1)} %get-tuple-element.23.e_in.refs_3_, bf16[2,84,2048]{2,1,0:T(8,128)(2,1)} %get-tuple-element.24.x_in, bf16[2,84,1,128]{3,2,1,0:T(2,128)(2,1)} %copy-done.6, ...), custom_call_target="tpu_custom_call" | custom-call | flops 1610612736 | bytes 9000000 | tf_op jit(solution)/shard_map/forward1/pallas_call | solution.py:399
  42.5 0.0 copy-start
  42.6 2.2 %all-to-all-done.preds = bf16[8,168,128]{2,1,0:T(8,128)(2,1)S(1)} async-done(((bf16[8,168,128]{2,1,0:T(8,128)(2,1)}), bf16[8,168,128]{2,1,0:T(8,128)(2,1)S(1)}, u32[]{:S(2)}, u32[]{:S(2)}) %all-to-all-start) | async-done | bytes 344096 | tf_op jit(solution)/shard_map/all_to_all | solution.py:435
  44.8 0.0 copy-start.4
  44.8 3.4 %all-to-all-start.2 = ((bf16[8,168,128]{2,1,0:T(8,128)(2,1)}), bf16[8,168,128]{2,1,0:T(8,128)(2,1)S(1)}, u32[]{:S(2)}, u32[]{:S(2)}) async-start(bf16[8,168,128]{2,1,0:T(8,128)(2,1)} %get-tuple-element.33), calls=%async_computation.2 | async-start | bytes 688128 | tf_op jit(solution)/shard_map/all_to_all | solution.py:435
  48.2 0.0 copy-done.4
  48.2 4.3 %pairs0.1 = bf16[8,168,128]{2,1,0:T(8,128)(2,1)} custom-call(s32[4,16]{1,0:T(4,128)} %match.3, s32[1]{0:T(128)} %bitcast.device, bf16[8,168,128]{2,1,0:T(8,128)(2,1)} %copy-done.4, bf16[2,8,84,128]{3,2,1,0:T(8,128)(2,1)} %get-tuple-element.27.truth), custom_call_target="tpu_custom_call" | custom-call | flops 3604480 | bytes 2000000 | tf_op jit(solution)/shard_map/pairs0/pallas_call | solution.py:438
  52.5 7.1 %all-to-all-done.2.preds = bf16[8,168,128]{2,1,0:T(8,128)(2,1)S(1)} async-done(((bf16[8,168,128]{2,1,0:T(8,128)(2,1)}), bf16[8,168,128]{2,1,0:T(8,128)(2,1)S(1)}, u32[]{:S(2)}, u32[]{:S(2)}) %all-to-all-start.2) | async-done | bytes 344096 | tf_op jit(solution)/shard_map/all_to_all | solution.py:435
  59.6 0.0 copy-start.5
  59.6 3.4 %all-to-all-start.1 = ((bf16[8,168,128]{2,1,0:T(8,128)(2,1)}), bf16[8,168,128]{2,1,0:T(8,128)(2,1)S(1)}, u32[]{:S(2)}, u32[]{:S(2)}) async-start(bf16[8,168,128]{2,1,0:T(8,128)(2,1)} %pairs0.1), calls=%async_computation.1 | async-start | bytes 688128 | tf_op jit(solution)/shard_map/all_to_all | solution.py:465
  63.0 0.0 copy-done.5
  63.0 4.3 %pairs1.1 = bf16[8,168,128]{2,1,0:T(8,128)(2,1)} custom-call(s32[4,16]{1,0:T(4,128)} %match.3, s32[1]{0:T(128)} %bitcast.device, bf16[8,168,128]{2,1,0:T(8,128)(2,1)} %copy-done.5, bf16[2,8,84,128]{3,2,1,0:T(8,128)(2,1)} %get-tuple-element.27.truth), custom_call_target="tpu_custom_call" | custom-call | flops 3604480 | bytes 2000000 | tf_op jit(solution)/shard_map/pairs1/pallas_call | solution.py:438
  67.3 7.1 %all-to-all-done.1.refs_0_ = bf16[8,168,128]{2,1,0:T(8,128)(2,1)S(1)} async-done(((bf16[8,168,128]{2,1,0:T(8,128)(2,1)}), bf16[8,168,128]{2,1,0:T(8,128)(2,1)S(1)}, u32[]{:S(2)}, u32[]{:S(2)}) %all-to-all-start.1) | async-done | bytes 344096 | tf_op jit(solution)/shard_map/all_to_all | solution.py:465
  74.4 0.0 copy-start.3
  74.4 3.6 %all-to-all-start.3 = ((bf16[8,168,128]{2,1,0:T(8,128)(2,1)}), bf16[8,168,128]{2,1,0:T(8,128)(2,1)S(1)}, u32[]{:S(2)}, u32[]{:S(2)}) async-start(bf16[8,168,128]{2,1,0:T(8,128)(2,1)} %pairs1.1), calls=%async_computation.3 | async-start | bytes 688128 | tf_op jit(solution)/shard_map/all_to_all | solution.py:465
  78.1 0.0 copy-done
  78.1 0.1 reshape.22
  78.2 1.0 pad.4.refs_7_.refs_4_
  79.1 0.0 copy-done.3
  79.1 12.4 %weights0.1 = (bf16[2,84,1024]{2,1,0:T(8,128)(2,1)}, bf16[2,512,1024]{2,1,0:T(8,128)(2,1)}, f32[512,852]{1,0:T(8,128)}, f32[2,1,84,128]{3,2,1,0:T(8,128)}) custom-call(bf16[8,168,128]{2,1,0:T(8,128)(2,1)} %copy-done.3, bf16[2,512,1024]{2,1,0:T(8,128)(2,1)} %get-tuple-element.28.refs_1_, bf16[2,512,1024]{2,1,0:T(8,128)(2,1)} %get-tuple-element.29.refs_2_, ...), custom_call_target="tpu_custom_call" | custom-call | flops 1610612736 | bytes 9000000 | tf_op jit(solution)/shard_map/weights0/pallas_call | solution.py:479
  91.6 0.0 all-to-all-done.3.refs_0_
  91.6 0.0 copy-start.2
  91.6 0.7 copy-done.2
  92.3 0.0 copy-start.8
  92.3 12.9 %weights1.1 = (bf16[2,84,1024]{2,1,0:T(8,128)(2,1)}, bf16[2,512,1024]{2,1,0:T(8,128)(2,1)}, bf16[512,896]{1,0:T(8,128)(2,1)}, f32[2,1,84,128]{3,2,1,0:T(8,128)}) custom-call(bf16[8,168,128]{2,1,0:T(8,128)(2,1)} %copy-done.2, bf16[2,512,1024]{2,1,0:T(8,128)(2,1)} %get-tuple-element.34.refs_1_, bf16[2,512,1024]{2,1,0:T(8,128)(2,1)} %get-tuple-element.35.refs_2_, ...), custom_call_target="tpu_custom_call" | custom-call | flops 1610612736 | bytes 9000000 | tf_op jit(solution)/shard_map/weights1/pallas_call | solution.py:479
  105.2 7.0 %all-to-all-start.4 = ((bf16[32,16,896]{2,1,0:T(8,128)(2,1)}), bf16[32,16,896]{2,1,0:T(8,128)(2,1)S(1)}, u32[]{:S(2)}, u32[]{:S(2)}) async-start(bf16[32,16,896]{2,1,0:T(8,128)(2,1)} %bitcast.9), calls=%async_computation.4 | async-start | bytes 1835008 | tf_op jit(solution)/shard_map/all_to_all | solution.py:521
  112.2 3.7 %collective-permute-start.3 = (f32[2,1,84,128]{3,2,1,0:T(8,128)}, f32[2,1,84,128]{3,2,1,0:T(8,128)S(1)}, u32[]{:S(2)}, u32[]{:S(2)}) collective-permute-start(f32[2,1,84,128]{3,2,1,0:T(8,128)} %get-tuple-element.41), channel_id=1, source_target_pairs={{0,1},{1,2},{2,3},{4,5},{5,6},{6,7},{8,9},{9,10},{10,11},{12,13},{... | collective-permute-start | bytes 258056 | tf_op jit(solution)/shard_map/ppermute | solution.py:525
  115.9 0.0 copy-done.8
  115.9 1.3 collective-permute-start.2
  117.2 4.2 %collective-permute-done.3.refs_6_ = f32[2,1,84,128]{3,2,1,0:T(8,128)S(1)} collective-permute-done((f32[2,1,84,128]{3,2,1,0:T(8,128)}, f32[2,1,84,128]{3,2,1,0:T(8,128)S(1)}, u32[]{:S(2)}, u32[]{:S(2)}) %collective-permute-start.3) | collective-permute-done | bytes 86048 | tf_op jit(solution)/shard_map/ppermute | solution.py:525
  121.3 0.0 copy-start.9
  121.3 5.1 %collective-permute-done.2.refs_5_ = f32[2,1,84,128]{3,2,1,0:T(8,128)S(1)} collective-permute-done((f32[2,1,84,128]{3,2,1,0:T(8,128)S(1)}, f32[2,1,84,128]{3,2,1,0:T(8,128)S(1)}, u32[]{:S(2)}, u32[]{:S(2)}) %collective-permute-start.2) | collective-permute-done | bytes 86048 | tf_op jit(solution)/shard_map/ppermute | solution.py:524
  126.4 0.0 copy-start.10
  126.4 0.0 copy-done.9
  126.4 0.6 copy-done.10
  127.1 7.5 %data.1 = bf16[2,84,16,128]{3,2,1,0:T(8,128)(2,1)} custom-call(bf16[2,512,1024]{2,1,0:T(8,128)(2,1)} %get-tuple-element.32.refs_0_, bf16[2,512,1024]{2,1,0:T(8,128)(2,1)} %get-tuple-element.37.refs_1_, bf16[2,84,1024]{2,1,0:T(8,128)(2,1)} %get-tuple-element.38.refs_2_, bf16[2,84,1024]{2,1,0:T(8,128)(2,1)} %get-tuple-element.39.refs_3_, ...), custom_call_target="tpu_custom_call" | custom-call | flops 3221225472 | bytes 8000000 | tf_op jit(solution)/shard_map/data/pallas_call | solution.py:527
  134.6 1.5 %all-to-all-done.4 = bf16[32,16,896]{2,1,0:T(8,128)(2,1)S(1)} async-done(((bf16[32,16,896]{2,1,0:T(8,128)(2,1)}), bf16[32,16,896]{2,1,0:T(8,128)(2,1)S(1)}, u32[]{:S(2)}, u32[]{:S(2)}) %all-to-all-start.4) | async-done | bytes 917536 | tf_op jit(solution)/shard_map/all_to_all | solution.py:521
  136.1 0.1 convert_reduce_fusion
  136.3 0.6 fusion
  136.9 0.7 mul.28
  (4 shorter events, 0.1 us)
Async XLA Ops:
  2.4 15.9 %collective-permute-start = (bf16[2,84,1,128]{3,2,1,0:T(2,128)(2,1)S(1)}, bf16[2,84,1,128]{3,2,1,0:T(2,128)(2,1)S(1)}, u32[]{:S(2)}, u32[]{:S(2)}) collective-permute-start(bf16[2,84,1,128]{3,2,1,0:T(2,128)(2,1)S(1)} %get-tuple-element.44), channel_id=1, source_target_pairs={{0,1},{1,2},{2,3},{4,5},{5,6},{6,7},{8,9},{9,10},{10,11},{12,13},{... | collective-permute-start | bytes 129032 | tf_op jit(solution)/shard_map/ppermute | solution.py:365
  7.2 11.0 %collective-permute-start.1 = (bf16[2,84,1,128]{3,2,1,0:T(2,128)(2,1)S(1)}, bf16[2,84,1,128]{3,2,1,0:T(2,128)(2,1)S(1)}, u32[]{:S(2)}, u32[]{:S(2)}) collective-permute-start(bf16[2,84,1,128]{3,2,1,0:T(2,128)(2,1)S(1)} %get-tuple-element.43), channel_id=1, source_target_pairs={{1,0},{2,1},{3,2},{5,4},{6,5},{7,6},{9,8},{10,9},{11,10},{13,12},{... | collective-permute-start | bytes 129032 | tf_op jit(solution)/shard_map/ppermute | solution.py:366
  9.6 8.6 %copy-start.1 = (bf16[84,512]{0,1:T(8,128)(2,1)}, bf16[84,512]{0,1:T(8,128)(2,1)S(1)}, u32[]{:S(2)}) copy-start(bf16[84,512]{0,1:T(8,128)(2,1)S(1)} %broadcast_multiply_fusion) | copy-start | bytes 258052
  18.3 0.6 copy-start.6
  18.3 0.7 copy-start.7
  28.4 16.4 %all-to-all-start = ((bf16[8,168,128]{2,1,0:T(8,128)(2,1)}), bf16[8,168,128]{2,1,0:T(8,128)(2,1)S(1)}, u32[]{:S(2)}, u32[]{:S(2)}) async-start(bf16[8,168,128]{2,1,0:T(8,128)(2,1)} %get-tuple-element.26), calls=%async_computation | async-start | bytes 688128 | tf_op jit(solution)/shard_map/all_to_all | solution.py:435
  42.5 35.5 %copy-start = (bf16[512,756]{0,1:T(8,128)(2,1)S(1)}, bf16[512,756]{0,1:T(8,128)(2,1)}, u32[]{:S(2)}) copy-start(bf16[512,756]{0,1:T(8,128)(2,1)} %param.9) | copy-start | bytes 2322436
  44.8 3.5 %copy-start.4 = (bf16[8,168,128]{2,1,0:T(8,128)(2,1)}, bf16[8,168,128]{2,1,0:T(8,128)(2,1)S(1)}, u32[]{:S(2)}) copy-start(bf16[8,168,128]{2,1,0:T(8,128)(2,1)S(1)} %all-to-all-done.preds) | copy-start | bytes 1032196
  44.8 14.8 %all-to-all-start.2 = ((bf16[8,168,128]{2,1,0:T(8,128)(2,1)}), bf16[8,168,128]{2,1,0:T(8,128)(2,1)S(1)}, u32[]{:S(2)}, u32[]{:S(2)}) async-start(bf16[8,168,128]{2,1,0:T(8,128)(2,1)} %get-tuple-element.33), calls=%async_computation.2 | async-start | bytes 688128 | tf_op jit(solution)/shard_map/all_to_all | solution.py:435
  59.6 3.4 %copy-start.5 = (bf16[8,168,128]{2,1,0:T(8,128)(2,1)}, bf16[8,168,128]{2,1,0:T(8,128)(2,1)S(1)}, u32[]{:S(2)}) copy-start(bf16[8,168,128]{2,1,0:T(8,128)(2,1)S(1)} %all-to-all-done.2.preds) | copy-start | bytes 1032196
  59.6 14.8 %all-to-all-start.1 = ((bf16[8,168,128]{2,1,0:T(8,128)(2,1)}), bf16[8,168,128]{2,1,0:T(8,128)(2,1)S(1)}, u32[]{:S(2)}, u32[]{:S(2)}) async-start(bf16[8,168,128]{2,1,0:T(8,128)(2,1)} %pairs0.1), calls=%async_computation.1 | async-start | bytes 688128 | tf_op jit(solution)/shard_map/all_to_all | solution.py:465
  74.4 4.7 %copy-start.3 = (bf16[8,168,128]{2,1,0:T(8,128)(2,1)}, bf16[8,168,128]{2,1,0:T(8,128)(2,1)S(1)}, u32[]{:S(2)}) copy-start(bf16[8,168,128]{2,1,0:T(8,128)(2,1)S(1)} %all-to-all-done.1.refs_0_) | copy-start | bytes 1032196
  74.4 17.1 %all-to-all-start.3 = ((bf16[8,168,128]{2,1,0:T(8,128)(2,1)}), bf16[8,168,128]{2,1,0:T(8,128)(2,1)S(1)}, u32[]{:S(2)}, u32[]{:S(2)}) async-start(bf16[8,168,128]{2,1,0:T(8,128)(2,1)} %pairs1.1), calls=%async_computation.3 | async-start | bytes 688128 | tf_op jit(solution)/shard_map/all_to_all | solution.py:465
  91.6 0.7 copy-start.2
  92.3 23.6 %copy-start.8 = (f32[2,1,84,128]{3,2,1,0:T(8,128)S(1)}, f32[2,1,84,128]{3,2,1,0:T(8,128)}, u32[]{:S(2)}) copy-start(f32[2,1,84,128]{3,2,1,0:T(8,128)} %get-tuple-element.40) | copy-start | bytes 258052
  105.2 30.9 %all-to-all-start.4 = ((bf16[32,16,896]{2,1,0:T(8,128)(2,1)}), bf16[32,16,896]{2,1,0:T(8,128)(2,1)S(1)}, u32[]{:S(2)}, u32[]{:S(2)}) async-start(bf16[32,16,896]{2,1,0:T(8,128)(2,1)} %bitcast.9), calls=%async_computation.4 | async-start | bytes 1835008 | tf_op jit(solution)/shard_map/all_to_all | solution.py:521
  112.2 9.2 %collective-permute-start.3 = (f32[2,1,84,128]{3,2,1,0:T(8,128)}, f32[2,1,84,128]{3,2,1,0:T(8,128)S(1)}, u32[]{:S(2)}, u32[]{:S(2)}) collective-permute-start(f32[2,1,84,128]{3,2,1,0:T(8,128)} %get-tuple-element.41), channel_id=1, source_target_pairs={{0,1},{1,2},{2,3},{4,5},{5,6},{6,7},{8,9},{9,10},{10,11},{12,13},{... | collective-permute-start | bytes 258056 | tf_op jit(solution)/shard_map/ppermute | solution.py:525
  115.9 10.6 %collective-permute-start.2 = (f32[2,1,84,128]{3,2,1,0:T(8,128)S(1)}, f32[2,1,84,128]{3,2,1,0:T(8,128)S(1)}, u32[]{:S(2)}, u32[]{:S(2)}) collective-permute-start(f32[2,1,84,128]{3,2,1,0:T(8,128)S(1)} %copy-done.8), channel_id=1, source_target_pairs={{1,0},{2,1},{3,2},{5,4},{6,5},{7,6},{9,8},{10,9},{11,10},{13,12},{... | collective-permute-start | bytes 258056 | tf_op jit(solution)/shard_map/ppermute | solution.py:524
  121.3 5.1 %copy-start.9 = (f32[2,1,84,128]{3,2,1,0:T(8,128)}, f32[2,1,84,128]{3,2,1,0:T(8,128)S(1)}, u32[]{:S(2)}) copy-start(f32[2,1,84,128]{3,2,1,0:T(8,128)S(1)} %collective-permute-done.3.refs_6_) | copy-start | bytes 258052
  126.4 0.6 copy-start.10

commit v3 on v0

v3 whole, which is shorter than its diff:
```python
import functools

import jax
import jax.numpy as jnp
from jax import lax
from jax.experimental import pallas as pl
from jax.experimental.pallas import tpu as pltpu
from jax.sharding import PartitionSpec as P

SQRT_HALF = 0.7071067811865476
INV_ROOT_TWO_PI = 0.3989422804014327
F32 = jnp.float32
BF16 = jnp.bfloat16
LANES = 128
TAPS = 256
LOG2_E = 1.4426950408889634


def call(kernel, name, outs, scratch, flops, moved, args, smem=(), limit=24, aliases=None):
    vmem = pl.BlockSpec(memory_space=pltpu.VMEM)
    scalars = pl.BlockSpec(memory_space=pltpu.SMEM)
    return pl.pallas_call(
        kernel,
        in_specs=[scalars if i in smem else vmem for i in range(len(args))],
        out_specs=[vmem] * len(outs),
        out_shape=[jax.ShapeDtypeStruct(*out) for out in outs],
        scratch_shapes=scratch,
        input_output_aliases=aliases or {},
        compiler_params=pltpu.CompilerParams(vmem_limit_bytes=limit * 1024 * 1024),
        cost_estimate=pl.CostEstimate(flops=flops, bytes_accessed=moved, transcendentals=0),
        name=name,
    )(*args)


def shift_right(vals):
    lane = lax.broadcasted_iota(jnp.int32, vals.shape, 1)
    return jnp.where(lane == 0, 0.0, pltpu.roll(vals, 1, 1))


def shift_left(vals):
    width = vals.shape[1]
    lane = lax.broadcasted_iota(jnp.int32, vals.shape, 1)
    return jnp.where(lane == width - 1, 0.0, pltpu.roll(vals, width - 1, 1))


def expand_row(vals, scratch):
    channels = vals.shape[0]
    scratch[pl.ds(0, channels), :] = shift_right(vals)
    scratch[pl.ds(channels, channels), :] = vals
    scratch[pl.ds(2 * channels, channels), :] = shift_left(vals)
    return scratch[...].astype(BF16)


def swap_blocks(rows):
    parts = len(rows)
    size = rows[0].shape[1] // parts
    lane = lax.broadcasted_iota(jnp.int32, rows[0].shape, 1)
    rows = list(rows)
    bit = 1
    while bit < parts:
        low = (lane & (bit * size)) == 0
        shift = bit * size
        width = rows[0].shape[1]
        for i in range(parts):
            if i & bit:
                continue
            a, b = rows[i], rows[i | bit]
            rows[i] = jnp.where(low, a, pltpu.roll(b, shift, 1))
            rows[i | bit] = jnp.where(low, pltpu.roll(a, width - shift, 1), b)
        bit *= 2
    return rows


class Sizes:
    def __init__(self, states, w_conv, member_count, band_count):
        self.mem, self.ch, self.lat, self.lon = states.shape
        self.hid = w_conv.shape[0]
        self.devs = member_count
        self.bands = band_count
        self.members = self.mem * member_count
        self.prows = self.lat // 8
        self.parts = member_count // self.prows
        self.groups = 8 // self.parts
        self.sub = self.groups * self.ch
        self.subpad = (self.sub + 7) // 8 * 8
        self.pos = self.lat * self.lon
        self.used = 3 * TAPS + self.ch
        self.cols = (self.used + LANES - 1) // LANES * LANES


def prep_kernel(sz, states, noise, target, wt3, e_out, x_out, t_out, w_out, xs, es, ps):
    es[...] = jnp.zeros_like(es)

    def one(m, carry):
        x = (states[m].astype(F32) + noise[m]).astype(BF16)
        xs[...] = x.astype(F32).reshape(sz.ch * sz.lat, sz.lon)
        for row in range(sz.lat):
            vals = xs[pl.ds(row, sz.ch, stride=sz.lat), :]
            x_out[m, :, row * sz.lon : (row + 1) * sz.lon] = vals.astype(BF16)
            e_out[m, :, (row + 1) * sz.lon : (row + 2) * sz.lon] = expand_row(vals, es)
        return carry

    lax.fori_loop(0, sz.mem, one, 0)
    xs[...] = target[...].astype(F32).reshape(sz.ch * sz.lat, sz.lon)
    if sz.subpad > sz.sub:
        ps[...] = jnp.zeros_like(ps)
    for prow in range(sz.prows):
        for group in range(sz.groups):
            first = prow * 8 + group * sz.parts
            rows = [xs[pl.ds(first + i, sz.ch, stride=sz.lat), :] for i in range(sz.parts)]
            for q, out in enumerate(swap_blocks(rows)):
                ps[q, pl.ds(group * sz.ch, sz.ch), :] = out
        for q in range(sz.parts):
            t_out[prow * sz.parts + q] = ps[q].astype(BF16)
    for ro in range(3):
        w_out[:, ro * TAPS : (ro + 1) * TAPS] = wt3[ro].T


def halo_row(sz, halos, band, side, m):
    other = band - 1 if side == 0 else band + 1
    inside = jnp.logical_and(other >= 0, other < sz.bands)
    vals = halos[jnp.clip(other, 0, sz.bands - 1), m].astype(F32)
    return vals * jnp.where(inside, 1.0, 0.0)


def forward_kernel(sz, place, e_in, x_in, halos, w3, w_proj, pre_out, hid_out, ext, snd, es, ps, preds):
    width = sz.lon
    pairs = sz.lat // 2
    es[...] = jnp.zeros_like(es)
    if sz.subpad > sz.sub:
        ps[...] = jnp.zeros_like(ps)

    def one(m, carry):
        ext[m, :, width : width + sz.pos] = e_in[m, :, width : width + sz.pos]
        for side in range(2):
            at = 0 if side == 0 else width + sz.pos
            ext[m, :, at : at + width] = expand_row(halo_row(sz, halos, place[1], side, m), es)

        def conv(pair):
            cols = jnp.concatenate(
                [ext[m, :, (pair * 2 + ro) * width : (pair * 2 + ro + 2) * width] for ro in range(3)],
                axis=0,
            )
            pre_out[m, :, pair * 2 * width : (pair + 1) * 2 * width] = jnp.dot(
                w3[...], cols, preferred_element_type=F32
            )

        def rest(pair):
            here = slice(pair * 2 * width, (pair + 1) * 2 * width)
            preact = pre_out[m, :, here]
            hidden = (preact * (1.0 + lax.erf(preact * SQRT_HALF))).astype(BF16)
            hid_out[m, :, here] = hidden
            pred = x_in[m, :, here].astype(F32) + 0.5 * jnp.dot(
                w_proj[...], hidden, preferred_element_type=F32
            )
            preds[:, here] = pred.astype(BF16).astype(F32)

        conv(0)
        for pair in range(pairs):
            if pair + 1 < pairs:
                conv(pair + 1)
            rest(pair)
        for prow in range(sz.prows):
            for group in range(sz.groups):
                first = prow * 8 + group * sz.parts
                rows = [
                    preds[:, (first + i) * width : (first + i + 1) * width]
                    for i in range(sz.parts)
                ]
                for q, out in enumerate(swap_blocks(rows)):
                    ps[q, pl.ds(group * sz.ch, sz.ch), :] = out
            for q in range(sz.parts):
                snd[prow * sz.parts + q, m] = ps[q].astype(BF16)
        return carry

    lax.fori_loop(0, sz.mem, one, 0)


def slope_kernel(sz, preact, slope):
    rows = 32
    per = sz.hid // rows

    def one(i, carry):
        m = i // per
        at = pl.ds(pl.multiple_of(i % per * rows, rows), rows)
        x = preact[m, at, :]
        twice = 1.0 + lax.erf(x * SQRT_HALF)
        bell = jnp.exp2(x * x * (-0.5 * LOG2_E)) * (2.0 * INV_ROOT_TWO_PI)
        slope[m, at, :] = twice + x * bell
        return carry

    lax.fori_loop(0, sz.mem * per, one, 0)


def pair_kernel(sz, count, match, place, preds, truth, grads, vals, tsc, sums, scale, inv):
    norm = 1.0 / (32.0 * sz.ch)
    members = sz.members
    folds = sz.subpad // 8
    vals[...] = preds[...].reshape(members, sz.subpad, LANES).astype(F32)
    tsc[...] = truth[place[0]].astype(F32)

    def squares(diff):
        return jnp.sum((diff * diff).reshape(folds, 8, LANES), axis=0)

    def first(m, carry):
        own = vals[m]
        sums[pl.ds(pl.multiple_of((count * members + m) * 8, 8), 8), :] = squares(own - tsc[...])
        for k in range(count):
            other = match[k, m]
            inv[k, other] = m
            at = pl.multiple_of((k * members + m) * 8, 8)
            sums[pl.ds(at, 8), :] = squares(own - vals[other])
        return carry

    lax.fori_loop(0, members, first, 0)
    rows = (count + 1) * members
    total = sums[pl.ds(0, rows, stride=8), :]
    for j in range(1, 8):
        total = total + sums[pl.ds(j, rows, stride=8), :]
    step = sz.lon // sz.parts
    while step < LANES:
        total = total + pltpu.roll(total, step, 1)
        step *= 2
    lane = lax.broadcasted_iota(jnp.int32, total.shape, 1)
    for bit in (1, 2):
        total = total + jnp.where(
            (lane & bit) == 0, pltpu.roll(total, LANES - bit, 1), pltpu.roll(total, bit, 1)
        )
    inverse = lax.rsqrt(total * norm + 1e-06)
    scale[pl.ds(0, count * members), :] = inverse[: count * members] * (0.5 / count)
    scale[pl.ds(count * members, members), :] = inverse[count * members :]

    def second(m, carry):
        weight = scale[pl.ds(count * members + m, 1), :]
        acc = None
        own_weight = weight
        for k in range(count):
            back = inv[k, m]
            for other, index in ((match[k, m], k * members + m), (back, k * members + back)):
                part = scale[pl.ds(index, 1), :]
                own_weight = own_weight - part
                term = part * vals[other]
                acc = term if acc is None else acc + term
        out = own_weight * vals[m] + (acc - weight * tsc[...])
        grads[m // sz.mem, m % sz.mem] = out.astype(BF16)
        return carry

    lax.fori_loop(0, members, second, 0)


def fold_taps(part, channels):
    return (
        part[channels : 2 * channels]
        + shift_left(part[0:channels])
        + shift_right(part[2 * channels : 3 * channels])
    )


def weight_sums(sz, core, gpre, hid, ext, gp, store):
    block = sz.hid // sz.devs

    def take(ref):
        rows = []
        for z in range(sz.devs // 2):
            at = pl.ds(pl.multiple_of((2 * z + core) * block, block), block)
            rows.append(jnp.concatenate([ref[m, at, :] for m in range(sz.mem)], axis=1))
        return jnp.concatenate(rows, axis=0)

    dims = (((1,), (1,)), ((), ()))
    left = take(gpre)
    for ro in range(3):
        cols = [ext[m, :, ro * sz.lon : ro * sz.lon + sz.pos] for m in range(sz.mem)]
        store(
            ro * TAPS,
            lax.dot_general(
                left, jnp.concatenate(cols, axis=1), dims, preferred_element_type=F32
            ),
        )
    cols = [gp[m] for m in range(sz.mem)]
    store(
        3 * TAPS,
        0.5
        * lax.dot_general(
            take(hid), jnp.concatenate(cols, axis=1), dims, preferred_element_type=F32
        ),
    )
    store(sz.used, jnp.zeros((sz.hid // 2, sz.cols - sz.used), F32))


def sibling_kernel(sz, place, back, slope, hid, ext, w_proj, wt3, gp, gpre, edges, sib, rows_f, wpt):
    width = sz.lon
    wpt[...] = (w_proj[...].astype(F32) * 0.5).T.astype(BF16)

    def one(m, carry):
        for prow in range(sz.prows):
            for q in range(sz.parts):
                rows_f[q] = back[prow * sz.parts + q, m].astype(F32)
            for group in range(sz.groups):
                outs = swap_blocks(
                    [rows_f[q, pl.ds(group * sz.ch, sz.ch), :] for q in range(sz.parts)]
                )
                for i, out in enumerate(outs):
                    row = prow * 8 + group * sz.parts + i
                    gp[m, :, row * width : (row + 1) * width] = out.astype(BF16)
        for pair in range(sz.lat // 2):
            here = slice(pair * 2 * width, (pair + 1) * 2 * width)
            dhid = jnp.dot(wpt[...], gp[m, :, here], preferred_element_type=F32)
            gpre[m, :, here] = (dhid * slope[m, :, here]).astype(BF16)
        for side in range(2):
            at = 0 if side == 0 else sz.pos - width
            part = jnp.dot(
                wt3[2 * side], gpre[m, :, at : at + width], preferred_element_type=F32
            )
            edges[side, m] = fold_taps(part, sz.ch)
        return carry

    lax.fori_loop(0, sz.mem, one, 0)

    def store(at, term):
        sib[:, at : at + term.shape[1]] = term.astype(BF16)

    weight_sums(sz, 1 - place[2], gpre, hid, ext, gp, store)


def own_kernel(sz, place, gpre, hid, ext, gp, own):
    def store(at, term):
        own[:, at : at + term.shape[1]] = term

    weight_sums(sz, place[2], gpre, hid, ext, gp, store)


def data_kernel(sz, gpre, gp, wt3, from_dn, from_up, out, gs):
    width = sz.lon

    def one(m, carry):
        def two_rows(first):
            low, high = max(first, 0), min(first + 2, sz.lat)
            cols = [gpre[m, :, low * width : high * width]]
            zero = jnp.zeros((sz.hid, width), BF16)
            if first < 0:
                cols.insert(0, zero)
            if first + 2 > sz.lat:
                cols.append(zero)
            return cols[0] if len(cols) == 1 else jnp.concatenate(cols, axis=1)

        for pair in range(sz.lat // 2):
            part = None
            for ro in range(3):
                term = jnp.dot(wt3[ro], two_rows(pair * 2 + 1 - ro), preferred_element_type=F32)
                part = term if part is None else part + term
            for i in range(2):
                row = pair * 2 + i
                at = row * width
                total = gp[m, :, at : at + width].astype(F32) + fold_taps(
                    part[:, i * width : (i + 1) * width], sz.ch
                )
                if row == 0:
                    total = total + from_up[m]
                if row == sz.lat - 1:
                    total = total + from_dn[m]
                gs[pl.ds(row, sz.ch, stride=sz.lat), :] = total
        out[m] = gs[...].reshape(sz.ch, sz.lat, width).astype(BF16)
        return carry

    lax.fori_loop(0, sz.mem, one, 0)


MEMBER = ("pair", "core")


def on_device(states, noise_field, target, w_conv, w_proj, matchings):
    member_count = lax.axis_size("pair") * lax.axis_size("core")
    band_count = lax.axis_size("band")
    sz = Sizes(states, w_conv, member_count, band_count)
    mem, ch, lat, lon, hid, pos = sz.mem, sz.ch, sz.lat, sz.lon, sz.hid, sz.pos
    count = matchings.shape[0]
    down = [(i, i + 1) for i in range(band_count - 1)]
    up = [(i + 1, i) for i in range(band_count - 1)]
    band = lax.axis_index("band").astype(jnp.int32)
    core = lax.axis_index("core").astype(jnp.int32)
    member = lax.axis_index("pair").astype(jnp.int32) * lax.axis_size("core") + core
    place = jnp.stack([member, band, core])

    def edge(row):
        return (states[:, :, row].astype(F32) + noise_field[:, :, row]).astype(BF16)

    after = (jnp.arange(band_count, dtype=jnp.int32) > band)[:, None, None, None]
    halos = lax.all_to_all(
        jnp.where(after, edge(lat - 1)[None], edge(0)[None]), "band", 0, 0, tiled=True
    )
    wt3 = jnp.pad(w_conv.T.reshape(3, 3 * ch, hid), ((0, 0), (0, TAPS - 3 * ch), (0, 0)))

    ext_shape = (mem, TAPS, pos + 2 * lon)
    e_in, x_in, truth, w3 = call(
        functools.partial(prep_kernel, sz),
        "prep",
        [
            (ext_shape, BF16),
            ((mem, ch, pos), BF16),
            ((sz.devs, sz.subpad, LANES), BF16),
            ((hid, 3 * TAPS), BF16),
        ],
        [
            pltpu.VMEM((ch * lat, lon), F32),
            pltpu.VMEM((TAPS, lon), F32),
            pltpu.VMEM((sz.parts, sz.subpad, LANES), F32),
        ],
        10_000_000,
        8_000_000,
        (states, noise_field, target, wt3),
    )

    conv_flops = 2 * mem * pos * hid * 3 * TAPS
    preact, hidden, ext, snd = call(
        functools.partial(forward_kernel, sz),
        "forward",
        [
            ((mem, hid, pos), F32),
            ((mem, hid, pos), BF16),
            (ext_shape, BF16),
            ((sz.devs, mem, sz.subpad, LANES), BF16),
        ],
        [
            pltpu.VMEM((TAPS, lon), F32),
            pltpu.VMEM((sz.parts, sz.subpad, LANES), F32),
            pltpu.VMEM((ch, pos), F32),
        ],
        conv_flops,
        9_000_000,
        (place, e_in, x_in, halos, w3, w_proj),
        smem=(0,),
        aliases={1: 2},
    )

    preds = lax.all_to_all(snd, MEMBER, 0, 0, tiled=True)
    preact, _ = lax.optimization_barrier((preact, snd))
    (slope,) = call(
        functools.partial(slope_kernel, sz),
        "slope",
        [((mem, hid, pos), F32)],
        [],
        10 * mem * hid * pos,
        8 * mem * hid * pos,
        (preact,),
        aliases={0: 0},
    )

    rows = (count + 1) * sz.members
    (grads,) = call(
        functools.partial(pair_kernel, sz, count),
        "pairs",
        [((sz.devs, mem, sz.subpad, LANES), BF16)],
        [
            pltpu.VMEM((sz.members, sz.subpad, LANES), F32),
            pltpu.VMEM((sz.subpad, LANES), F32),
            pltpu.VMEM((rows * 8, LANES), F32),
            pltpu.VMEM((rows, LANES), F32),
            pltpu.SMEM((count, sz.members), jnp.int32),
        ],
        sz.members * 30 * sz.subpad * LANES,
        2_000_000,
        (matchings, place, preds, truth),
        smem=(0, 1),
    )
    back = lax.all_to_all(grads, MEMBER, 0, 0, tiled=True)

    half = (hid // 2, sz.cols)
    grad_pred, grad_pre, edges, sibling = call(
        functools.partial(sibling_kernel, sz),
        "sibling",
        [
            ((mem, ch, pos), BF16),
            ((mem, hid, pos), BF16),
            ((2, mem, ch, lon), F32),
            (half, BF16),
        ],
        [pltpu.VMEM((sz.parts, sz.subpad, LANES), F32), pltpu.VMEM((hid, ch), BF16)],
        conv_flops,
        9_000_000,
        (place, back, slope, hidden, ext, w_proj, wt3),
        smem=(0,),
    )
    swapped = lax.ppermute(sibling, "core", [(0, 1), (1, 0)])
    (own,) = call(
        functools.partial(own_kernel, sz),
        "own",
        [(half, F32)],
        [],
        conv_flops // 2,
        9_000_000,
        (place, grad_pre, hidden, ext, grad_pred),
        smem=(0,),
    )
    shards = member_count * band_count
    each = hid // shards
    partial = (own + swapped.astype(F32)).astype(BF16).reshape(shards // 2, each, sz.cols)
    terms = lax.all_to_all(partial, ("pair", "band"), 0, 0, tiled=True)
    edges, _ = lax.optimization_barrier((edges, own))
    from_dn = lax.ppermute(edges[0], "band", up)
    from_up = lax.ppermute(edges[1], "band", down)

    (grad_states,) = call(
        functools.partial(data_kernel, sz),
        "data",
        [((mem, ch, lat, lon), BF16)],
        [pltpu.VMEM((ch * lat, lon), F32)],
        conv_flops,
        8_000_000,
        (grad_pre, grad_pred, wt3, from_dn, from_up),
    )

    factor = 1.0 / (pos * sz.members * band_count) ** 0.5
    total = jnp.sum(terms.astype(F32), axis=0) * factor
    grad_conv = total[:, : 3 * TAPS].reshape(each, 3, TAPS)[:, :, : 3 * ch].reshape(each, 9 * ch)
    grad_proj = total[:, 3 * TAPS : sz.used].T
    return grad_states, grad_conv, grad_proj


def solution(mesh):
    members = mesh.shape["member"]
    split = jax.sharding.Mesh(
        mesh.devices.reshape(members // 2, 2, mesh.shape["band"]), MEMBER + ("band",)
    )
    return jax.shard_map(
        on_device,
        mesh=split,
        in_specs=(
            P(MEMBER, None, "band", None),
            P(MEMBER, None, "band", None),
            P(None, "band", None),
            P(),
            P(),
            P(),
        ),
        out_specs=(
            P(MEMBER, None, "band", None),
            P(MEMBER + ("band",), None),
            P(None, MEMBER + ("band",)),
        ),
        check_vma=False,
    )
```

time: 418 us -> 128 us (0.31)
  the two profiles are of different devices: /device:TPU:0 before, /device:TPU:20 now
where the time goes in v3:
time: 128 us; the launch traced here: 127 us
  local copies, waits for them, and re-layouts  36.1 us (28%)
  Pallas kernels  29.3 us (23%)
  starting transfers between devices  25.2 us (20%)
  blocking collectives  20.8 us (16%)
  waiting for transfers between devices  12.8 us (10%)
  other arithmetic  1.96 us (2%)
    unnamed x48, local copies, waits for them, and re-layouts  29.7 us
    pallas_call x7, Pallas kernels, call(): pl.pallas_call(kernel, in_specs=[scalars if i in smem else vmem for i in...  29.3 us
    all_to_all x1, blocking collectives, on_device(): preds = lax.all_to_all(snd, MEMBER, 0, 0, tiled=True)  20.8 us
    all_to_all x1, starting transfers between devices, on_device(): terms = lax.all_to_all(partial, ('pair', 'band'), 0, 0, tiled=True)  7.74 us
    all_to_all x1, starting transfers between devices, on_device(): back = lax.all_to_all(grads, MEMBER, 0, 0, tiled=True)  7.13 us
    all_to_all x1, waiting for transfers between devices, on_device(): back = lax.all_to_all(grads, MEMBER, 0, 0, tiled=True)  5.8 us
    all_to_all x1, starting transfers between devices, on_device(): lax.all_to_all(jnp.where(after, edge(lat - 1)[None], edge(0)[None]), 'ban...  4.45 us
    ppermute x1, waiting for transfers between devices, on_device(): from_up = lax.ppermute(edges[1], 'band', down)  3.51 us
  transfers between devices with their start and end apart: 6, of which 3 were waited for; matrix products, arithmetic and copies ran while one was open for 1% of the time, Pallas kernels for 11%

profile of v3, /device:TPU:20, one launch (start us, length us, event | category | flops | bytes accessed | tf_op | source)
XLA Modules:
  0.0 127.1 jit_solution(8797114079239380910)
XLA Ops:
  0.6 0.0 copy-start.14
  0.7 1.5 %fusion.4 = (f32[2,84,1,128]{3,2,1,0:T(1,128)S(1)}, f32[2,84,1,128]{3,2,1,0:T(1,128)S(1)}) fusion(f32[2,84,16,128]{3,2,1,0:T(8,128)} %noise.1), kind=kLoop, calls=%fused_computation.15 | loop fusion | bytes 344064 | tf_op jit(solution)/shard_map/slice | solution.py:385
  2.1 1.2 fusion.5
  3.5 0.9 broadcast_select_fusion
  4.3 4.5 %all-to-all-start = ((bf16[4,2,84,128]{3,1,2,0:T(2,128)(2,1)}), bf16[4,2,84,128]{3,1,2,0:T(2,128)(2,1)}, u32[]{:S(2)}, u32[]{:S(2)}) async-start(bf16[4,2,84,128]{3,1,2,0:T(2,128)(2,1)} %broadcast_select_fusion), calls=%async_computation | async-start | bytes 344064 | tf_op jit(solution)/shard_map/all_to_all | solution.py:388
  8.8 1.2 reshape.50
  10.0 0.1 pad.4.wt3
  10.1 0.0 copy-done.14
  10.1 0.0 copy-start.10
  10.1 1.3 %copy-done.10 = f32[2,84,16,128]{3,2,1,0:T(8,128)S(1)} copy-done((f32[2,84,16,128]{3,2,1,0:T(8,128)S(1)}, f32[2,84,16,128]{3,2,1,0:T(8,128)}, u32[]{:S(2)}) %copy-start.10) | copy-done | bytes 1376280
  11.5 1.1 copy-done.11
  12.6 2.4 %prep.1 = (bf16[2,256,2304]{2,1,0:T(8,128)(2,1)S(1)}, bf16[2,84,2048]{2,1,0:T(8,128)(2,1)S(1)}, bf16[8,168,128]{2,1,0:T(8,128)(2,1)S(1)}, bf16[512,768]{1,0:T(8,128)(2,1)S(1)}) custom-call(bf16[2,84,16,128]{3,2,1,0:T(8,128)(2,1)S(1)} %copy-done.11, f32[2,84,16,128]{3,2,1,0:T(8,128)S(1)} %copy-done.10, bf16[84,16,128]{2,1,0:T(8,128)(2,1)S(1)} %copy-done.14, ...), custom_call_target="tpu_custom_call" | custom-call | flops 10000000 | bytes 8000000 | tf_op jit(solution)/shard_map/prep/pallas_call | solution.py:22
  15.0 0.0 copy-start.15
  15.0 0.7 copy-done.15
  15.7 0.9 copy-done.20
  16.6 0.9 copy-done.22
  17.5 0.1 pad_add_fusion.place
  17.6 0.0 all-to-all-done
  17.6 0.9 copy.21.halos
  18.5 0.0 copy-start.17
  18.5 0.9 copy-done.17
  19.4 1.1 copy-done.21
  20.5 1.1 copy-done.23
  21.6 6.5 %forward.1 = (f32[2,512,2048]{2,1,0:T(8,128)S(1)}, bf16[2,512,2048]{2,1,0:T(8,128)(2,1)S(1)}, bf16[2,256,2304]{2,1,0:T(8,128)(2,1)S(1)}, bf16[8,2,168,128]{3,2,1,0:T(8,128)(2,1)S(1)}) custom-call(s32[3]{0:T(128)S(1)} %pad_add_fusion.place, bf16[2,256,2304]{2,1,0:T(8,128)(2,1)S(1)} %get-tuple-element.17.e_in, ...), custom_call_target="tpu_custom_call", output_to_operand_aliasing={{2}: (1, {})} | custom-call | flops 3221225472 | bytes 9000000 | tf_op jit(solution)/shard_map/forward/pallas_call | solution.py:22
  28.2 0.0 copy-start
  28.2 3.3 %copy-done = f32[2,512,2048]{2,1,0:T(8,128)} copy-done((f32[2,512,2048]{2,1,0:T(8,128)}, f32[2,512,2048]{2,1,0:T(8,128)S(1)}, u32[]{:S(2)}) %copy-start) | copy-done | bytes 8388632
  31.5 2.0 %copy-done.4 = bf16[2,512,2048]{2,1,0:T(8,128)(2,1)} copy-done((bf16[2,512,2048]{2,1,0:T(8,128)(2,1)}, bf16[2,512,2048]{2,1,0:T(8,128)(2,1)S(1)}, u32[]{:S(2)}) %copy-start.4) | copy-done | bytes 4194328
  33.4 20.8 %all_to_all.20.preds = bf16[8,2,168,128]{3,2,1,0:T(8,128)(2,1)S(1)} all-to-all(bf16[8,2,168,128]{3,2,1,0:T(8,128)(2,1)S(1)} %get-tuple-element.20), channel_id=1, replica_groups=mesh['pair'=4,'core'=2,'band'=4] {'pair','core'}, dimensions={0} | all-to-all | bytes 1376256 | tf_op jit(solution)/shard_map/all_to_all | solution.py:435
  54.3 0.0 copy-done.16
  54.3 0.0 copy-done.19
  54.3 3.2 %pairs.1 = bf16[8,2,168,128]{3,2,1,0:T(8,128)(2,1)S(1)} custom-call(s32[4,16]{1,0:T(4,128)S(1)} %copy-done.19, s32[3]{0:T(128)S(1)} %pad_add_fusion.place, bf16[8,2,168,128]{3,2,1,0:T(8,128)(2,1)S(1)} %all_to_all.20.preds, bf16[8,168,128]{2,1,0:T(8,128)(2,1)S(1)} %copy-done.16), custom_call_target="tpu_custom_call" | custom-call | flops 10321920 | bytes 2000000 | tf_op jit(solution)/shard_map/pairs/pallas_call | solution.py:22
  57.5 0.0 copy-start.9
  57.5 0.8 copy-done.9
  58.4 7.1 %all-to-all-start.2 = ((bf16[8,2,168,128]{3,2,1,0:T(8,128)(2,1)}), bf16[8,2,168,128]{3,2,1,0:T(8,128)(2,1)}, u32[]{:S(2)}, u32[]{:S(2)}) async-start(bf16[8,2,168,128]{3,2,1,0:T(8,128)(2,1)} %copy-done.9), calls=%async_computation.2 | async-start | bytes 1376256 | tf_op jit(solution)/shard_map/all_to_all | solution.py:465
  65.5 3.4 %copy-done.1 = f32[2,512,2048]{2,1,0:T(8,128)S(1)} copy-done((f32[2,512,2048]{2,1,0:T(8,128)S(1)}, f32[2,512,2048]{2,1,0:T(8,128)}, u32[]{:S(2)}) %copy-start.1) | copy-done | bytes 8388632
  68.9 3.1 %slope.1 = f32[2,512,2048]{2,1,0:T(8,128)S(1)} custom-call(f32[2,512,2048]{2,1,0:T(8,128)S(1)} %copy-done.1), custom_call_target="tpu_custom_call", output_to_operand_aliasing={{}: (0, {})} | custom-call | flops 20971520 | bytes 16777216 | tf_op jit(solution)/shard_map/slope/pallas_call | solution.py:22
  72.0 0.0 copy-start.2
  72.0 3.3 %copy-done.2 = f32[2,512,2048]{2,1,0:T(8,128)} copy-done((f32[2,512,2048]{2,1,0:T(8,128)}, f32[2,512,2048]{2,1,0:T(8,128)S(1)}, u32[]{:S(2)}) %copy-start.2) | copy-done | bytes 8388632
  75.3 5.8 %all-to-all-done.2.back = bf16[8,2,168,128]{3,2,1,0:T(8,128)(2,1)} async-done(((bf16[8,2,168,128]{3,2,1,0:T(8,128)(2,1)}), bf16[8,2,168,128]{3,2,1,0:T(8,128)(2,1)}, u32[]{:S(2)}, u32[]{:S(2)}) %all-to-all-start.2) | async-done | bytes 688160 | tf_op jit(solution)/shard_map/all_to_all | solution.py:465
  81.1 0.0 copy-done.18
  81.1 3.4 %copy-done.3 = f32[2,512,2048]{2,1,0:T(8,128)S(1)} copy-done((f32[2,512,2048]{2,1,0:T(8,128)S(1)}, f32[2,512,2048]{2,1,0:T(8,128)}, u32[]{:S(2)}) %copy-start.3) | copy-done | bytes 8388632
  84.5 2.2 %copy-done.5 = bf16[2,512,2048]{2,1,0:T(8,128)(2,1)S(1)} copy-done((bf16[2,512,2048]{2,1,0:T(8,128)(2,1)S(1)}, bf16[2,512,2048]{2,1,0:T(8,128)(2,1)}, u32[]{:S(2)}) %copy-start.5) | copy-done | bytes 4194328
  86.6 6.1 %sibling.1 = (bf16[2,84,2048]{2,1,0:T(8,128)(2,1)S(1)}, bf16[2,512,2048]{2,1,0:T(8,128)(2,1)S(1)}, f32[2,2,84,128]{3,2,1,0:T(8,128)S(1)}, bf16[256,896]{1,0:T(8,128)(2,1)S(1)}) custom-call(s32[3]{0:T(128)S(1)} %pad_add_fusion.place, bf16[8,2,168,128]{3,2,1,0:T(8,128)(2,1)} %all-to-all-done.2.back, f32[2,512,2048]{2,1,0:T(8,128)S(1)} %copy-done.3, ...), custom_call_target="tpu_custom_call" | custom-call | flops 3221225472 | bytes 9000000 | tf_op jit(solution)/shard_map/sibling/pallas_call | solution.py:22
  92.7 0.0 copy-start.7
  92.7 0.0 copy-start.12
  92.7 0.1 collective-permute-start.2
  92.8 0.0 copy-done.6
  92.8 2.9 %own.1 = f32[256,896]{1,0:T(8,128)S(1)} custom-call(s32[3]{0:T(128)S(1)} %pad_add_fusion.place, bf16[2,512,2048]{2,1,0:T(8,128)(2,1)S(1)} %get-tuple-element.26.gpre, bf16[2,512,2048]{2,1,0:T(8,128)(2,1)S(1)} %copy-done.6, bf16[2,256,2304]{2,1,0:T(8,128)(2,1)S(1)} %get-tuple-element.25.ext, bf16[2,84,2048]{2,1,0:T(8,128)(2,1)S(1)} %get-tuple-element.27.gp), custom_call_target="tpu_custom_call" | custom-call | flops 1610612736 | bytes 9000000 | tf_op jit(solution)/shard_map/own/pallas_call | solution.py:22
  95.8 0.0 copy-done.7
  95.8 0.0 copy-done.12
  95.8 0.0 collective-permute-done.2
  95.8 0.9 add_convert_fusion
  96.7 7.7 %all-to-all-start.3 = ((bf16[16,16,896]{2,1,0:T(8,128)(2,1)}), bf16[16,16,896]{2,1,0:T(8,128)(2,1)S(1)}, u32[]{:S(2)}, u32[]{:S(2)}) async-start(bf16[16,16,896]{2,1,0:T(8,128)(2,1)} %bitcast.8), calls=%async_computation.3 | async-start | bytes 917504 | tf_op jit(solution)/shard_map/all_to_all | solution.py:497
  104.5 3.4 %collective-permute-start = (f32[2,84,128]{2,1,0:T(8,128)S(1)}, f32[2,84,128]{2,1,0:T(8,128)S(1)}, u32[]{:S(2)}, u32[]{:S(2)}) collective-permute-start(f32[2,84,128]{2,1,0:T(8,128)S(1)} %get-tuple-element.36), channel_id=1, source_target_pairs={{1,0},{2,1},{3,2},{5,4},{6,5},{7,6},{9,8},{10,9},{11,10},{13,12},{... | collective-permute-start | bytes 258056 | tf_op jit(solution)/shard_map/ppermute | solution.py:499
  107.8 2.5 %collective-permute-start.1 = (f32[2,84,128]{2,1,0:T(8,128)S(1)}, f32[2,84,128]{2,1,0:T(8,128)S(1)}, u32[]{:S(2)}, u32[]{:S(2)}) collective-permute-start(f32[2,84,128]{2,1,0:T(8,128)S(1)} %get-tuple-element.35), channel_id=1, source_target_pairs={{0,1},{1,2},{2,3},{4,5},{5,6},{6,7},{8,9},{9,10},{10,11},{12,13},{... | collective-permute-start | bytes 258056 | tf_op jit(solution)/shard_map/ppermute | solution.py:500
  110.3 3.5 %collective-permute-done.from_dn = f32[2,84,128]{2,1,0:T(8,128)S(1)} collective-permute-done((f32[2,84,128]{2,1,0:T(8,128)S(1)}, f32[2,84,128]{2,1,0:T(8,128)S(1)}, u32[]{:S(2)}, u32[]{:S(2)}) %collective-permute-start) | collective-permute-done | bytes 86048 | tf_op jit(solution)/shard_map/ppermute | solution.py:499
  113.8 3.5 %collective-permute-done.1.from_up = f32[2,84,128]{2,1,0:T(8,128)S(1)} collective-permute-done((f32[2,84,128]{2,1,0:T(8,128)S(1)}, f32[2,84,128]{2,1,0:T(8,128)S(1)}, u32[]{:S(2)}, u32[]{:S(2)}) %collective-permute-start.1) | collective-permute-done | bytes 86048 | tf_op jit(solution)/shard_map/ppermute | solution.py:500
  117.3 2.2 %copy-done.8 = bf16[2,512,2048]{2,1,0:T(8,128)(2,1)S(1)} copy-done((bf16[2,512,2048]{2,1,0:T(8,128)(2,1)S(1)}, bf16[2,512,2048]{2,1,0:T(8,128)(2,1)}, u32[]{:S(2)}) %copy-start.8) | copy-done | bytes 4194328
  119.5 1.1 copy-done.13
  120.6 5.0 %data.1 = bf16[2,84,16,128]{3,2,1,0:T(8,128)(2,1)} custom-call(bf16[2,512,2048]{2,1,0:T(8,128)(2,1)S(1)} %copy-done.8, bf16[2,84,2048]{2,1,0:T(8,128)(2,1)S(1)} %copy-done.13, bf16[3,256,512]{2,1,0:T(8,128)(2,1)S(1)} %pad.4.wt3, f32[2,84,128]{2,1,0:T(8,128)S(1)} %collective-permute-done.from_dn, f32[2,84,128]{2,1,0:T(8,128)S(1)} %collective-permute-done.1.from_up), custom_call_target="tpu_custom_call" | custom-call | flops 3221225472 | bytes 8000000 | tf_op jit(solution)/shard_map/data/pallas_call | solution.py:22
  125.7 0.0 all-to-all-done.3
  125.7 0.1 convert_reduce_fusion
  125.8 0.6 slice_bitcast_fusion.2
  126.4 0.7 reshape.53
  (23 shorter events, 0.2 us)
Async XLA Ops:
  0.6 9.5 %copy-start.14 = (bf16[84,16,128]{2,1,0:T(8,128)(2,1)S(1)}, bf16[84,16,128]{2,1,0:T(8,128)(2,1)}, u32[]{:S(2)}) copy-start(bf16[84,16,128]{2,1,0:T(8,128)(2,1)} %target.1) | copy-start | bytes 1032196
  4.3 13.2 %all-to-all-start = ((bf16[4,2,84,128]{3,1,2,0:T(2,128)(2,1)}), bf16[4,2,84,128]{3,1,2,0:T(2,128)(2,1)}, u32[]{:S(2)}, u32[]{:S(2)}) async-start(bf16[4,2,84,128]{3,1,2,0:T(2,128)(2,1)} %broadcast_select_fusion), calls=%async_computation | async-start | bytes 344064 | tf_op jit(solution)/shard_map/all_to_all | solution.py:388
  10.1 1.3 %copy-start.10 = (f32[2,84,16,128]{3,2,1,0:T(8,128)S(1)}, f32[2,84,16,128]{3,2,1,0:T(8,128)}, u32[]{:S(2)}) copy-start(f32[2,84,16,128]{3,2,1,0:T(8,128)} %noise.1) | copy-start | bytes 4128772
  11.5 1.1 copy-start.11
  15.0 0.7 copy-start.15
  15.7 0.9 copy-start.20
  16.6 0.9 copy-start.22
  18.5 0.9 copy-start.17
  19.4 1.1 copy-start.21
  20.5 1.1 copy-start.23
  21.6 32.6 %copy-start.16 = (bf16[8,168,128]{2,1,0:T(8,128)(2,1)S(1)}, bf16[8,168,128]{2,1,0:T(8,128)(2,1)}, u32[]{:S(2)}) copy-start(bf16[8,168,128]{2,1,0:T(8,128)(2,1)} %copy-done.15) | copy-start | bytes 1032196
  21.6 32.6 %copy-start.19 = (s32[4,16]{1,0:T(4,128)S(1)}, s32[4,16]{1,0:T(4,128)}, u32[]{:S(2)}) copy-start(s32[4,16]{1,0:T(4,128)} %match.1) | copy-start | bytes 772
  28.2 3.3 %copy-start = (f32[2,512,2048]{2,1,0:T(8,128)}, f32[2,512,2048]{2,1,0:T(8,128)S(1)}, u32[]{:S(2)}) copy-start(f32[2,512,2048]{2,1,0:T(8,128)S(1)} %get-tuple-element.23.preact) | copy-start | bytes 25165828
  31.4 2.0 %copy-start.4 = (bf16[2,512,2048]{2,1,0:T(8,128)(2,1)}, bf16[2,512,2048]{2,1,0:T(8,128)(2,1)S(1)}, u32[]{:S(2)}) copy-start(bf16[2,512,2048]{2,1,0:T(8,128)(2,1)S(1)} %get-tuple-element.24.hid) | copy-start | bytes 12582916
  57.5 0.8 copy-start.9
  58.4 22.7 %all-to-all-start.2 = ((bf16[8,2,168,128]{3,2,1,0:T(8,128)(2,1)}), bf16[8,2,168,128]{3,2,1,0:T(8,128)(2,1)}, u32[]{:S(2)}, u32[]{:S(2)}) async-start(bf16[8,2,168,128]{3,2,1,0:T(8,128)(2,1)} %copy-done.9), calls=%async_computation.2 | async-start | bytes 1376256 | tf_op jit(solution)/shard_map/all_to_all | solution.py:465
  65.5 3.4 %copy-start.1 = (f32[2,512,2048]{2,1,0:T(8,128)S(1)}, f32[2,512,2048]{2,1,0:T(8,128)}, u32[]{:S(2)}) copy-start(f32[2,512,2048]{2,1,0:T(8,128)} %copy-done) | copy-start | bytes 25165828
  68.9 12.2 %copy-start.18 = (bf16[84,512]{1,0:T(8,128)(2,1)S(1)}, bf16[84,512]{1,0:T(8,128)(2,1)}, u32[]{:S(2)}) copy-start(bf16[84,512]{1,0:T(8,128)(2,1)} %w_proj.3) | copy-start | bytes 258052
  72.0 3.3 %copy-start.2 = (f32[2,512,2048]{2,1,0:T(8,128)}, f32[2,512,2048]{2,1,0:T(8,128)S(1)}, u32[]{:S(2)}) copy-start(f32[2,512,2048]{2,1,0:T(8,128)S(1)} %slope.1) | copy-start | bytes 25165828
  81.1 3.4 %copy-start.3 = (f32[2,512,2048]{2,1,0:T(8,128)S(1)}, f32[2,512,2048]{2,1,0:T(8,128)}, u32[]{:S(2)}) copy-start(f32[2,512,2048]{2,1,0:T(8,128)} %copy-done.2) | copy-start | bytes 25165828
  84.4 2.2 %copy-start.5 = (bf16[2,512,2048]{2,1,0:T(8,128)(2,1)S(1)}, bf16[2,512,2048]{2,1,0:T(8,128)(2,1)}, u32[]{:S(2)}) copy-start(bf16[2,512,2048]{2,1,0:T(8,128)(2,1)} %copy-done.4) | copy-start | bytes 12582916
  86.6 6.2 %copy-start.6 = (bf16[2,512,2048]{2,1,0:T(8,128)(2,1)S(1)}, bf16[2,512,2048]{2,1,0:T(8,128)(2,1)}, u32[]{:S(2)}) copy-start(bf16[2,512,2048]{2,1,0:T(8,128)(2,1)} %copy-done.4) | copy-start | bytes 12582916
  92.7 3.0 %copy-start.7 = (bf16[2,512,2048]{2,1,0:T(8,128)(2,1)}, bf16[2,512,2048]{2,1,0:T(8,128)(2,1)S(1)}, u32[]{:S(2)}) copy-start(bf16[2,512,2048]{2,1,0:T(8,128)(2,1)S(1)} %get-tuple-element.26.gpre) | copy-start | bytes 12582916
  92.7 3.0 %copy-start.12 = (bf16[2,84,2048]{2,1,0:T(8,128)(2,1)}, bf16[2,84,2048]{2,1,0:T(8,128)(2,1)S(1)}, u32[]{:S(2)}) copy-start(bf16[2,84,2048]{2,1,0:T(8,128)(2,1)S(1)} %get-tuple-element.27.gp) | copy-start | bytes 2064388
  92.7 3.0 %collective-permute-start.2 = (bf16[256,896]{1,0:T(8,128)(2,1)S(1)}, bf16[256,896]{1,0:T(8,128)(2,1)S(1)}, u32[]{:S(2)}, u32[]{:S(2)}) collective-permute-start(bf16[256,896]{1,0:T(8,128)(2,1)S(1)} %get-tuple-element.30), channel_id=1, source_target_pairs={{0,4},{4,0},{1,5},{5,1},{2,6},{6,2},{3,7},{7,3},{8,12},{12,8},{9,1... | collective-permute-start | bytes 1376264 | tf_op jit(solution)/shard_map/ppermute | solution.py:483
  96.7 29.0 %all-to-all-start.3 = ((bf16[16,16,896]{2,1,0:T(8,128)(2,1)}), bf16[16,16,896]{2,1,0:T(8,128)(2,1)S(1)}, u32[]{:S(2)}, u32[]{:S(2)}) async-start(bf16[16,16,896]{2,1,0:T(8,128)(2,1)} %bitcast.8), calls=%async_computation.3 | async-start | bytes 917504 | tf_op jit(solution)/shard_map/all_to_all | solution.py:497
  104.5 9.4 %collective-permute-start = (f32[2,84,128]{2,1,0:T(8,128)S(1)}, f32[2,84,128]{2,1,0:T(8,128)S(1)}, u32[]{:S(2)}, u32[]{:S(2)}) collective-permute-start(f32[2,84,128]{2,1,0:T(8,128)S(1)} %get-tuple-element.36), channel_id=1, source_target_pairs={{1,0},{2,1},{3,2},{5,4},{6,5},{7,6},{9,8},{10,9},{11,10},{13,12},{... | collective-permute-start | bytes 258056 | tf_op jit(solution)/shard_map/ppermute | solution.py:499
  107.8 9.5 %collective-permute-start.1 = (f32[2,84,128]{2,1,0:T(8,128)S(1)}, f32[2,84,128]{2,1,0:T(8,128)S(1)}, u32[]{:S(2)}, u32[]{:S(2)}) collective-permute-start(f32[2,84,128]{2,1,0:T(8,128)S(1)} %get-tuple-element.35), channel_id=1, source_target_pairs={{0,1},{1,2},{2,3},{4,5},{5,6},{6,7},{8,9},{9,10},{10,11},{12,13},{... | collective-permute-start | bytes 258056 | tf_op jit(solution)/shard_map/ppermute | solution.py:500
  117.3 2.2 %copy-start.8 = (bf16[2,512,2048]{2,1,0:T(8,128)(2,1)S(1)}, bf16[2,512,2048]{2,1,0:T(8,128)(2,1)}, u32[]{:S(2)}) copy-start(bf16[2,512,2048]{2,1,0:T(8,128)(2,1)} %copy-done.7) | copy-start | bytes 12582916
  119.5 1.1 copy-start.13

commit v4 on v3

v4 whole, which is shorter than its diff:
```python
import functools

import jax
import jax.numpy as jnp
from jax import lax
from jax.experimental import pallas as pl
from jax.experimental.pallas import tpu as pltpu
from jax.sharding import PartitionSpec as P

SQRT_HALF = 0.7071067811865476
INV_ROOT_TWO_PI = 0.3989422804014327
F32 = jnp.float32
BF16 = jnp.bfloat16
LANES = 128
TAPS = 256
LOG2_E = 1.4426950408889634


def call(kernel, name, outs, scratch, flops, moved, args, smem=(), vmem=(), vmem_outs=(), limit=60):
    kinds = {"hbm": pltpu.HBM, "vmem": pltpu.VMEM, "smem": pltpu.SMEM}
    specs = {kind: pl.BlockSpec(memory_space=space) for kind, space in kinds.items()}

    def kind(i):
        return "smem" if i in smem else "vmem" if i in vmem else "hbm"

    return pl.pallas_call(
        kernel,
        in_specs=[specs[kind(i)] for i in range(len(args))],
        out_specs=[specs["vmem" if i in vmem_outs else "hbm"] for i in range(len(outs))],
        out_shape=[jax.ShapeDtypeStruct(*out) for out in outs],
        scratch_shapes=scratch,
        compiler_params=pltpu.CompilerParams(vmem_limit_bytes=limit * 1024 * 1024),
        cost_estimate=pl.CostEstimate(flops=flops, bytes_accessed=moved, transcendentals=0),
        name=name,
    )(*args)


class Copies:
    def __init__(self, sems):
        self.sems, self.used, self.open = sems, 0, []

    def start(self, src, dst):
        copy = pltpu.make_async_copy(src, dst, self.sems.at[self.used])
        self.used += 1
        copy.start()
        self.open.append(copy)
        return copy

    def finish(self, copies=None):
        for copy in list(self.open) if copies is None else copies:
            if any(copy is other for other in self.open):
                self.open = [other for other in self.open if other is not copy]
                copy.wait()


def dma(count):
    return pltpu.SemaphoreType.DMA((count,))


def shift_right(vals):
    lane = lax.broadcasted_iota(jnp.int32, vals.shape, 1)
    return jnp.where(lane == 0, 0.0, pltpu.roll(vals, 1, 1))


def shift_left(vals):
    width = vals.shape[1]
    lane = lax.broadcasted_iota(jnp.int32, vals.shape, 1)
    return jnp.where(lane == width - 1, 0.0, pltpu.roll(vals, width - 1, 1))


def expand_row(vals, scratch):
    channels = vals.shape[0]
    scratch[pl.ds(0, channels), :] = shift_right(vals)
    scratch[pl.ds(channels, channels), :] = vals
    scratch[pl.ds(2 * channels, channels), :] = shift_left(vals)
    return scratch[...].astype(BF16)


def swap_blocks(rows):
    parts = len(rows)
    size = rows[0].shape[1] // parts
    lane = lax.broadcasted_iota(jnp.int32, rows[0].shape, 1)
    rows = list(rows)
    bit = 1
    while bit < parts:
        low = (lane & (bit * size)) == 0
        shift = bit * size
        width = rows[0].shape[1]
        for i in range(parts):
            if i & bit:
                continue
            a, b = rows[i], rows[i | bit]
            rows[i] = jnp.where(low, a, pltpu.roll(b, shift, 1))
            rows[i | bit] = jnp.where(low, pltpu.roll(a, width - shift, 1), b)
        bit *= 2
    return rows


class Sizes:
    def __init__(self, states, w_conv, member_count, band_count):
        self.mem, self.ch, self.lat, self.lon = states.shape
        self.hid = w_conv.shape[0]
        self.devs = member_count
        self.bands = band_count
        self.members = self.mem * member_count
        self.prows = self.lat // 8
        self.parts = member_count // self.prows
        self.groups = 8 // self.parts
        self.sub = self.groups * self.ch
        self.subpad = (self.sub + 7) // 8 * 8
        self.pos = self.lat * self.lon
        self.used = 3 * TAPS + self.ch
        self.cols = (self.used + LANES - 1) // LANES * LANES


def inputs_kernel(sz, place, states, noise, x_out, send, st, ns, xs, xv, sv, rows, sems):
    copies = Copies(sems)
    loads = []
    for m in range(sz.mem):
        loads.append(
            [copies.start(states.at[m], st.at[m]), copies.start(noise.at[m], ns.at[m])]
        )
    for m in range(sz.mem):
        copies.finish(loads[m])
        xs[...] = (st[m].astype(F32) + ns[m]).astype(BF16).astype(F32).reshape(
            sz.ch * sz.lat, sz.lon
        )
        for row in range(sz.lat):
            vals = xs[pl.ds(row, sz.ch, stride=sz.lat), :].astype(BF16)
            xv[m, :, row * sz.lon : (row + 1) * sz.lon] = vals
        first = xs[pl.ds(0, sz.ch, stride=sz.lat), :]
        last = xs[pl.ds(sz.lat - 1, sz.ch, stride=sz.lat), :]
        rows[0, pl.ds(m * sz.ch, sz.ch), :] = first
        rows[1, pl.ds(m * sz.ch, sz.ch), :] = last
        copies.start(xv.at[m], x_out.at[m])
    for other in range(sz.bands):
        after = jnp.where(other > place[1], 1.0, 0.0)
        sv[other] = (rows[1] * after + rows[0] * (1.0 - after)).astype(BF16)
    copies.start(sv, send)
    copies.finish()


def prep_kernel(sz, x_in, target, wt3, e_out, t_out, w_out, xv, tv, wv, ev, tov, wov, xs, es, ps, sems):
    copies = Copies(sems)
    x_loads = [copies.start(x_in.at[m], xv.at[m]) for m in range(sz.mem)]
    t_load = copies.start(target, tv)
    w_load = copies.start(wt3, wv)
    es[...] = jnp.zeros_like(es)
    inner = slice(sz.lon, sz.lon + sz.pos)
    for m in range(sz.mem):
        copies.finish([x_loads[m]])
        for row in range(sz.lat):
            here = slice(row * sz.lon, (row + 1) * sz.lon)
            ev[m, :, here] = expand_row(xv[m, :, here].astype(F32), es)
        copies.start(ev.at[m], e_out.at[m, :, inner])
    copies.finish([t_load])
    xs[...] = tv[...].astype(F32).reshape(sz.ch * sz.lat, sz.lon)
    if sz.subpad > sz.sub:
        ps[...] = jnp.zeros_like(ps)
    for prow in range(sz.prows):
        for group in range(sz.groups):
            first = prow * 8 + group * sz.parts
            rows = [xs[pl.ds(first + i, sz.ch, stride=sz.lat), :] for i in range(sz.parts)]
            for q, out in enumerate(swap_blocks(rows)):
                ps[q, pl.ds(group * sz.ch, sz.ch), :] = out
        for q in range(sz.parts):
            tov[prow * sz.parts + q] = ps[q].astype(BF16)
    copies.start(tov, t_out)
    copies.finish([w_load])
    for ro in range(3):
        wov[:, ro * TAPS : (ro + 1) * TAPS] = wv[ro].T
    copies.start(wov, w_out)
    copies.finish()


def halo_rows(sz, halos, band, side):
    other = band - 1 if side == 0 else band + 1
    inside = jnp.logical_and(other >= 0, other < sz.bands)
    vals = halos[jnp.clip(other, 0, sz.bands - 1)].astype(F32)
    return vals * jnp.where(inside, 1.0, 0.0)


def forward_kernel(
    sz, place, e_in, x_in, halos, w3, w_proj, pre_out, hid_out, ext_out, snd_out,
    ext, xv, hv, wv, wpv, pre, hid, snd, es, ps, preds, hr, sems,
):
    width = sz.lon
    pairs = sz.lat // 2
    copies = Copies(sems)
    inner = slice(width, width + sz.pos)
    load_h = copies.start(halos, hv)
    load_w = copies.start(w3, wv)
    load_e = [copies.start(e_in.at[m, :, inner], ext.at[m, :, inner]) for m in range(sz.mem)]
    load_p = copies.start(w_proj, wpv)
    load_x = [copies.start(x_in.at[m], xv.at[m]) for m in range(sz.mem)]
    es[...] = jnp.zeros_like(es)
    if sz.subpad > sz.sub:
        ps[...] = jnp.zeros_like(ps)
    copies.finish([load_h])
    for side in range(2):
        at = 0 if side == 0 else width + sz.pos
        hr[...] = halo_rows(sz, hv, place[1], side)
        for m in range(sz.mem):
            ext[m, :, at : at + width] = expand_row(hr[pl.ds(m * sz.ch, sz.ch), :], es)
    copies.finish([load_w])

    def conv(m, pair):
        cols = jnp.concatenate(
            [ext[m, :, (pair * 2 + ro) * width : (pair * 2 + ro + 2) * width] for ro in range(3)],
            axis=0,
        )
        pre[m, :, pair * 2 * width : (pair + 1) * 2 * width] = jnp.dot(
            wv[...], cols, preferred_element_type=F32
        )

    def rest(m, pair):
        here = slice(pair * 2 * width, (pair + 1) * 2 * width)
        preact = pre[m, :, here]
        hidden = (preact * (1.0 + lax.erf(preact * SQRT_HALF))).astype(BF16)
        hid[m, :, here] = hidden
        pred = xv[m, :, here].astype(F32) + 0.5 * jnp.dot(
            wpv[...], hidden, preferred_element_type=F32
        )
        preds[:, here] = pred.astype(BF16).astype(F32)

    for m in range(sz.mem):
        copies.finish([load_e[m]])
        copies.start(ext.at[m], ext_out.at[m])
        conv(m, 0)
        copies.finish([load_p, load_x[m]])
        for pair in range(pairs):
            if pair + 1 < pairs:
                conv(m, pair + 1)
            rest(m, pair)
            if pair % 2 == 1:
                here = slice((pair - 1) * 2 * width, (pair + 1) * 2 * width)
                copies.start(pre.at[m, :, here], pre_out.at[m, :, here])
                copies.start(hid.at[m, :, here], hid_out.at[m, :, here])
        for prow in range(sz.prows):
            for group in range(sz.groups):
                first = prow * 8 + group * sz.parts
                rows = [
                    preds[:, (first + i) * width : (first + i + 1) * width]
                    for i in range(sz.parts)
                ]
                for q, out in enumerate(swap_blocks(rows)):
                    ps[q, pl.ds(group * sz.ch, sz.ch), :] = out
            for q in range(sz.parts):
                snd[prow * sz.parts + q, m] = ps[q].astype(BF16)
    copies.start(snd, snd_out)
    copies.finish()


def slope_kernel(preact, slope):
    rows = 32

    def one(i, carry):
        at = pl.ds(pl.multiple_of(i * rows, rows), rows)
        x = preact[0, at, :]
        twice = 1.0 + lax.erf(x * SQRT_HALF)
        bell = jnp.exp2(x * x * (-0.5 * LOG2_E)) * (2.0 * INV_ROOT_TWO_PI)
        slope[0, at, :] = twice + x * bell
        return carry

    lax.fori_loop(0, preact.shape[1] // rows, one, 0)


def pair_kernel(sz, count, match, place, preds, truth, grads_out, pv, tv, grads, vals, tsc, sums, scale, inv, sems):
    norm = 1.0 / (32.0 * sz.ch)
    members = sz.members
    folds = sz.subpad // 8
    copies = Copies(sems)
    copies.start(preds, pv)
    copies.start(truth.at[place[0]], tv)
    copies.finish()
    vals[...] = pv[...].reshape(members, sz.subpad, LANES).astype(F32)
    tsc[...] = tv[...].astype(F32)

    def squares(diff):
        return jnp.sum((diff * diff).reshape(folds, 8, LANES), axis=0)

    def first(m, carry):
        own = vals[m]
        sums[pl.ds(pl.multiple_of((count * members + m) * 8, 8), 8), :] = squares(own - tsc[...])
        for k in range(count):
            other = match[k, m]
            inv[k, other] = m
            at = pl.multiple_of((k * members + m) * 8, 8)
            sums[pl.ds(at, 8), :] = squares(own - vals[other])
        return carry

    lax.fori_loop(0, members, first, 0)
    rows = (count + 1) * members
    total = sums[pl.ds(0, rows, stride=8), :]
    for j in range(1, 8):
        total = total + sums[pl.ds(j, rows, stride=8), :]
    step = sz.lon // sz.parts
    while step < LANES:
        total = total + pltpu.roll(total, step, 1)
        step *= 2
    lane = lax.broadcasted_iota(jnp.int32, total.shape, 1)
    for bit in (1, 2):
        total = total + jnp.where(
            (lane & bit) == 0, pltpu.roll(total, LANES - bit, 1), pltpu.roll(total, bit, 1)
        )
    inverse = lax.rsqrt(total * norm + 1e-06)
    scale[pl.ds(0, count * members), :] = inverse[: count * members] * (0.5 / count)
    scale[pl.ds(count * members, members), :] = inverse[count * members :]

    def second(m, carry):
        weight = scale[pl.ds(count * members + m, 1), :]
        acc = None
        own_weight = weight
        for k in range(count):
            back = inv[k, m]
            for other, index in ((match[k, m], k * members + m), (back, k * members + back)):
                part = scale[pl.ds(index, 1), :]
                own_weight = own_weight - part
                term = part * vals[other]
                acc = term if acc is None else acc + term
        out = own_weight * vals[m] + (acc - weight * tsc[...])
        grads[m // sz.mem, m % sz.mem] = out.astype(BF16)
        return carry

    lax.fori_loop(0, members, second, 0)
    copies.start(grads, grads_out)
    copies.finish()


def fold_taps(part, channels):
    return (
        part[channels : 2 * channels]
        + shift_left(part[0:channels])
        + shift_right(part[2 * channels : 3 * channels])
    )


def weight_sums(sz, core, gpre, hid_half, ext, gp, store):
    block = sz.hid // sz.devs

    def take(ref):
        rows = []
        for z in range(sz.devs // 2):
            at = pl.ds(pl.multiple_of((2 * z + core) * block, block), block)
            rows.append(jnp.concatenate([ref[m, at, :] for m in range(sz.mem)], axis=1))
        return jnp.concatenate(rows, axis=0)

    dims = (((1,), (1,)), ((), ()))
    left = take(gpre)
    for ro in range(3):
        cols = [ext[m, :, ro * sz.lon : ro * sz.lon + sz.pos] for m in range(sz.mem)]
        store(
            ro * TAPS,
            lax.dot_general(
                left, jnp.concatenate(cols, axis=1), dims, preferred_element_type=F32
            ),
        )
    cols = [gp[m] for m in range(sz.mem)]
    store(
        3 * TAPS,
        0.5
        * lax.dot_general(
            jnp.concatenate([hid_half[m] for m in range(sz.mem)], axis=1),
            jnp.concatenate(cols, axis=1),
            dims,
            preferred_element_type=F32,
        ),
    )
    store(sz.used, jnp.zeros((sz.hid // 2, sz.cols - sz.used), F32))


def sibling_kernel(
    sz, place, back, slope_in, hid_in, ext, w_proj, wt3,
    gp, gpre, hid, edge_up, edge_dn, sib,
    bv, sv, wpv, wv, rows_f, wpt, hid_sib, sems,
):
    width = sz.lon
    copies = Copies(sems)
    load_b = copies.start(back, bv)
    load_p = copies.start(w_proj, wpv)
    quarter = sz.pos // 4
    load_s = []
    for m in range(sz.mem):
        for part in range(4):
            at = slice(part * quarter, (part + 1) * quarter)
            load_s.append(copies.start(slope_in.at[m, :, at], sv.at[m, :, at]))
    load_w = copies.start(wt3, wv)
    block = sz.hid // sz.devs
    load_h = []
    for half, core in ((hid_sib, 1 - place[2]), (hid, place[2])):
        for m in range(sz.mem):
            for z in range(sz.devs // 2):
                at = pl.ds(pl.multiple_of((2 * z + core) * block, block), block)
                to = slice(z * block, (z + 1) * block)
                load_h.append(copies.start(hid_in.at[m, at, :], half.at[m, to, :]))
    copies.finish([load_p])
    wpt[...] = (wpv[...].astype(F32) * 0.5).T.astype(BF16)
    copies.finish([load_b])
    for m in range(sz.mem):
        for prow in range(sz.prows):
            for q in range(sz.parts):
                rows_f[q] = bv[prow * sz.parts + q, m].astype(F32)
            for group in range(sz.groups):
                outs = swap_blocks(
                    [rows_f[q, pl.ds(group * sz.ch, sz.ch), :] for q in range(sz.parts)]
                )
                for i, out in enumerate(outs):
                    row = prow * 8 + group * sz.parts + i
                    gp[m, :, row * width : (row + 1) * width] = out.astype(BF16)
        for pair in range(sz.lat // 2):
            here = slice(pair * 2 * width, (pair + 1) * 2 * width)
            if here.start % quarter == 0:
                copies.finish([load_s[m * 4 + here.start // quarter]])
            dhid = jnp.dot(wpt[...], gp[m, :, here], preferred_element_type=F32)
            gpre[m, :, here] = (dhid * sv[m, :, here]).astype(BF16)
    copies.finish([load_w])
    for m in range(sz.mem):
        for side, edge in enumerate((edge_up, edge_dn)):
            at = 0 if side == 0 else sz.pos - width
            part = jnp.dot(
                wv[2 * side], gpre[m, :, at : at + width], preferred_element_type=F32
            )
            edge[m] = fold_taps(part, sz.ch)
    copies.finish(load_h[: len(load_h) // 2])

    def store(at, term):
        sib[:, at : at + term.shape[1]] = term.astype(BF16)

    weight_sums(sz, 1 - place[2], gpre, hid_sib, ext, gp, store)
    copies.finish()


def own_kernel(sz, place, gpre, hid, ext, gp, own):
    def store(at, term):
        own[:, at : at + term.shape[1]] = term

    weight_sums(sz, place[2], gpre, hid, ext, gp, store)


def merge_kernel(own, other, out):
    out[...] = (own[...] + other[...].astype(F32)).astype(BF16)


def data_kernel(sz, gpre, gp, wt3, ov, ev, gs):
    width = sz.lon
    for m in range(sz.mem):

        def two_rows(first):
            low, high = max(first, 0), min(first + 2, sz.lat)
            cols = [gpre[m, :, low * width : high * width]]
            zero = jnp.zeros((sz.hid, width), BF16)
            if first < 0:
                cols.insert(0, zero)
            if first + 2 > sz.lat:
                cols.append(zero)
            return cols[0] if len(cols) == 1 else jnp.concatenate(cols, axis=1)

        for pair in range(sz.lat // 2):
            part = None
            for ro in range(3):
                term = jnp.dot(wt3[ro], two_rows(pair * 2 + 1 - ro), preferred_element_type=F32)
                part = term if part is None else part + term
            for i in range(2):
                row = pair * 2 + i
                at = row * width
                total = gp[m, :, at : at + width].astype(F32) + fold_taps(
                    part[:, i * width : (i + 1) * width], sz.ch
                )
                if row in (0, sz.lat - 1):
                    ev[0 if row == 0 else 1, m] = total
                gs[pl.ds(row, sz.ch, stride=sz.lat), :] = total
        ov[m] = gs[...].reshape(sz.ch, sz.lat, width).astype(BF16)


def border_kernel(sz, part, ev, uv, dv, out, ov, gs, sems):
    width = sz.lon
    copies = Copies(sems)
    for m in range(sz.mem):
        gs[...] = part[m].astype(F32).reshape(sz.ch * sz.lat, width)
        gs[pl.ds(0, sz.ch, stride=sz.lat), :] = ev[0, m] + uv[m]
        gs[pl.ds(sz.lat - 1, sz.ch, stride=sz.lat), :] = ev[1, m] + dv[m]
        ov[m] = gs[...].reshape(sz.ch, sz.lat, width).astype(BF16)
        copies.start(ov.at[m], out.at[m])
    copies.finish()


def final_kernel(sz, factor, terms, conv, proj):
    total = terms[0].astype(F32)
    for i in range(1, terms.shape[0]):
        total = total + terms[i].astype(F32)
    total = total * factor
    taps = 3 * sz.ch
    for ro in range(3):
        conv[:, ro * taps : (ro + 1) * taps] = total[:, ro * TAPS : ro * TAPS + taps]
    proj[...] = total[:, 3 * TAPS : sz.used]


MEMBER = ("pair", "core")


def on_device(states, noise_field, target, w_conv, w_proj, matchings):
    member_count = lax.axis_size("pair") * lax.axis_size("core")
    band_count = lax.axis_size("band")
    sz = Sizes(states, w_conv, member_count, band_count)
    mem, ch, lat, lon, hid, pos = sz.mem, sz.ch, sz.lat, sz.lon, sz.hid, sz.pos
    count = matchings.shape[0]
    down = [(i, i + 1) for i in range(band_count - 1)]
    up = [(i + 1, i) for i in range(band_count - 1)]
    band = lax.axis_index("band").astype(jnp.int32)
    core = lax.axis_index("core").astype(jnp.int32)
    member = lax.axis_index("pair").astype(jnp.int32) * lax.axis_size("core") + core
    place = jnp.stack([member, band, core])

    wt3 = jnp.pad(w_conv.T.reshape(3, 3 * ch, hid), ((0, 0), (0, TAPS - 3 * ch), (0, 0)))
    ext_shape = (mem, TAPS, pos + 2 * lon)
    part_shape = (sz.devs, mem, sz.subpad, LANES)
    flat = pltpu.VMEM((ch * lat, lon), F32)
    taps_row = pltpu.VMEM((TAPS, lon), F32)
    regroup_rows = pltpu.VMEM((sz.parts, sz.subpad, LANES), F32)
    wide_bf = pltpu.VMEM((mem, hid, pos), BF16)
    wide_f = pltpu.VMEM((mem, hid, pos), F32)
    rows_bf = pltpu.VMEM((mem, ch, pos), BF16)
    halo_shape = (band_count, mem * ch, lon)

    x_in, send = call(
        functools.partial(inputs_kernel, sz),
        "inputs",
        [((mem, ch, pos), BF16), (halo_shape, BF16)],
        [
            pltpu.VMEM((mem, ch, lat, lon), BF16),
            pltpu.VMEM((mem, ch, lat, lon), F32),
            flat,
            rows_bf,
            pltpu.VMEM(halo_shape, BF16),
            pltpu.VMEM((2, mem * ch, lon), F32),
            dma(3 * mem + 1),
        ],
        1_000_000,
        4_000_000,
        (place, states, noise_field),
        smem=(0,),
    )
    halos = lax.all_to_all(send, "band", 0, 0, tiled=True)
    e_in, truth, w3 = call(
        functools.partial(prep_kernel, sz),
        "prep",
        [(ext_shape, BF16), ((sz.devs, sz.subpad, LANES), BF16), ((hid, 3 * TAPS), BF16)],
        [
            rows_bf,
            pltpu.VMEM((ch, lat, lon), BF16),
            pltpu.VMEM((3, TAPS, hid), BF16),
            pltpu.VMEM((mem, TAPS, pos), BF16),
            pltpu.VMEM((sz.devs, sz.subpad, LANES), BF16),
            pltpu.VMEM((hid, 3 * TAPS), BF16),
            flat,
            taps_row,
            regroup_rows,
            dma(2 * mem + 4),
        ],
        10_000_000,
        8_000_000,
        (x_in, target, wt3),
    )

    conv_flops = 2 * mem * pos * hid * 3 * TAPS
    preact, hidden, ext, snd = call(
        functools.partial(forward_kernel, sz),
        "forward",
        [((mem, hid, pos), F32), ((mem, hid, pos), BF16), (ext_shape, BF16), (part_shape, BF16)],
        [
            pltpu.VMEM(ext_shape, BF16),
            rows_bf,
            pltpu.VMEM(halo_shape, BF16),
            pltpu.VMEM((hid, 3 * TAPS), BF16),
            pltpu.VMEM(w_proj.shape, BF16),
            wide_f,
            wide_bf,
            pltpu.VMEM(part_shape, BF16),
            taps_row,
            regroup_rows,
            pltpu.VMEM((ch, pos), F32),
            pltpu.VMEM((mem * ch, lon), F32),
            dma(4 + 3 * mem + mem * lat // 2),
        ],
        conv_flops,
        9_000_000,
        (place, e_in, x_in, halos, w3, w_proj),
        smem=(0,),
    )

    preds = lax.all_to_all(snd, MEMBER, 0, 0, tiled=True)
    block = pl.BlockSpec((1, hid // 4, pos), lambda m, i: (m, i, 0))
    slope = pl.pallas_call(
        slope_kernel,
        grid=(mem, 4),
        in_specs=[block],
        out_specs=block,
        out_shape=jax.ShapeDtypeStruct((mem, hid, pos), F32),
        compiler_params=pltpu.CompilerParams(vmem_limit_bytes=16 * 1024 * 1024),
        cost_estimate=pl.CostEstimate(
            flops=10 * mem * hid * pos, bytes_accessed=8 * mem * hid * pos, transcendentals=0
        ),
        name="slope",
    )(preact)

    rows = (count + 1) * sz.members
    (grads,) = call(
        functools.partial(pair_kernel, sz, count),
        "pairs",
        [(part_shape, BF16)],
        [
            pltpu.VMEM(part_shape, BF16),
            pltpu.VMEM((sz.subpad, LANES), BF16),
            pltpu.VMEM(part_shape, BF16),
            pltpu.VMEM((sz.members, sz.subpad, LANES), F32),
            pltpu.VMEM((sz.subpad, LANES), F32),
            pltpu.VMEM((rows * 8, LANES), F32),
            pltpu.VMEM((rows, LANES), F32),
            pltpu.SMEM((count, sz.members), jnp.int32),
            dma(3),
        ],
        sz.members * 30 * sz.subpad * LANES,
        2_000_000,
        (matchings, place, preds, truth),
        smem=(0, 1),
    )
    back = lax.all_to_all(grads, MEMBER, 0, 0, tiled=True)

    half = (hid // 2, sz.cols)
    edge_shape = (mem, ch, lon)
    grad_pred, grad_pre, hid_v, edge_up, edge_dn, sibling = call(
        functools.partial(sibling_kernel, sz),
        "sibling",
        [
            ((mem, ch, pos), BF16),
            ((mem, hid, pos), BF16),
            ((mem, hid // 2, pos), BF16),
            (edge_shape, F32),
            (edge_shape, F32),
            (half, BF16),
        ],
        [
            pltpu.VMEM(part_shape, BF16),
            wide_f,
            pltpu.VMEM(w_proj.shape, BF16),
            pltpu.VMEM((3, TAPS, hid), BF16),
            regroup_rows,
            pltpu.VMEM((hid, ch), BF16),
            pltpu.VMEM((mem, hid // 2, pos), BF16),
            dma(3 + 4 * mem + mem * sz.devs),
        ],
        conv_flops,
        9_000_000,
        (place, back, slope, hidden, ext, w_proj, wt3),
        smem=(0,),
        vmem=(4,),
        vmem_outs=range(6),
        limit=40,
    )
    swapped = lax.ppermute(sibling, "core", [(0, 1), (1, 0)])
    (own,) = call(
        functools.partial(own_kernel, sz),
        "own",
        [(half, F32)],
        [],
        conv_flops // 2,
        9_000_000,
        (place, grad_pre, hid_v, ext, grad_pred),
        smem=(0,),
        vmem=range(1, 5),
        vmem_outs=(0,),
        limit=16,
    )
    (partial,) = call(
        merge_kernel,
        "merge",
        [(half, BF16)],
        [],
        500_000,
        2_000_000,
        (own, swapped),
        vmem=(0, 1),
        vmem_outs=(0,),
        limit=16,
    )
    shards = member_count * band_count
    each = hid // shards
    terms = lax.all_to_all(
        partial.reshape(shards // 2, each, sz.cols), ("pair", "band"), 0, 0, tiled=True
    )
    edge_up, edge_dn, _ = lax.optimization_barrier((edge_up, edge_dn, partial))
    from_dn = lax.ppermute(edge_up, "band", up)
    from_up = lax.ppermute(edge_dn, "band", down)

    part_states, edge_sums = call(
        functools.partial(data_kernel, sz),
        "data",
        [((mem, ch, lat, lon), BF16), ((2,) + edge_shape, F32)],
        [flat],
        conv_flops,
        8_000_000,
        (grad_pre, grad_pred, wt3),
        vmem=range(3),
        vmem_outs=(0, 1),
        limit=16,
    )
    (grad_states,) = call(
        functools.partial(border_kernel, sz),
        "border",
        [((mem, ch, lat, lon), BF16)],
        [
            pltpu.VMEM((mem, ch, lat, lon), BF16),
            flat,
            dma(mem),
        ],
        1_000_000,
        2_000_000,
        (part_states, edge_sums, from_up, from_dn),
        vmem=range(4),
        limit=16,
    )

    factor = 1.0 / (pos * sz.members * band_count) ** 0.5
    grad_conv, grad_proj = call(
        functools.partial(final_kernel, sz, factor),
        "final",
        [((each, 9 * ch), F32), ((each, ch), F32)],
        [],
        500_000,
        500_000,
        (terms,),
        vmem=(0,),
        vmem_outs=(0, 1),
        limit=16,
    )
    return grad_states, grad_conv, grad_proj.T


def solution(mesh):
    members = mesh.shape["member"]
    split = jax.sharding.Mesh(
        mesh.devices.reshape(members // 2, 2, mesh.shape["band"]), MEMBER + ("band",)
    )
    return jax.shard_map(
        on_device,
        mesh=split,
        in_specs=(
            P(MEMBER, None, "band", None),
            P(MEMBER, None, "band", None),
            P(None, "band", None),
            P(),
            P(),
            P(),
        ),
        out_specs=(
            P(MEMBER, None, "band", None),
            P(MEMBER + ("band",), None),
            P(None, MEMBER + ("band",)),
        ),
        check_vma=False,
    )
```

time: 128 us -> 112 us (0.88)
  the two profiles are of different devices: /device:TPU:20 before, /device:TPU:0 now
where the time goes in v4:
time: 112 us; the launch traced here: 111 us
  Pallas kernels  43 us (38%)
  blocking collectives  23.8 us (21%)
  starting transfers between devices  19.8 us (18%)
  local copies, waits for them, and re-layouts  12.8 us (11%)
  waiting for transfers between devices  10.1 us (9%)
    pallas_call x10, Pallas kernels, call(): pl.pallas_call(kernel, in_specs=[specs[kind(i)] for i in range(len(args))...  40.1 us
    all_to_all x1, blocking collectives, on_device(): preds = lax.all_to_all(snd, MEMBER, 0, 0, tiled=True)  23.8 us
    unnamed x22, local copies, waits for them, and re-layouts  10.6 us
    all_to_all x1, waiting for transfers between devices, on_device(): back = lax.all_to_all(grads, MEMBER, 0, 0, tiled=True)  9.14 us
    all_to_all x1, starting transfers between devices, on_device(): halos = lax.all_to_all(send, 'band', 0, 0, tiled=True)  5.2 us
    all_to_all x1, starting transfers between devices, on_device(): lax.all_to_all(partial.reshape(shards // 2, each, sz.cols), ('pair', 'ban...  5.05 us
    all_to_all x1, starting transfers between devices, on_device(): back = lax.all_to_all(grads, MEMBER, 0, 0, tiled=True)  4.4 us
    ppermute x1, starting transfers between devices, on_device(): from_up = lax.ppermute(edge_dn, 'band', down)  3.82 us
  transfers between devices with their start and end apart: 6, of which 3 were waited for; matrix products, arithmetic and copies ran while one was open for 2% of the time, Pallas kernels for 13%

profile of v4, /device:TPU:0, one launch (start us, length us, event | category | flops | bytes accessed | tf_op | source)
XLA Modules:
  0.0 111.0 jit_solution(15024535427212162647)
XLA Ops:
  0.6 0.6 pad_add_fusion.place
  1.2 3.5 %inputs.1 = (bf16[2,84,2048]{2,1,0:T(8,128)(2,1)}, bf16[4,168,128]{2,1,0:T(8,128)(2,1)}) custom-call(s32[3]{0:T(128)} %pad_add_fusion.place, bf16[2,84,16,128]{3,2,1,0:T(8,128)(2,1)} %states.1, f32[2,84,16,128]{3,2,1,0:T(8,128)} %noise.1), custom_call_target="tpu_custom_call" | custom-call | flops 1000000 | bytes 4000000 | tf_op jit(solution)/shard_map/inputs/pallas_call | solution.py:26
  4.7 5.2 %all-to-all-start = ((bf16[4,168,128]{2,1,0:T(8,128)(2,1)}), bf16[4,168,128]{2,1,0:T(8,128)(2,1)S(1)}, u32[]{:S(2)}, u32[]{:S(2)}) async-start(bf16[4,168,128]{2,1,0:T(8,128)(2,1)} %get-tuple-element.26), calls=%async_computation | async-start | bytes 344064 | tf_op jit(solution)/shard_map/all_to_all | solution.py:543
  9.9 1.2 %reshape.12 = bf16[3,252,512]{2,1,0:T(8,128)(2,1)S(1)} reshape(bf16[756,512]{1,0:T(8,128)(2,1)} %bitcast.6) | data formatting | bytes 1548288 | tf_op jit(solution)/shard_map/reshape | solution.py:514
  11.2 1.0 pad.4.wt3
  12.2 3.7 %prep.1 = (bf16[2,256,2304]{2,1,0:T(8,128)(2,1)}, bf16[8,168,128]{2,1,0:T(8,128)(2,1)}, bf16[512,768]{1,0:T(8,128)(2,1)}) custom-call(bf16[2,84,2048]{2,1,0:T(8,128)(2,1)} %get-tuple-element.24.x_in, bf16[84,16,128]{2,1,0:T(8,128)(2,1)} %target.1, bf16[3,256,512]{2,1,0:T(8,128)(2,1)} %pad.4.wt3), custom_call_target="tpu_custom_call" | custom-call | flops 10000000 | bytes 8000000 | tf_op jit(solution)/shard_map/prep/pallas_call | solution.py:26
  15.8 0.0 all-to-all-done.halos
  15.8 0.0 copy-start.10
  15.9 0.7 copy-done.10
  16.5 10.5 %forward.1 = (f32[2,512,2048]{2,1,0:T(8,128)}, bf16[2,512,2048]{2,1,0:T(8,128)(2,1)}, bf16[2,256,2304]{2,1,0:T(8,128)(2,1)}, bf16[8,2,168,128]{3,2,1,0:T(8,128)(2,1)}) custom-call(s32[3]{0:T(128)} %pad_add_fusion.place, bf16[2,256,2304]{2,1,0:T(8,128)(2,1)} %get-tuple-element.25.e_in, bf16[2,84,2048]{2,1,0:T(8,128)(2,1)} %get-tuple-element.24.x_in, ...), custom_call_target="tpu_custom_call" | custom-call | flops 3221225472 | bytes 9000000 | tf_op jit(solution)/shard_map/forward/pallas_call | solution.py:26
  27.0 23.8 %all_to_all.20.preds = bf16[8,2,168,128]{3,2,1,0:T(8,128)(2,1)} all-to-all(bf16[8,2,168,128]{3,2,1,0:T(8,128)(2,1)} %get-tuple-element.28), channel_id=1, replica_groups=mesh['pair'=4,'core'=2,'band'=4] {'pair','core'}, dimensions={0} | all-to-all | bytes 1376256 | tf_op jit(solution)/shard_map/all_to_all | solution.py:591
  50.8 5.3 %pairs.1 = bf16[8,2,168,128]{3,2,1,0:T(8,128)(2,1)} custom-call(s32[4,16]{1,0:T(4,128)} %match.1, s32[3]{0:T(128)} %pad_add_fusion.place, bf16[8,2,168,128]{3,2,1,0:T(8,128)(2,1)} %all_to_all.20.preds, bf16[8,168,128]{2,1,0:T(8,128)(2,1)} %get-tuple-element.29.truth), custom_call_target="tpu_custom_call" | custom-call | flops 10321920 | bytes 2000000 | tf_op jit(solution)/shard_map/pairs/pallas_call | solution.py:26
  56.2 4.4 %all-to-all-start.2 = ((bf16[8,2,168,128]{3,2,1,0:T(8,128)(2,1)}), bf16[8,2,168,128]{3,2,1,0:T(8,128)(2,1)}, u32[]{:S(2)}, u32[]{:S(2)}) async-start(bf16[8,2,168,128]{3,2,1,0:T(8,128)(2,1)} %pairs.1), calls=%async_computation.2 | async-start | bytes 1376256 | tf_op jit(solution)/shard_map/all_to_all | solution.py:627
  60.6 0.0 copy-start.2
  60.6 3.4 %copy-done.2 = f32[2,512,2048]{2,1,0:T(8,128)S(1)} copy-done((f32[2,512,2048]{2,1,0:T(8,128)S(1)}, f32[2,512,2048]{2,1,0:T(8,128)}, u32[]{:S(2)}) %copy-start.2) | copy-done | bytes 8388632
  63.9 0.0 copy-start.1
  63.9 0.0 copy-start.3
  63.9 0.0 copy-start.8
  64.0 0.0 copy-start.9
  64.0 2.9 %slope.1.slope_in = f32[2,512,2048]{2,1,0:T(8,128)S(1)} custom-call(f32[2,512,2048]{2,1,0:T(8,128)S(1)} %copy-done.2), custom_call_target="tpu_custom_call" | custom-call | flops 20971520 | bytes 16777216 | tf_op jit(solution)/shard_map/slope/pallas_call | solution.py:593
  66.8 0.0 copy-start
  66.8 3.3 %copy-done = f32[2,512,2048]{2,1,0:T(8,128)} copy-done((f32[2,512,2048]{2,1,0:T(8,128)}, f32[2,512,2048]{2,1,0:T(8,128)S(1)}, u32[]{:S(2)}) %copy-start) | copy-done | bytes 8388632
  70.1 9.1 %all-to-all-done.2.back = bf16[8,2,168,128]{3,2,1,0:T(8,128)(2,1)} async-done(((bf16[8,2,168,128]{3,2,1,0:T(8,128)(2,1)}), bf16[8,2,168,128]{3,2,1,0:T(8,128)(2,1)}, u32[]{:S(2)}, u32[]{:S(2)}) %all-to-all-start.2) | async-done | bytes 688160 | tf_op jit(solution)/shard_map/all_to_all | solution.py:627
  79.2 0.0 copy-done.1
  79.2 0.0 copy-done.3
  79.2 0.0 copy-done.8
  79.2 0.0 copy-done.9
  79.2 7.7 %sibling.1 = (bf16[2,84,2048]{2,1,0:T(8,128)(2,1)S(1)}, bf16[2,512,2048]{2,1,0:T(8,128)(2,1)S(1)}, bf16[2,256,2048]{2,1,0:T(8,128)(2,1)S(1)}, f32[2,84,128]{2,1,...) custom-call(s32[3]{0:T(128)S(1)} %copy-done.9, bf16[8,2,168,128]{3,2,1,0:T(8,128)(2,1)} %all-to-all-done.2.back, ...), custom_call_target="tpu_custom_call" | custom-call | flops 3221225472 | bytes 9000000 | tf_op jit(solution)/shard_map/sibling/pallas_call | solution.py:26
  87.0 0.0 copy-start.4
  87.0 0.0 copy-start.6
  87.0 0.1 collective-permute-start
  87.1 2.9 %own.1 = f32[256,896]{1,0:T(8,128)S(1)} custom-call(s32[3]{0:T(128)S(1)} %copy-done.9, bf16[2,512,2048]{2,1,0:T(8,128)(2,1)S(1)} %get-tuple-element.33.gpre, bf16[2,256,2048]{2,1,0:T(8,128)(2,1)S(1)} %get-tuple-element.39.hid, bf16[2,256,2304]{2,1,0:T(8,128)(2,1)S(1)} %copy-done.1, bf16[2,84,2048]{2,1,0:T(8,128)(2,1)S(1)} %get-tuple-element.34.gp), custom_call_target="tpu_custom_call" | custom-call | flops 1610612736 | bytes 9000000 | tf_op jit(solution)/shard_map/own/pallas_call | solution.py:26
  90.0 0.0 copy-done.4
  90.0 0.0 copy-done.6
  90.0 0.0 collective-permute-done.other
  90.0 0.9 merge.1
  90.9 5.0 %all-to-all-start.3 = ((bf16[16,16,896]{2,1,0:T(8,128)(2,1)}), bf16[16,16,896]{2,1,0:T(8,128)(2,1)S(1)}, u32[]{:S(2)}, u32[]{:S(2)}) async-start(bf16[16,16,896]{2,1,0:T(8,128)(2,1)} %bitcast.4), calls=%async_computation.3 | async-start | bytes 917504 | tf_op jit(solution)/shard_map/all_to_all | solution.py:688
  95.9 3.8 %collective-permute-start.1 = (f32[2,84,128]{2,1,0:T(8,128)S(1)}, f32[2,84,128]{2,1,0:T(8,128)S(1)}, u32[]{:S(2)}, u32[]{:S(2)}) collective-permute-start(f32[2,84,128]{2,1,0:T(8,128)S(1)} %get-tuple-element.41), channel_id=1, source_target_pairs={{0,1},{1,2},{2,3},{4,5},{5,6},{6,7},{8,9},{9,10},{10,11},{12,13},{... | collective-permute-start | bytes 258056 | tf_op jit(solution)/shard_map/ppermute | solution.py:693
  99.8 1.3 %collective-permute-start.2 = (f32[2,84,128]{2,1,0:T(8,128)S(1)}, f32[2,84,128]{2,1,0:T(8,128)S(1)}, u32[]{:S(2)}, u32[]{:S(2)}) collective-permute-start(f32[2,84,128]{2,1,0:T(8,128)S(1)} %get-tuple-element.42), channel_id=1, source_target_pairs={{1,0},{2,1},{3,2},{5,4},{6,5},{7,6},{9,8},{10,9},{11,10},{13,12},{... | collective-permute-start | bytes 258056 | tf_op jit(solution)/shard_map/ppermute | solution.py:692
  101.1 0.0 copy-start.5
  101.1 2.2 %copy-done.5 = bf16[2,512,2048]{2,1,0:T(8,128)(2,1)S(1)} copy-done((bf16[2,512,2048]{2,1,0:T(8,128)(2,1)S(1)}, bf16[2,512,2048]{2,1,0:T(8,128)(2,1)}, u32[]{:S(2)}) %copy-start.5) | copy-done | bytes 4194328
  103.2 0.0 copy-start.7
  103.2 1.1 copy-done.7
  104.4 3.9 %data.1 = (bf16[2,84,16,128]{3,2,1,0:T(8,128)(2,1)S(1)}, f32[2,2,84,128]{3,2,1,0:T(8,128)S(1)}) custom-call(bf16[2,512,2048]{2,1,0:T(8,128)(2,1)S(1)} %copy-done.5, bf16[2,84,2048]{2,1,0:T(8,128)(2,1)S(1)} %copy-done.7, bf16[3,256,512]{2,1,0:T(8,128)(2,1)S(1)} %copy-done.3), custom_call_target="tpu_custom_call" | custom-call | flops 3221225472 | bytes 8000000 | tf_op jit(solution)/shard_map/data/pallas_call | solution.py:26
  108.3 0.0 collective-permute-done.1.uv
  108.3 0.2 collective-permute-done.2.dv
  108.5 1.0 border.1
  109.5 0.8 all-to-all-done.3.terms
  110.3 0.7 final.1
Async XLA Ops:
  4.7 11.1 %all-to-all-start = ((bf16[4,168,128]{2,1,0:T(8,128)(2,1)}), bf16[4,168,128]{2,1,0:T(8,128)(2,1)S(1)}, u32[]{:S(2)}, u32[]{:S(2)}) async-start(bf16[4,168,128]{2,1,0:T(8,128)(2,1)} %get-tuple-element.26), calls=%async_computation | async-start | bytes 344064 | tf_op jit(solution)/shard_map/all_to_all | solution.py:543
  15.8 0.7 copy-start.10
  56.2 23.1 %all-to-all-start.2 = ((bf16[8,2,168,128]{3,2,1,0:T(8,128)(2,1)}), bf16[8,2,168,128]{3,2,1,0:T(8,128)(2,1)}, u32[]{:S(2)}, u32[]{:S(2)}) async-start(bf16[8,2,168,128]{3,2,1,0:T(8,128)(2,1)} %pairs.1), calls=%async_computation.2 | async-start | bytes 1376256 | tf_op jit(solution)/shard_map/all_to_all | solution.py:627
  60.6 3.4 %copy-start.2 = (f32[2,512,2048]{2,1,0:T(8,128)S(1)}, f32[2,512,2048]{2,1,0:T(8,128)}, u32[]{:S(2)}) copy-start(f32[2,512,2048]{2,1,0:T(8,128)} %get-tuple-element.30.preact) | copy-start | bytes 25165828
  63.9 15.3 %copy-start.1 = (bf16[2,256,2304]{2,1,0:T(8,128)(2,1)S(1)}, bf16[2,256,2304]{2,1,0:T(8,128)(2,1)}, u32[]{:S(2)}) copy-start(bf16[2,256,2304]{2,1,0:T(8,128)(2,1)} %get-tuple-element.32.ext) | copy-start | bytes 7077892
  63.9 15.3 %copy-start.3 = (bf16[3,256,512]{2,1,0:T(8,128)(2,1)S(1)}, bf16[3,256,512]{2,1,0:T(8,128)(2,1)}, u32[]{:S(2)}) copy-start(bf16[3,256,512]{2,1,0:T(8,128)(2,1)} %pad.4.wt3) | copy-start | bytes 2359300
  63.9 15.3 %copy-start.8 = (bf16[84,512]{1,0:T(8,128)(2,1)S(1)}, bf16[84,512]{1,0:T(8,128)(2,1)}, u32[]{:S(2)}) copy-start(bf16[84,512]{1,0:T(8,128)(2,1)} %w_proj.3) | copy-start | bytes 258052
  64.0 15.3 %copy-start.9 = (s32[3]{0:T(128)S(1)}, s32[3]{0:T(128)}, u32[]{:S(2)}) copy-start(s32[3]{0:T(128)} %pad_add_fusion.place) | copy-start | bytes 40
  66.8 3.3 %copy-start = (f32[2,512,2048]{2,1,0:T(8,128)}, f32[2,512,2048]{2,1,0:T(8,128)S(1)}, u32[]{:S(2)}) copy-start(f32[2,512,2048]{2,1,0:T(8,128)S(1)} %slope.1.slope_in) | copy-start | bytes 25165828
  87.0 3.0 %copy-start.4 = (bf16[2,512,2048]{2,1,0:T(8,128)(2,1)}, bf16[2,512,2048]{2,1,0:T(8,128)(2,1)S(1)}, u32[]{:S(2)}) copy-start(bf16[2,512,2048]{2,1,0:T(8,128)(2,1)S(1)} %get-tuple-element.33.gpre) | copy-start | bytes 12582916
  87.0 3.0 %copy-start.6 = (bf16[2,84,2048]{2,1,0:T(8,128)(2,1)}, bf16[2,84,2048]{2,1,0:T(8,128)(2,1)S(1)}, u32[]{:S(2)}) copy-start(bf16[2,84,2048]{2,1,0:T(8,128)(2,1)S(1)} %get-tuple-element.34.gp) | copy-start | bytes 2064388
  87.0 3.0 %collective-permute-start = (bf16[256,896]{1,0:T(8,128)(2,1)S(1)}, bf16[256,896]{1,0:T(8,128)(2,1)S(1)}, u32[]{:S(2)}, u32[]{:S(2)}) collective-permute-start(bf16[256,896]{1,0:T(8,128)(2,1)S(1)} %get-tuple-element.40), channel_id=1, source_target_pairs={{0,4},{4,0},{1,5},{5,1},{2,6},{6,2},{3,7},{7,3},{8,12},{12,8},{9,1... | collective-permute-start | bytes 1376264 | tf_op jit(solution)/shard_map/ppermute | solution.py:660
  90.9 19.4 %all-to-all-start.3 = ((bf16[16,16,896]{2,1,0:T(8,128)(2,1)}), bf16[16,16,896]{2,1,0:T(8,128)(2,1)S(1)}, u32[]{:S(2)}, u32[]{:S(2)}) async-start(bf16[16,16,896]{2,1,0:T(8,128)(2,1)} %bitcast.4), calls=%async_computation.3 | async-start | bytes 917504 | tf_op jit(solution)/shard_map/all_to_all | solution.py:688
  95.9 12.4 %collective-permute-start.1 = (f32[2,84,128]{2,1,0:T(8,128)S(1)}, f32[2,84,128]{2,1,0:T(8,128)S(1)}, u32[]{:S(2)}, u32[]{:S(2)}) collective-permute-start(f32[2,84,128]{2,1,0:T(8,128)S(1)} %get-tuple-element.41), channel_id=1, source_target_pairs={{0,1},{1,2},{2,3},{4,5},{5,6},{6,7},{8,9},{9,10},{10,11},{12,13},{... | collective-permute-start | bytes 258056 | tf_op jit(solution)/shard_map/ppermute | solution.py:693
  99.8 8.7 %collective-permute-start.2 = (f32[2,84,128]{2,1,0:T(8,128)S(1)}, f32[2,84,128]{2,1,0:T(8,128)S(1)}, u32[]{:S(2)}, u32[]{:S(2)}) collective-permute-start(f32[2,84,128]{2,1,0:T(8,128)S(1)} %get-tuple-element.42), channel_id=1, source_target_pairs={{1,0},{2,1},{3,2},{5,4},{6,5},{7,6},{9,8},{10,9},{11,10},{13,12},{... | collective-permute-start | bytes 258056 | tf_op jit(solution)/shard_map/ppermute | solution.py:692
  101.1 2.2 %copy-start.5 = (bf16[2,512,2048]{2,1,0:T(8,128)(2,1)S(1)}, bf16[2,512,2048]{2,1,0:T(8,128)(2,1)}, u32[]{:S(2)}) copy-start(bf16[2,512,2048]{2,1,0:T(8,128)(2,1)} %copy-done.4) | copy-start | bytes 12582916
  103.2 1.1 copy-start.7

commit v5 on v4

--- a/solution.py
+++ b/solution.py
@@ -16,7 +16,10 @@
 LOG2_E = 1.4426950408889634
 
 
-def call(kernel, name, outs, scratch, flops, moved, args, smem=(), vmem=(), vmem_outs=(), limit=60):
+def call(
+    kernel, name, outs, scratch, flops, moved, args,
+    smem=(), vmem=(), vmem_outs=(), limit=60, aliases=None,
+):
     kinds = {"hbm": pltpu.HBM, "vmem": pltpu.VMEM, "smem": pltpu.SMEM}
     specs = {kind: pl.BlockSpec(memory_space=space) for kind, space in kinds.items()}
 
@@ -29,6 +32,7 @@
         out_specs=[specs["vmem" if i in vmem_outs else "hbm"] for i in range(len(outs))],
         out_shape=[jax.ShapeDtypeStruct(*out) for out in outs],
         scratch_shapes=scratch,
+        input_output_aliases=aliases or {},
         compiler_params=pltpu.CompilerParams(vmem_limit_bytes=limit * 1024 * 1024),
         cost_estimate=pl.CostEstimate(flops=flops, bytes_accessed=moved, transcendentals=0),
         name=name,
@@ -113,48 +117,68 @@
         self.cols = (self.used + LANES - 1) // LANES * LANES
 
 
-def inputs_kernel(sz, place, states, noise, x_out, send, st, ns, xs, xv, sv, rows, sems):
+def edges_kernel(sz, place, states, noise, send, st, ns, xs, sv, rows, sems):
     copies = Copies(sems)
     loads = []
     for m in range(sz.mem):
         loads.append(
             [copies.start(states.at[m], st.at[m]), copies.start(noise.at[m], ns.at[m])]
         )
+    for m in range(sz.mem):
+        copies.finish(loads[m])
+        at = pl.ds(m * sz.ch, sz.ch)
+        for side, tile in enumerate((0, sz.lat - 8)):
+            xs[...] = st[m, :, tile : tile + 8, :].astype(F32).reshape(sz.ch * 8, sz.lon)
+            row = xs[pl.ds(0 if side == 0 else 7, sz.ch, stride=8), :]
+            noise_rows = ns.at[m]
+            rows[side, at, :] = row + noise_rows[:, 0 if side == 0 else sz.lat - 1, :]
+    for other in range(sz.bands):
+        after = jnp.where(other > place[1], 1.0, 0.0)
+        sv[other] = (rows[1] * after + rows[0] * (1.0 - after)).astype(BF16)
+    copies.start(sv, send)
+    copies.finish()
+
+
+def prep_kernel(
+    sz, states, noise, w_t, x_out, e_out, w_out, wt3_out,
+    st, ns, wv, xv, ev, wov, wt3v, xs, es, sems,
+):
+    copies = Copies(sems)
+    w_load = copies.start(w_t, wv)
+    loads = []
+    for m in range(sz.mem):
+        loads.append(
+            [copies.start(states.at[m], st.at[m]), copies.start(noise.at[m], ns.at[m])]
+        )
+    es[...] = jnp.zeros_like(es)
+    inner = slice(sz.lon, sz.lon + sz.pos)
+    taps = 3 * sz.ch
+    copies.finish([w_load])
+    for ro in range(3):
+        piece = jnp.concatenate(
+            [wv[ro * taps : (ro + 1) * taps, :], jnp.zeros((TAPS - taps, sz.hid), BF16)], axis=0
+        )
+        wt3v[ro] = piece
+        wov[:, ro * TAPS : (ro + 1) * TAPS] = piece.T
+    copies.start(wov, w_out)
+    copies.start(wt3v, wt3_out)
     for m in range(sz.mem):
         copies.finish(loads[m])
         xs[...] = (st[m].astype(F32) + ns[m]).astype(BF16).astype(F32).reshape(
             sz.ch * sz.lat, sz.lon
         )
         for row in range(sz.lat):
-            vals = xs[pl.ds(row, sz.ch, stride=sz.lat), :].astype(BF16)
-            xv[m, :, row * sz.lon : (row + 1) * sz.lon] = vals
-        first = xs[pl.ds(0, sz.ch, stride=sz.lat), :]
-        last = xs[pl.ds(sz.lat - 1, sz.ch, stride=sz.lat), :]
-        rows[0, pl.ds(m * sz.ch, sz.ch), :] = first
-        rows[1, pl.ds(m * sz.ch, sz.ch), :] = last
+            here = slice(row * sz.lon, (row + 1) * sz.lon)
+            vals = xs[pl.ds(row, sz.ch, stride=sz.lat), :]
+            xv[m, :, here] = vals.astype(BF16)
+            ev[m, :, here] = expand_row(vals, es)
+        copies.start(ev.at[m], e_out.at[m, :, inner])
         copies.start(xv.at[m], x_out.at[m])
-    for other in range(sz.bands):
-        after = jnp.where(other > place[1], 1.0, 0.0)
-        sv[other] = (rows[1] * after + rows[0] * (1.0 - after)).astype(BF16)
-    copies.start(sv, send)
     copies.finish()
 
 
-def prep_kernel(sz, x_in, target, wt3, e_out, t_out, w_out, xv, tv, wv, ev, tov, wov, xs, es, ps, sems):
-    copies = Copies(sems)
-    x_loads = [copies.start(x_in.at[m], xv.at[m]) for m in range(sz.mem)]
-    t_load = copies.start(target, tv)
-    w_load = copies.start(wt3, wv)
-    es[...] = jnp.zeros_like(es)
-    inner = slice(sz.lon, sz.lon + sz.pos)
-    for m in range(sz.mem):
-        copies.finish([x_loads[m]])
-        for row in range(sz.lat):
-            here = slice(row * sz.lon, (row + 1) * sz.lon)
-            ev[m, :, here] = expand_row(xv[m, :, here].astype(F32), es)
-        copies.start(ev.at[m], e_out.at[m, :, inner])
-    copies.finish([t_load])
-    xs[...] = tv[...].astype(F32).reshape(sz.ch * sz.lat, sz.lon)
+def truth_kernel(sz, target, t_out, xs, ps):
+    xs[...] = target[...].astype(F32).reshape(sz.ch * sz.lat, sz.lon)
     if sz.subpad > sz.sub:
         ps[...] = jnp.zeros_like(ps)
     for prow in range(sz.prows):
@@ -164,13 +188,7 @@
             for q, out in enumerate(swap_blocks(rows)):
                 ps[q, pl.ds(group * sz.ch, sz.ch), :] = out
         for q in range(sz.parts):
-            tov[prow * sz.parts + q] = ps[q].astype(BF16)
-    copies.start(tov, t_out)
-    copies.finish([w_load])
-    for ro in range(3):
-        wov[:, ro * TAPS : (ro + 1) * TAPS] = wv[ro].T
-    copies.start(wov, w_out)
-    copies.finish()
+            t_out[prow * sz.parts + q] = ps[q].astype(BF16)
 
 
 def halo_rows(sz, halos, band, side):
@@ -182,15 +200,17 @@
 
 def forward_kernel(
     sz, place, e_in, x_in, halos, w3, w_proj, pre_out, hid_out, ext_out, snd_out,
-    ext, xv, hv, wv, wpv, pre, hid, snd, es, ps, preds, hr, sems,
+    ext, xv, hv, wv, wpv, pre, preb, hid, snd, es, ps, preds, hr, hx, sems,
 ):
     width = sz.lon
     pairs = sz.lat // 2
     copies = Copies(sems)
     inner = slice(width, width + sz.pos)
     load_h = copies.start(halos, hv)
+    load_e = [copies.start(e_in.at[0, :, inner], ext.at[0, :, inner])]
     load_w = copies.start(w3, wv)
-    load_e = [copies.start(e_in.at[m, :, inner], ext.at[m, :, inner]) for m in range(sz.mem)]
+    for m in range(1, sz.mem):
+        load_e.append(copies.start(e_in.at[m, :, inner], ext.at[m, :, inner]))
     load_p = copies.start(w_proj, wpv)
     load_x = [copies.start(x_in.at[m], xv.at[m]) for m in range(sz.mem)]
     es[...] = jnp.zeros_like(es)
@@ -201,7 +221,12 @@
         at = 0 if side == 0 else width + sz.pos
         hr[...] = halo_rows(sz, hv, place[1], side)
         for m in range(sz.mem):
-            ext[m, :, at : at + width] = expand_row(hr[pl.ds(m * sz.ch, sz.ch), :], es)
+            row = expand_row(hr[pl.ds(m * sz.ch, sz.ch), :], es)
+            ext[m, :, at : at + width] = row
+            hx[side, m] = row
+    for side in range(2):
+        at = 0 if side == 0 else width + sz.pos
+        copies.start(hx.at[side], ext_out.at[:, :, at : at + width])
     copies.finish([load_w])
 
     def conv(m, pair):
@@ -209,13 +234,12 @@
             [ext[m, :, (pair * 2 + ro) * width : (pair * 2 + ro + 2) * width] for ro in range(3)],
             axis=0,
         )
-        pre[m, :, pair * 2 * width : (pair + 1) * 2 * width] = jnp.dot(
-            wv[...], cols, preferred_element_type=F32
-        )
+        pre[pair % 2] = jnp.dot(wv[...], cols, preferred_element_type=F32)
 
     def rest(m, pair):
         here = slice(pair * 2 * width, (pair + 1) * 2 * width)
-        preact = pre[m, :, here]
+        preact = pre[pair % 2]
+        preb[m, :, here] = preact.astype(BF16)
         hidden = (preact * (1.0 + lax.erf(preact * SQRT_HALF))).astype(BF16)
         hid[m, :, here] = hidden
         pred = xv[m, :, here].astype(F32) + 0.5 * jnp.dot(
@@ -225,7 +249,6 @@
 
     for m in range(sz.mem):
         copies.finish([load_e[m]])
-        copies.start(ext.at[m], ext_out.at[m])
         conv(m, 0)
         copies.finish([load_p, load_x[m]])
         for pair in range(pairs):
@@ -234,7 +257,7 @@
             rest(m, pair)
             if pair % 2 == 1:
                 here = slice((pair - 1) * 2 * width, (pair + 1) * 2 * width)
-                copies.start(pre.at[m, :, here], pre_out.at[m, :, here])
+                copies.start(preb.at[m, :, here], pre_out.at[m, :, here])
                 copies.start(hid.at[m, :, here], hid_out.at[m, :, here])
         for prow in range(sz.prows):
             for group in range(sz.groups):
@@ -246,8 +269,8 @@
                 for q, out in enumerate(swap_blocks(rows)):
                     ps[q, pl.ds(group * sz.ch, sz.ch), :] = out
             for q in range(sz.parts):
-                snd[prow * sz.parts + q, m] = ps[q].astype(BF16)
-    copies.start(snd, snd_out)
+                snd[m, prow * sz.parts + q] = ps[q].astype(BF16)
+        copies.start(snd.at[m], snd_out.at[:, m])
     copies.finish()
 
 
@@ -256,7 +279,7 @@
 
     def one(i, carry):
         at = pl.ds(pl.multiple_of(i * rows, rows), rows)
-        x = preact[0, at, :]
+        x = preact[0, at, :].astype(F32)
         twice = 1.0 + lax.erf(x * SQRT_HALF)
         bell = jnp.exp2(x * x * (-0.5 * LOG2_E)) * (2.0 * INV_ROOT_TWO_PI)
         slope[0, at, :] = twice + x * bell
@@ -265,16 +288,13 @@
     lax.fori_loop(0, preact.shape[1] // rows, one, 0)
 
 
-def pair_kernel(sz, count, match, place, preds, truth, grads_out, pv, tv, grads, vals, tsc, sums, scale, inv, sems):
+def pair_kernel(sz, count, match, place, preds, truth, grads_out, grads, vals, tsc, sums, scale, inv, sems):
     norm = 1.0 / (32.0 * sz.ch)
     members = sz.members
     folds = sz.subpad // 8
     copies = Copies(sems)
-    copies.start(preds, pv)
-    copies.start(truth.at[place[0]], tv)
-    copies.finish()
-    vals[...] = pv[...].reshape(members, sz.subpad, LANES).astype(F32)
-    tsc[...] = tv[...].astype(F32)
+    vals[...] = preds[...].reshape(members, sz.subpad, LANES).astype(F32)
+    tsc[...] = truth[place[0]].astype(F32)
 
     def squares(diff):
         return jnp.sum((diff * diff).reshape(folds, 8, LANES), axis=0)
@@ -307,7 +327,7 @@
     scale[pl.ds(0, count * members), :] = inverse[: count * members] * (0.5 / count)
     scale[pl.ds(count * members, members), :] = inverse[count * members :]
 
-    def second(m, carry):
+    def second(m):
         weight = scale[pl.ds(count * members + m, 1), :]
         acc = None
         own_weight = weight
@@ -318,12 +338,19 @@
                 own_weight = own_weight - part
                 term = part * vals[other]
                 acc = term if acc is None else acc + term
-        out = own_weight * vals[m] + (acc - weight * tsc[...])
-        grads[m // sz.mem, m % sz.mem] = out.astype(BF16)
-        return carry
-
-    lax.fori_loop(0, members, second, 0)
-    copies.start(grads, grads_out)
+        return (own_weight * vals[m] + (acc - weight * tsc[...])).astype(BF16)
+
+    quarter = sz.devs // 4
+    for part in range(4):
+
+        def several(i, carry):
+            m = part * (members // 4) + i
+            grads[m // sz.mem, m % sz.mem] = second(m)
+            return carry
+
+        lax.fori_loop(0, members // 4, several, 0)
+        at = slice(part * quarter, (part + 1) * quarter)
+        copies.start(grads.at[at], grads_out.at[at])
     copies.finish()
 
 
@@ -370,21 +397,18 @@
 
 
 def sibling_kernel(
-    sz, place, back, slope_in, hid_in, ext, w_proj, wt3,
-    gp, gpre, hid, edge_up, edge_dn, sib,
-    bv, sv, wpv, wv, rows_f, wpt, hid_sib, sems,
+    sz, place, back, slope_in, hid_in, ext, w_proj, wt3_in, gp, gpre, hid, edge_up, edge_dn, sib,
+    slope, hid_sib, wt3, rows_f, wpt, sems,
 ):
     width = sz.lon
     copies = Copies(sems)
-    load_b = copies.start(back, bv)
-    load_p = copies.start(w_proj, wpv)
     quarter = sz.pos // 4
     load_s = []
     for m in range(sz.mem):
         for part in range(4):
             at = slice(part * quarter, (part + 1) * quarter)
-            load_s.append(copies.start(slope_in.at[m, :, at], sv.at[m, :, at]))
-    load_w = copies.start(wt3, wv)
+            load_s.append(copies.start(slope_in.at[m, :, at], slope.at[m, :, at]))
+    load_w = copies.start(wt3_in, wt3)
     block = sz.hid // sz.devs
     load_h = []
     for half, core in ((hid_sib, 1 - place[2]), (hid, place[2])):
@@ -393,13 +417,11 @@
                 at = pl.ds(pl.multiple_of((2 * z + core) * block, block), block)
                 to = slice(z * block, (z + 1) * block)
                 load_h.append(copies.start(hid_in.at[m, at, :], half.at[m, to, :]))
-    copies.finish([load_p])
-    wpt[...] = (wpv[...].astype(F32) * 0.5).T.astype(BF16)
-    copies.finish([load_b])
+    wpt[...] = (w_proj[...].astype(F32) * 0.5).T.astype(BF16)
     for m in range(sz.mem):
         for prow in range(sz.prows):
             for q in range(sz.parts):
-                rows_f[q] = bv[prow * sz.parts + q, m].astype(F32)
+                rows_f[q] = back[prow * sz.parts + q, m].astype(F32)
             for group in range(sz.groups):
                 outs = swap_blocks(
                     [rows_f[q, pl.ds(group * sz.ch, sz.ch), :] for q in range(sz.parts)]
@@ -412,20 +434,20 @@
             if here.start % quarter == 0:
                 copies.finish([load_s[m * 4 + here.start // quarter]])
             dhid = jnp.dot(wpt[...], gp[m, :, here], preferred_element_type=F32)
-            gpre[m, :, here] = (dhid * sv[m, :, here]).astype(BF16)
+            gpre[m, :, here] = (dhid * slope[m, :, here]).astype(BF16)
     copies.finish([load_w])
     for m in range(sz.mem):
         for side, edge in enumerate((edge_up, edge_dn)):
             at = 0 if side == 0 else sz.pos - width
             part = jnp.dot(
-                wv[2 * side], gpre[m, :, at : at + width], preferred_element_type=F32
+                wt3[2 * side], gpre[m, :, at : at + width], preferred_element_type=F32
             )
             edge[m] = fold_taps(part, sz.ch)
-    copies.finish(load_h[: len(load_h) // 2])
 
     def store(at, term):
         sib[:, at : at + term.shape[1]] = term.astype(BF16)
 
+    copies.finish(load_h[: len(load_h) // 2])
     weight_sums(sz, 1 - place[2], gpre, hid_sib, ext, gp, store)
     copies.finish()
 
@@ -511,84 +533,99 @@
     member = lax.axis_index("pair").astype(jnp.int32) * lax.axis_size("core") + core
     place = jnp.stack([member, band, core])
 
-    wt3 = jnp.pad(w_conv.T.reshape(3, 3 * ch, hid), ((0, 0), (0, TAPS - 3 * ch), (0, 0)))
     ext_shape = (mem, TAPS, pos + 2 * lon)
     part_shape = (sz.devs, mem, sz.subpad, LANES)
     flat = pltpu.VMEM((ch * lat, lon), F32)
     taps_row = pltpu.VMEM((TAPS, lon), F32)
     regroup_rows = pltpu.VMEM((sz.parts, sz.subpad, LANES), F32)
     wide_bf = pltpu.VMEM((mem, hid, pos), BF16)
-    wide_f = pltpu.VMEM((mem, hid, pos), F32)
     rows_bf = pltpu.VMEM((mem, ch, pos), BF16)
     halo_shape = (band_count, mem * ch, lon)
 
-    x_in, send = call(
-        functools.partial(inputs_kernel, sz),
-        "inputs",
-        [((mem, ch, pos), BF16), (halo_shape, BF16)],
+    both_bf = pltpu.VMEM((mem, ch, lat, lon), BF16)
+    both_f = pltpu.VMEM((mem, ch, lat, lon), F32)
+    (send,) = call(
+        functools.partial(edges_kernel, sz),
+        "edges",
+        [(halo_shape, BF16)],
         [
-            pltpu.VMEM((mem, ch, lat, lon), BF16),
-            pltpu.VMEM((mem, ch, lat, lon), F32),
-            flat,
-            rows_bf,
+            both_bf,
+            both_f,
+            pltpu.VMEM((ch * 8, lon), F32),
             pltpu.VMEM(halo_shape, BF16),
             pltpu.VMEM((2, mem * ch, lon), F32),
-            dma(3 * mem + 1),
+            dma(2 * mem + 1),
         ],
         1_000_000,
-        4_000_000,
+        3_000_000,
         (place, states, noise_field),
         smem=(0,),
     )
     halos = lax.all_to_all(send, "band", 0, 0, tiled=True)
-    e_in, truth, w3 = call(
+    x_in, e_in, w3, wt3 = call(
         functools.partial(prep_kernel, sz),
         "prep",
-        [(ext_shape, BF16), ((sz.devs, sz.subpad, LANES), BF16), ((hid, 3 * TAPS), BF16)],
+        [((mem, ch, pos), BF16), (ext_shape, BF16), ((hid, 3 * TAPS), BF16), ((3, TAPS, hid), BF16)],
         [
+            both_bf,
+            both_f,
+            pltpu.VMEM((9 * ch, hid), BF16),
             rows_bf,
-            pltpu.VMEM((ch, lat, lon), BF16),
+            pltpu.VMEM((mem, TAPS, pos), BF16),
+            pltpu.VMEM((hid, 3 * TAPS), BF16),
             pltpu.VMEM((3, TAPS, hid), BF16),
-            pltpu.VMEM((mem, TAPS, pos), BF16),
-            pltpu.VMEM((sz.devs, sz.subpad, LANES), BF16),
-            pltpu.VMEM((hid, 3 * TAPS), BF16),
             flat,
             taps_row,
-            regroup_rows,
-            dma(2 * mem + 4),
+            dma(4 * mem + 3),
         ],
         10_000_000,
         8_000_000,
-        (x_in, target, wt3),
+        (states, noise_field, w_conv.T),
     )
 
     conv_flops = 2 * mem * pos * hid * 3 * TAPS
     preact, hidden, ext, snd = call(
         functools.partial(forward_kernel, sz),
         "forward",
-        [((mem, hid, pos), F32), ((mem, hid, pos), BF16), (ext_shape, BF16), (part_shape, BF16)],
+        [((mem, hid, pos), BF16), ((mem, hid, pos), BF16), (ext_shape, BF16), (part_shape, BF16)],
         [
             pltpu.VMEM(ext_shape, BF16),
             rows_bf,
             pltpu.VMEM(halo_shape, BF16),
             pltpu.VMEM((hid, 3 * TAPS), BF16),
             pltpu.VMEM(w_proj.shape, BF16),
-            wide_f,
+            pltpu.VMEM((2, hid, 2 * lon), F32),
             wide_bf,
-            pltpu.VMEM(part_shape, BF16),
+            wide_bf,
+            pltpu.VMEM((mem, sz.devs, sz.subpad, LANES), BF16),
             taps_row,
             regroup_rows,
             pltpu.VMEM((ch, pos), F32),
             pltpu.VMEM((mem * ch, lon), F32),
-            dma(4 + 3 * mem + mem * lat // 2),
+            pltpu.VMEM((2, mem, TAPS, lon), BF16),
+            dma(5 + 3 * mem + mem * lat // 2),
         ],
         conv_flops,
         9_000_000,
         (place, e_in, x_in, halos, w3, w_proj),
         smem=(0,),
+        aliases={1: 2},
     )
 
     preds = lax.all_to_all(snd, MEMBER, 0, 0, tiled=True)
+    late_target, _ = lax.optimization_barrier((target, snd))
+    (truth,) = call(
+        functools.partial(truth_kernel, sz),
+        "truth",
+        [((sz.devs, sz.subpad, LANES), BF16)],
+        [flat, regroup_rows],
+        5_000_000,
+        2_000_000,
+        (late_target,),
+        vmem=(0,),
+        vmem_outs=(0,),
+        limit=16,
+    )
     block = pl.BlockSpec((1, hid // 4, pos), lambda m, i: (m, i, 0))
     slope = pl.pallas_call(
         slope_kernel,
@@ -610,25 +647,25 @@
         [(part_shape, BF16)],
         [
             pltpu.VMEM(part_shape, BF16),
-            pltpu.VMEM((sz.subpad, LANES), BF16),
-            pltpu.VMEM(part_shape, BF16),
             pltpu.VMEM((sz.members, sz.subpad, LANES), F32),
             pltpu.VMEM((sz.subpad, LANES), F32),
             pltpu.VMEM((rows * 8, LANES), F32),
             pltpu.VMEM((rows, LANES), F32),
             pltpu.SMEM((count, sz.members), jnp.int32),
-            dma(3),
+            dma(4),
         ],
         sz.members * 30 * sz.subpad * LANES,
         2_000_000,
         (matchings, place, preds, truth),
         smem=(0, 1),
+        vmem=(2, 3),
+        limit=16,
     )
     back = lax.all_to_all(grads, MEMBER, 0, 0, tiled=True)
 
     half = (hid // 2, sz.cols)
     edge_shape = (mem, ch, lon)
-    grad_pred, grad_pre, hid_v, edge_up, edge_dn, sibling = call(
+    grad_pred, grad_pre, hid_own, edge_up, edge_dn, sibling = call(
         functools.partial(sibling_kernel, sz),
         "sibling",
         [
@@ -640,20 +677,18 @@
             (half, BF16),
         ],
         [
-            pltpu.VMEM(part_shape, BF16),
-            wide_f,
-            pltpu.VMEM(w_proj.shape, BF16),
+            pltpu.VMEM((mem, hid, pos), F32),
+            pltpu.VMEM((mem, hid // 2, pos), BF16),
             pltpu.VMEM((3, TAPS, hid), BF16),
             regroup_rows,
             pltpu.VMEM((hid, ch), BF16),
-            pltpu.VMEM((mem, hid // 2, pos), BF16),
-            dma(3 + 4 * mem + mem * sz.devs),
+            dma(1 + 4 * mem + mem * sz.devs),
         ],
         conv_flops,
         9_000_000,
         (place, back, slope, hidden, ext, w_proj, wt3),
         smem=(0,),
-        vmem=(4,),
+        vmem=(1, 4, 5),
         vmem_outs=range(6),
         limit=40,
     )
@@ -665,7 +700,7 @@
         [],
         conv_flops // 2,
         9_000_000,
-        (place, grad_pre, hid_v, ext, grad_pred),
+        (place, grad_pre, hid_own, ext, grad_pred),
         smem=(0,),
         vmem=range(1, 5),
         vmem_outs=(0,),

time: 112 us -> 108 us (0.964)
  blocking collectives: 23.8 us -> 0 us
  waiting for transfers between devices: 10.1 us -> 29.9 us
  starting transfers between devices: 19.8 us -> 23.1 us
  local copies, waits for them, and re-layouts: 12.8 us -> 10.6 us
    all_to_all x1 -> x0, blocking collectives: 23.8 us -> none  [on_device(): preds = lax.all_to_all(snd, MEMBER, 0, 0, tiled=True)]
    all_to_all x0 -> x1, waiting for transfers between devices: none -> 18.1 us  [on_device(): preds = lax.all_to_all(snd, MEMBER, 0, 0, tiled=True)]
    all_to_all x0 -> x1, starting transfers between devices: none -> 4.89 us  [on_device(): preds = lax.all_to_all(snd, MEMBER, 0, 0, tiled=True)]
    reshape x1 -> x0, local copies, waits for them, and re-layouts: 1.23 us -> none  [on_device(): w_conv.T.reshape(3, 3 * ch, hid)]
    pallas_call x10 -> x11, Pallas kernels: 40.1 us -> 39 us  [call(): pl.pallas_call(kernel, in_specs=[specs[kind(i)] for i in range(len(args))...]
    unnamed x22 -> x28, local copies, waits for them, and re-layouts: 10.6 us -> 10.6 us
  transfers between devices with their start and end apart: 6 -> 7, of which waited for: 3 -> 4; matrix products, arithmetic and copies ran while one was open for 2% -> 0% of each run, Pallas kernels for 13% -> 15%
where the time goes in v5:
time: 108 us; the launch traced here: 107 us
  Pallas kernels  42 us (39%)
  waiting for transfers between devices  29.9 us (28%)
  starting transfers between devices  23.1 us (21%)
  local copies, waits for them, and re-layouts  10.6 us (10%)
    pallas_call x11, Pallas kernels, call(): pl.pallas_call(kernel, in_specs=[specs[kind(i)] for i in range(len(args))...  39 us
    all_to_all x1, waiting for transfers between devices, on_device(): preds = lax.all_to_all(snd, MEMBER, 0, 0, tiled=True)  18.1 us
    unnamed x28, local copies, waits for them, and re-layouts  10.6 us
    all_to_all x1, waiting for transfers between devices, on_device(): back = lax.all_to_all(grads, MEMBER, 0, 0, tiled=True)  10 us
    all_to_all x1, starting transfers between devices, on_device(): halos = lax.all_to_all(send, 'band', 0, 0, tiled=True)  5.2 us
    all_to_all x1, starting transfers between devices, on_device(): preds = lax.all_to_all(snd, MEMBER, 0, 0, tiled=True)  4.89 us
    all_to_all x1, starting transfers between devices, on_device(): lax.all_to_all(partial.reshape(shards // 2, each, sz.cols), ('pair', 'ban...  4.04 us
    ppermute x1, starting transfers between devices, on_device(): from_up = lax.ppermute(edge_dn, 'band', down)  3.82 us
  transfers between devices with their start and end apart: 7, of which 4 were waited for; matrix products, arithmetic and copies ran while one was open for 0% of the time, Pallas kernels for 15%

profile of v5, /device:TPU:0, one launch (start us, length us, event | category | flops | bytes accessed | tf_op | source)
XLA Modules:
  0.0 107.1 jit_solution(16767736322766139297)
XLA Ops:
  0.6 0.7 pad_add_fusion.place
  1.3 3.0 %edges.1 = bf16[4,168,128]{2,1,0:T(8,128)(2,1)} custom-call(s32[3]{0:T(128)} %pad_add_fusion.place, bf16[2,84,16,128]{3,2,1,0:T(8,128)(2,1)} %states.3, f32[2,84,16,128]{3,2,1,0:T(8,128)} %noise.3), custom_call_target="tpu_custom_call" | custom-call | flops 1000000 | bytes 3000000 | tf_op jit(solution)/shard_map/edges/pallas_call | solution.py:29
  4.3 5.2 %all-to-all-start = ((bf16[4,168,128]{2,1,0:T(8,128)(2,1)}), bf16[4,168,128]{2,1,0:T(8,128)(2,1)S(1)}, u32[]{:S(2)}, u32[]{:S(2)}) async-start(bf16[4,168,128]{2,1,0:T(8,128)(2,1)} %edges.1), calls=%async_computation | async-start | bytes 344064 | tf_op jit(solution)/shard_map/all_to_all | solution.py:564
  9.5 4.1 %prep.1 = (bf16[2,84,2048]{2,1,0:T(8,128)(2,1)}, bf16[2,256,2304]{2,1,0:T(8,128)(2,1)}, bf16[512,768]{1,0:T(8,128)(2,1)}, bf16[3,256,512]{2,1,0:T(8,128)(2,1)}) custom-call(bf16[2,84,16,128]{3,2,1,0:T(8,128)(2,1)} %states.3, f32[2,84,16,128]{3,2,1,0:T(8,128)} %noise.3, bf16[756,512]{1,0:T(8,128)(2,1)} %bitcast.6), custom_call_target="tpu_custom_call" | custom-call | flops 10000000 | bytes 8000000 | tf_op jit(solution)/shard_map/prep/pallas_call | solution.py:29
  13.7 1.0 all-to-all-done.halos
  14.7 0.0 copy-start.13
  14.7 0.7 copy-done.13
  15.3 0.0 copy-start.9
  15.3 0.0 copy-start.11
  15.3 0.0 copy-start.12
  15.3 10.0 %forward.1 = (bf16[2,512,2048]{2,1,0:T(8,128)(2,1)}, bf16[2,512,2048]{2,1,0:T(8,128)(2,1)}, bf16[2,256,2304]{2,1,0:T(8,128)(2,1)}, bf16[8,2,168,128]{3,2,1,0:T(8,128)(2,1)}) custom-call(s32[3]{0:T(128)} %pad_add_fusion.place, bf16[2,256,2304]{2,1,0:T(8,128)(2,1)} %get-tuple-element.24.e_in, ...), custom_call_target="tpu_custom_call", output_to_operand_aliasing={{2}: (1, {})} | custom-call | flops 3221225472 | bytes 9000000 | tf_op jit(solution)/shard_map/forward/pallas_call | solution.py:29
  25.4 4.9 %all-to-all-start.1 = ((bf16[8,2,168,128]{3,2,1,0:T(8,128)(2,1)}), bf16[8,2,168,128]{3,2,1,0:T(8,128)(2,1)S(1)}, u32[]{:S(2)}, u32[]{:S(2)}) async-start(bf16[8,2,168,128]{3,2,1,0:T(8,128)(2,1)} %get-tuple-element.27), calls=%async_computation.1 | async-start | bytes 1376256 | tf_op jit(solution)/shard_map/all_to_all | solution.py:615
  30.2 0.0 copy-done.9
  30.2 0.7 truth.1
  31.0 18.1 %all-to-all-done.1.preds = bf16[8,2,168,128]{3,2,1,0:T(8,128)(2,1)S(1)} async-done(((bf16[8,2,168,128]{3,2,1,0:T(8,128)(2,1)}), bf16[8,2,168,128]{3,2,1,0:T(8,128)(2,1)S(1)}, u32[]{:S(2)}, u32[]{:S(2)}) %all-to-all-start.1) | async-done | bytes 688160 | tf_op jit(solution)/shard_map/all_to_all | solution.py:615
  49.1 0.0 copy-done.11
  49.1 0.0 copy-done.12
  49.1 4.0 %pairs.1 = bf16[8,2,168,128]{3,2,1,0:T(8,128)(2,1)} custom-call(s32[4,16]{1,0:T(4,128)S(1)} %copy-done.12, s32[3]{0:T(128)S(1)} %copy-done.11, bf16[8,2,168,128]{3,2,1,0:T(8,128)(2,1)S(1)} %all-to-all-done.1.preds, bf16[8,168,128]{2,1,0:T(8,128)(2,1)S(1)} %truth.1), custom_call_target="tpu_custom_call" | custom-call | flops 10321920 | bytes 2000000 | tf_op jit(solution)/shard_map/pairs/pallas_call | solution.py:29
  53.1 3.7 %all-to-all-start.2 = ((bf16[8,2,168,128]{3,2,1,0:T(8,128)(2,1)}), bf16[8,2,168,128]{3,2,1,0:T(8,128)(2,1)S(1)}, u32[]{:S(2)}, u32[]{:S(2)}) async-start(bf16[8,2,168,128]{3,2,1,0:T(8,128)(2,1)} %pairs.1), calls=%async_computation.2 | async-start | bytes 1376256 | tf_op jit(solution)/shard_map/all_to_all | solution.py:664
  56.8 0.0 copy-start.4
  56.8 2.2 %copy-done.4 = bf16[2,512,2048]{2,1,0:T(8,128)(2,1)S(1)} copy-done((bf16[2,512,2048]{2,1,0:T(8,128)(2,1)S(1)}, bf16[2,512,2048]{2,1,0:T(8,128)(2,1)}, u32[]{:S(2)}) %copy-start.4) | copy-done | bytes 4194328
  59.0 0.0 copy-start.1
  59.0 0.0 copy-start.10
  59.0 3.1 %slope.1.slope_in = f32[2,512,2048]{2,1,0:T(8,128)S(1)} custom-call(bf16[2,512,2048]{2,1,0:T(8,128)(2,1)S(1)} %copy-done.4), custom_call_target="tpu_custom_call" | custom-call | flops 20971520 | bytes 16777216 | tf_op jit(solution)/shard_map/slope/pallas_call | solution.py:630
  62.1 0.0 copy-start
  62.1 3.3 %copy-done = f32[2,512,2048]{2,1,0:T(8,128)} copy-done((f32[2,512,2048]{2,1,0:T(8,128)}, f32[2,512,2048]{2,1,0:T(8,128)S(1)}, u32[]{:S(2)}) %copy-start) | copy-done | bytes 8388632
  65.4 10.0 %all-to-all-done.2.back = bf16[8,2,168,128]{3,2,1,0:T(8,128)(2,1)S(1)} async-done(((bf16[8,2,168,128]{3,2,1,0:T(8,128)(2,1)}), bf16[8,2,168,128]{3,2,1,0:T(8,128)(2,1)S(1)}, u32[]{:S(2)}, u32[]{:S(2)}) %all-to-all-start.2) | async-done | bytes 688160 | tf_op jit(solution)/shard_map/all_to_all | solution.py:664
  75.4 0.0 copy-done.1
  75.4 0.0 copy-done.10
  75.4 0.0 copy-start.5
  75.4 1.1 %copy-done.5 = bf16[3,256,512]{2,1,0:T(8,128)(2,1)S(1)} copy-done((bf16[3,256,512]{2,1,0:T(8,128)(2,1)S(1)}, bf16[3,256,512]{2,1,0:T(8,128)(2,1)}, u32[]{:S(2)}) %copy-start.5) | copy-done | bytes 786456
  76.5 7.5 %sibling.1 = (bf16[2,84,2048]{2,1,0:T(8,128)(2,1)S(1)}, bf16[2,512,2048]{2,1,0:T(8,128)(2,1)S(1)}, bf16[2,256,2048]{2,1,0:T(8,128)(2,1)S(1)}, f32[2,84,128]{2,1,...) custom-call(s32[3]{0:T(128)S(1)} %copy-done.11, ...), custom_call_target="tpu_custom_call" | custom-call | flops 3221225472 | bytes 9000000 | tf_op jit(solution)/shard_map/sibling/pallas_call | solution.py:29
  84.0 0.0 copy-start.2
  84.0 0.0 copy-start.7
  84.0 0.1 collective-permute-start
  84.1 0.0 copy-start.6
  84.1 2.9 %own.1 = f32[256,896]{1,0:T(8,128)S(1)} custom-call(s32[3]{0:T(128)S(1)} %copy-done.11, bf16[2,512,2048]{2,1,0:T(8,128)(2,1)S(1)} %get-tuple-element.33.gpre, bf16[2,256,2048]{2,1,0:T(8,128)(2,1)S(1)} %get-tuple-element.39.hid, bf16[2,256,2304]{2,1,0:T(8,128)(2,1)S(1)} %copy-done.1, bf16[2,84,2048]{2,1,0:T(8,128)(2,1)S(1)} %get-tuple-element.34.gp), custom_call_target="tpu_custom_call" | custom-call | flops 1610612736 | bytes 9000000 | tf_op jit(solution)/shard_map/own/pallas_call | solution.py:29
  87.0 0.0 copy-done.2
  87.0 0.0 copy-done.7
  87.0 0.0 collective-permute-done.other
  87.1 0.9 merge.1
  87.9 4.0 %all-to-all-start.3 = ((bf16[16,16,896]{2,1,0:T(8,128)(2,1)}), bf16[16,16,896]{2,1,0:T(8,128)(2,1)S(1)}, u32[]{:S(2)}, u32[]{:S(2)}) async-start(bf16[16,16,896]{2,1,0:T(8,128)(2,1)} %bitcast.4), calls=%async_computation.3 | async-start | bytes 917504 | tf_op jit(solution)/shard_map/all_to_all | solution.py:723
  92.0 3.8 %collective-permute-start.1 = (f32[2,84,128]{2,1,0:T(8,128)S(1)}, f32[2,84,128]{2,1,0:T(8,128)S(1)}, u32[]{:S(2)}, u32[]{:S(2)}) collective-permute-start(f32[2,84,128]{2,1,0:T(8,128)S(1)} %get-tuple-element.41), channel_id=1, source_target_pairs={{0,1},{1,2},{2,3},{4,5},{5,6},{6,7},{8,9},{9,10},{10,11},{12,13},{... | collective-permute-start | bytes 258056 | tf_op jit(solution)/shard_map/ppermute | solution.py:728
  95.8 1.3 %collective-permute-start.2 = (f32[2,84,128]{2,1,0:T(8,128)S(1)}, f32[2,84,128]{2,1,0:T(8,128)S(1)}, u32[]{:S(2)}, u32[]{:S(2)}) collective-permute-start(f32[2,84,128]{2,1,0:T(8,128)S(1)} %get-tuple-element.42), channel_id=1, source_target_pairs={{1,0},{2,1},{3,2},{5,4},{6,5},{7,6},{9,8},{10,9},{11,10},{13,12},{... | collective-permute-start | bytes 258056 | tf_op jit(solution)/shard_map/ppermute | solution.py:727
  97.1 0.0 copy-done.6
  97.1 0.0 copy-start.3
  97.1 2.2 %copy-done.3 = bf16[2,512,2048]{2,1,0:T(8,128)(2,1)S(1)} copy-done((bf16[2,512,2048]{2,1,0:T(8,128)(2,1)S(1)}, bf16[2,512,2048]{2,1,0:T(8,128)(2,1)}, u32[]{:S(2)}) %copy-start.3) | copy-done | bytes 4194328
  99.3 0.0 copy-start.8
  99.3 1.1 %copy-done.8 = bf16[2,84,2048]{2,1,0:T(8,128)(2,1)S(1)} copy-done((bf16[2,84,2048]{2,1,0:T(8,128)(2,1)S(1)}, bf16[2,84,2048]{2,1,0:T(8,128)(2,1)}, u32[]{:S(2)}) %copy-start.8) | copy-done | bytes 688152
  100.4 4.1 %data.1 = (bf16[2,84,16,128]{3,2,1,0:T(8,128)(2,1)S(1)}, f32[2,2,84,128]{3,2,1,0:T(8,128)S(1)}) custom-call(bf16[2,512,2048]{2,1,0:T(8,128)(2,1)S(1)} %copy-done.3, bf16[2,84,2048]{2,1,0:T(8,128)(2,1)S(1)} %copy-done.8, bf16[3,256,512]{2,1,0:T(8,128)(2,1)S(1)} %copy-done.6), custom_call_target="tpu_custom_call" | custom-call | flops 3221225472 | bytes 8000000 | tf_op jit(solution)/shard_map/data/pallas_call | solution.py:29
  104.6 0.0 collective-permute-done.1.uv
  104.6 0.0 collective-permute-done.2.dv
  104.6 1.0 border.1
  105.6 0.7 all-to-all-done.3.terms
  106.3 0.7 final.1
Async XLA Ops:
  4.3 10.3 %all-to-all-start = ((bf16[4,168,128]{2,1,0:T(8,128)(2,1)}), bf16[4,168,128]{2,1,0:T(8,128)(2,1)S(1)}, u32[]{:S(2)}, u32[]{:S(2)}) async-start(bf16[4,168,128]{2,1,0:T(8,128)(2,1)} %edges.1), calls=%async_computation | async-start | bytes 344064 | tf_op jit(solution)/shard_map/all_to_all | solution.py:564
  14.7 0.7 copy-start.13
  15.3 14.9 %copy-start.9 = (bf16[84,16,128]{2,1,0:T(8,128)(2,1)S(1)}, bf16[84,16,128]{2,1,0:T(8,128)(2,1)}, u32[]{:S(2)}) copy-start(bf16[84,16,128]{2,1,0:T(8,128)(2,1)} %target) | copy-start | bytes 1032196
  15.3 33.7 %copy-start.11 = (s32[3]{0:T(128)S(1)}, s32[3]{0:T(128)}, u32[]{:S(2)}) copy-start(s32[3]{0:T(128)} %pad_add_fusion.place) | copy-start | bytes 40
  15.3 33.7 %copy-start.12 = (s32[4,16]{1,0:T(4,128)S(1)}, s32[4,16]{1,0:T(4,128)}, u32[]{:S(2)}) copy-start(s32[4,16]{1,0:T(4,128)} %match.1) | copy-start | bytes 772
  25.4 23.7 %all-to-all-start.1 = ((bf16[8,2,168,128]{3,2,1,0:T(8,128)(2,1)}), bf16[8,2,168,128]{3,2,1,0:T(8,128)(2,1)S(1)}, u32[]{:S(2)}, u32[]{:S(2)}) async-start(bf16[8,2,168,128]{3,2,1,0:T(8,128)(2,1)} %get-tuple-element.27), calls=%async_computation.1 | async-start | bytes 1376256 | tf_op jit(solution)/shard_map/all_to_all | solution.py:615
  53.1 22.3 %all-to-all-start.2 = ((bf16[8,2,168,128]{3,2,1,0:T(8,128)(2,1)}), bf16[8,2,168,128]{3,2,1,0:T(8,128)(2,1)S(1)}, u32[]{:S(2)}, u32[]{:S(2)}) async-start(bf16[8,2,168,128]{3,2,1,0:T(8,128)(2,1)} %pairs.1), calls=%async_computation.2 | async-start | bytes 1376256 | tf_op jit(solution)/shard_map/all_to_all | solution.py:664
  56.8 2.2 %copy-start.4 = (bf16[2,512,2048]{2,1,0:T(8,128)(2,1)S(1)}, bf16[2,512,2048]{2,1,0:T(8,128)(2,1)}, u32[]{:S(2)}) copy-start(bf16[2,512,2048]{2,1,0:T(8,128)(2,1)} %get-tuple-element.29.preact) | copy-start | bytes 12582916
  59.0 16.4 %copy-start.1 = (bf16[2,256,2304]{2,1,0:T(8,128)(2,1)S(1)}, bf16[2,256,2304]{2,1,0:T(8,128)(2,1)}, u32[]{:S(2)}) copy-start(bf16[2,256,2304]{2,1,0:T(8,128)(2,1)} %get-tuple-element.31.ext) | copy-start | bytes 7077892
  59.0 16.4 %copy-start.10 = (bf16[84,512]{1,0:T(8,128)(2,1)S(1)}, bf16[84,512]{1,0:T(8,128)(2,1)}, u32[]{:S(2)}) copy-start(bf16[84,512]{1,0:T(8,128)(2,1)} %w_proj.3) | copy-start | bytes 258052
  62.1 3.3 %copy-start = (f32[2,512,2048]{2,1,0:T(8,128)}, f32[2,512,2048]{2,1,0:T(8,128)S(1)}, u32[]{:S(2)}) copy-start(f32[2,512,2048]{2,1,0:T(8,128)S(1)} %slope.1.slope_in) | copy-start | bytes 25165828
  75.4 1.1 %copy-start.5 = (bf16[3,256,512]{2,1,0:T(8,128)(2,1)S(1)}, bf16[3,256,512]{2,1,0:T(8,128)(2,1)}, u32[]{:S(2)}) copy-start(bf16[3,256,512]{2,1,0:T(8,128)(2,1)} %get-tuple-element.32.wt3_in.wt3) | copy-start | bytes 2359300
  84.0 3.0 %copy-start.2 = (bf16[2,512,2048]{2,1,0:T(8,128)(2,1)}, bf16[2,512,2048]{2,1,0:T(8,128)(2,1)S(1)}, u32[]{:S(2)}) copy-start(bf16[2,512,2048]{2,1,0:T(8,128)(2,1)S(1)} %get-tuple-element.33.gpre) | copy-start | bytes 12582916
  84.0 3.0 %copy-start.7 = (bf16[2,84,2048]{2,1,0:T(8,128)(2,1)}, bf16[2,84,2048]{2,1,0:T(8,128)(2,1)S(1)}, u32[]{:S(2)}) copy-start(bf16[2,84,2048]{2,1,0:T(8,128)(2,1)S(1)} %get-tuple-element.34.gp) | copy-start | bytes 2064388
  84.0 3.0 %collective-permute-start = (bf16[256,896]{1,0:T(8,128)(2,1)S(1)}, bf16[256,896]{1,0:T(8,128)(2,1)S(1)}, u32[]{:S(2)}, u32[]{:S(2)}) collective-permute-start(bf16[256,896]{1,0:T(8,128)(2,1)S(1)} %get-tuple-element.40), channel_id=1, source_target_pairs={{0,4},{4,0},{1,5},{5,1},{2,6},{6,2},{3,7},{7,3},{8,12},{12,8},{9,1... | collective-permute-start | bytes 1376264 | tf_op jit(solution)/shard_map/ppermute | solution.py:695
  84.1 13.0 %copy-start.6 = (bf16[3,256,512]{2,1,0:T(8,128)(2,1)S(1)}, bf16[3,256,512]{2,1,0:T(8,128)(2,1)}, u32[]{:S(2)}) copy-start(bf16[3,256,512]{2,1,0:T(8,128)(2,1)} %get-tuple-element.32.wt3_in.wt3) | copy-start | bytes 2359300
  87.9 18.4 %all-to-all-start.3 = ((bf16[16,16,896]{2,1,0:T(8,128)(2,1)}), bf16[16,16,896]{2,1,0:T(8,128)(2,1)S(1)}, u32[]{:S(2)}, u32[]{:S(2)}) async-start(bf16[16,16,896]{2,1,0:T(8,128)(2,1)} %bitcast.4), calls=%async_computation.3 | async-start | bytes 917504 | tf_op jit(solution)/shard_map/all_to_all | solution.py:723
  92.0 12.6 %collective-permute-start.1 = (f32[2,84,128]{2,1,0:T(8,128)S(1)}, f32[2,84,128]{2,1,0:T(8,128)S(1)}, u32[]{:S(2)}, u32[]{:S(2)}) collective-permute-start(f32[2,84,128]{2,1,0:T(8,128)S(1)} %get-tuple-element.41), channel_id=1, source_target_pairs={{0,1},{1,2},{2,3},{4,5},{5,6},{6,7},{8,9},{9,10},{10,11},{12,13},{... | collective-permute-start | bytes 258056 | tf_op jit(solution)/shard_map/ppermute | solution.py:728
  95.8 8.8 %collective-permute-start.2 = (f32[2,84,128]{2,1,0:T(8,128)S(1)}, f32[2,84,128]{2,1,0:T(8,128)S(1)}, u32[]{:S(2)}, u32[]{:S(2)}) collective-permute-start(f32[2,84,128]{2,1,0:T(8,128)S(1)} %get-tuple-element.42), channel_id=1, source_target_pairs={{1,0},{2,1},{3,2},{5,4},{6,5},{7,6},{9,8},{10,9},{11,10},{13,12},{... | collective-permute-start | bytes 258056 | tf_op jit(solution)/shard_map/ppermute | solution.py:727
  97.1 2.2 %copy-start.3 = (bf16[2,512,2048]{2,1,0:T(8,128)(2,1)S(1)}, bf16[2,512,2048]{2,1,0:T(8,128)(2,1)}, u32[]{:S(2)}) copy-start(bf16[2,512,2048]{2,1,0:T(8,128)(2,1)} %copy-done.2) | copy-start | bytes 12582916
  99.3 1.1 %copy-start.8 = (bf16[2,84,2048]{2,1,0:T(8,128)(2,1)S(1)}, bf16[2,84,2048]{2,1,0:T(8,128)(2,1)}, u32[]{:S(2)}) copy-start(bf16[2,84,2048]{2,1,0:T(8,128)(2,1)} %copy-done.7) | copy-start | bytes 2064388

commit v6 on v5

--- a/solution.py
+++ b/solution.py
@@ -117,7 +117,7 @@
         self.cols = (self.used + LANES - 1) // LANES * LANES
 
 
-def edges_kernel(sz, place, states, noise, send, st, ns, xs, sv, rows, sems):
+def edges_kernel(sz, states, noise, send, st, ns, xs, sv, rows, sems):
     copies = Copies(sems)
     loads = []
     for m in range(sz.mem):
@@ -133,47 +133,95 @@
             noise_rows = ns.at[m]
             rows[side, at, :] = row + noise_rows[:, 0 if side == 0 else sz.lat - 1, :]
     for other in range(sz.bands):
-        after = jnp.where(other > place[1], 1.0, 0.0)
+        after = jnp.where(other > lax.axis_index("band"), 1.0, 0.0)
         sv[other] = (rows[1] * after + rows[0] * (1.0 - after)).astype(BF16)
     copies.start(sv, send)
     copies.finish()
 
 
-def prep_kernel(
-    sz, states, noise, w_t, x_out, e_out, w_out, wt3_out,
-    st, ns, wv, xv, ev, wov, wt3v, xs, es, sems,
+def conv_pair(sz, ext, w3, m, pair):
+    width = sz.lon
+    cols = jnp.concatenate(
+        [ext[m, :, (pair * 2 + ro) * width : (pair * 2 + ro + 2) * width] for ro in range(3)],
+        axis=0,
+    )
+    return jnp.dot(w3[...], cols, preferred_element_type=F32)
+
+
+def hidden_pair(preact):
+    return (preact * (1.0 + lax.erf(preact * SQRT_HALF))).astype(BF16)
+
+
+def project_pair(x, w_proj, hidden):
+    pred = x.astype(F32) + 0.5 * jnp.dot(w_proj[...], hidden, preferred_element_type=F32)
+    return pred.astype(BF16).astype(F32)
+
+
+def front_kernel(
+    sz, states, noise, w_t, w_proj, pre_out, hid_out, ext_out, preds_out, w3_out, wt3_out,
+    st, ns, wv, xv, pre, preb, hid, ext, preds, w3, wt3v, xs, es, sems,
 ):
     copies = Copies(sems)
-    w_load = copies.start(w_t, wv)
+    width = sz.lon
     loads = []
     for m in range(sz.mem):
         loads.append(
             [copies.start(states.at[m], st.at[m]), copies.start(noise.at[m], ns.at[m])]
         )
+        if m == 0:
+            w_load = copies.start(w_t, wv)
     es[...] = jnp.zeros_like(es)
-    inner = slice(sz.lon, sz.lon + sz.pos)
     taps = 3 * sz.ch
-    copies.finish([w_load])
-    for ro in range(3):
-        piece = jnp.concatenate(
-            [wv[ro * taps : (ro + 1) * taps, :], jnp.zeros((TAPS - taps, sz.hid), BF16)], axis=0
-        )
-        wt3v[ro] = piece
-        wov[:, ro * TAPS : (ro + 1) * TAPS] = piece.T
-    copies.start(wov, w_out)
-    copies.start(wt3v, wt3_out)
-    for m in range(sz.mem):
+    last = sz.lat // 2 - 1
+
+    def expand(m):
         copies.finish(loads[m])
         xs[...] = (st[m].astype(F32) + ns[m]).astype(BF16).astype(F32).reshape(
             sz.ch * sz.lat, sz.lon
         )
         for row in range(sz.lat):
-            here = slice(row * sz.lon, (row + 1) * sz.lon)
             vals = xs[pl.ds(row, sz.ch, stride=sz.lat), :]
-            xv[m, :, here] = vals.astype(BF16)
-            ev[m, :, here] = expand_row(vals, es)
-        copies.start(ev.at[m], e_out.at[m, :, inner])
-        copies.start(xv.at[m], x_out.at[m])
+            xv[:, row * width : (row + 1) * width] = vals
+            ext[m, :, (row + 1) * width : (row + 2) * width] = expand_row(vals, es)
+
+    def rest(m, pair):
+        here = slice(pair * 2 * width, (pair + 1) * 2 * width)
+        preact = pre[pair % 2]
+        preb[m, :, here] = preact.astype(BF16)
+        hidden = hidden_pair(preact)
+        hid[m, :, here] = hidden
+        preds[m, :, here] = project_pair(xv[:, here], w_proj, hidden)
+
+    for m in range(sz.mem):
+        expand(m)
+        if m == 0:
+            copies.finish([w_load])
+            for ro in range(3):
+                piece = jnp.concatenate(
+                    [
+                        wv[ro * taps : (ro + 1) * taps, :],
+                        jnp.zeros((TAPS - taps, sz.hid), BF16),
+                    ],
+                    axis=0,
+                )
+                wt3v[ro] = piece
+                w3[:, ro * TAPS : (ro + 1) * TAPS] = piece.T
+            copies.start(w3, w3_out)
+            copies.start(wt3v, wt3_out)
+        inner = slice(width, width + sz.pos)
+        copies.start(ext.at[m, :, inner], ext_out.at[m, :, inner])
+        pre[1] = conv_pair(sz, ext, w3, m, 1)
+        for pair in range(1, last):
+            if pair + 1 < last:
+                pre[(pair + 1) % 2] = conv_pair(sz, ext, w3, m, pair + 1)
+            rest(m, pair)
+            if pair % 2 == 0 or pair + 1 == last:
+                first = pair if pair % 2 else pair - 1
+                here = slice(first * 2 * width, (pair + 1) * 2 * width)
+                copies.start(preb.at[m, :, here], pre_out.at[m, :, here])
+                copies.start(hid.at[m, :, here], hid_out.at[m, :, here])
+        here = slice(2 * width, sz.pos - 2 * width)
+        copies.start(preds.at[m, :, here], preds_out.at[m, :, here])
     copies.finish()
 
 
@@ -191,81 +239,82 @@
             t_out[prow * sz.parts + q] = ps[q].astype(BF16)
 
 
-def halo_rows(sz, halos, band, side):
+def halo_rows(sz, halos, side):
+    band = lax.axis_index("band")
     other = band - 1 if side == 0 else band + 1
     inside = jnp.logical_and(other >= 0, other < sz.bands)
     vals = halos[jnp.clip(other, 0, sz.bands - 1)].astype(F32)
     return vals * jnp.where(inside, 1.0, 0.0)
 
 
-def forward_kernel(
-    sz, place, e_in, x_in, halos, w3, w_proj, pre_out, hid_out, ext_out, snd_out,
-    ext, xv, hv, wv, wpv, pre, preb, hid, snd, es, ps, preds, hr, hx, sems,
+def rim_kernel(
+    sz, halos_in, pre_in, hid_in, ext_in, preds_in, w3_in, w_proj_in,
+    pre_out, hid_out, ext_out, snd_out,
+    pre, preb, hid, snd, halos, ends, preds, w3, w_proj, xf, rim, es, ps, hr, sems,
 ):
     width = sz.lon
-    pairs = sz.lat // 2
     copies = Copies(sems)
-    inner = slice(width, width + sz.pos)
-    load_h = copies.start(halos, hv)
-    load_e = [copies.start(e_in.at[0, :, inner], ext.at[0, :, inner])]
-    load_w = copies.start(w3, wv)
-    for m in range(1, sz.mem):
-        load_e.append(copies.start(e_in.at[m, :, inner], ext.at[m, :, inner]))
-    load_p = copies.start(w_proj, wpv)
-    load_x = [copies.start(x_in.at[m], xv.at[m]) for m in range(sz.mem)]
+    load_h = copies.start(halos_in, halos)
+    load_w = copies.start(w3_in, w3)
+    load_e = []
+    for side in range(2):
+        at = width if side == 0 else sz.pos - 2 * width
+        to = width if side == 0 else 0
+        load_e.append(
+            copies.start(
+                ext_in.at[:, :, at : at + 3 * width], ends.at[side, :, :, to : to + 3 * width]
+            )
+        )
+    load_p = copies.start(w_proj_in, w_proj)
+    here = slice(2 * width, sz.pos - 2 * width)
+    load_f = [copies.start(preds_in.at[m, :, here], preds.at[m, :, here]) for m in range(sz.mem)]
     es[...] = jnp.zeros_like(es)
     if sz.subpad > sz.sub:
         ps[...] = jnp.zeros_like(ps)
     copies.finish([load_h])
     for side in range(2):
-        at = 0 if side == 0 else width + sz.pos
-        hr[...] = halo_rows(sz, hv, place[1], side)
+        at = 0 if side == 0 else 3 * width
+        hr[...] = halo_rows(sz, halos, side)
         for m in range(sz.mem):
-            row = expand_row(hr[pl.ds(m * sz.ch, sz.ch), :], es)
-            ext[m, :, at : at + width] = row
-            hx[side, m] = row
-    for side in range(2):
-        at = 0 if side == 0 else width + sz.pos
-        copies.start(hx.at[side], ext_out.at[:, :, at : at + width])
-    copies.finish([load_w])
-
-    def conv(m, pair):
-        cols = jnp.concatenate(
-            [ext[m, :, (pair * 2 + ro) * width : (pair * 2 + ro + 2) * width] for ro in range(3)],
-            axis=0,
-        )
-        pre[pair % 2] = jnp.dot(wv[...], cols, preferred_element_type=F32)
-
-    def rest(m, pair):
-        here = slice(pair * 2 * width, (pair + 1) * 2 * width)
-        preact = pre[pair % 2]
-        preb[m, :, here] = preact.astype(BF16)
-        hidden = (preact * (1.0 + lax.erf(preact * SQRT_HALF))).astype(BF16)
-        hid[m, :, here] = hidden
-        pred = xv[m, :, here].astype(F32) + 0.5 * jnp.dot(
-            wpv[...], hidden, preferred_element_type=F32
-        )
-        preds[:, here] = pred.astype(BF16).astype(F32)
-
-    for m in range(sz.mem):
-        copies.finish([load_e[m]])
-        conv(m, 0)
-        copies.finish([load_p, load_x[m]])
-        for pair in range(pairs):
-            if pair + 1 < pairs:
-                conv(m, pair + 1)
-            rest(m, pair)
-            if pair % 2 == 1:
-                here = slice((pair - 1) * 2 * width, (pair + 1) * 2 * width)
-                copies.start(preb.at[m, :, here], pre_out.at[m, :, here])
-                copies.start(hid.at[m, :, here], hid_out.at[m, :, here])
+            ends[side, m, :, at : at + width] = expand_row(hr[pl.ds(m * sz.ch, sz.ch), :], es)
+        to = 0 if side == 0 else width + sz.pos
+        copies.start(ends.at[side, :, :, at : at + width], ext_out.at[:, :, to : to + width])
+    copies.finish([load_w] + load_e)
+    last = sz.lat // 2 - 1
+    units = [(m, side) for m in range(sz.mem) for side in range(2)]
+
+    def conv(i):
+        m, side = units[i]
+        pre[i % 2] = conv_pair(sz, ends.at[side], w3, m, 0)
+
+    conv(0)
+    copies.finish([load_p])
+    for i, (m, side) in enumerate(units):
+        if i + 1 < len(units):
+            conv(i + 1)
+        here = slice(side * last * 2 * width, (side * last + 1) * 2 * width)
+        preact = pre[i % 2]
+        preb[i] = preact.astype(BF16)
+        hidden = hidden_pair(preact)
+        hid[i] = hidden
+        copies.start(preb.at[i], pre_out.at[m, :, here])
+        copies.start(hid.at[i], hid_out.at[m, :, here])
+        xf[...] = ends[side, m, :, width : 3 * width].astype(F32)
+        rim[side] = project_pair(xf[pl.ds(sz.ch, sz.ch), :], w_proj, hidden)
+        if side == 0:
+            continue
+        copies.finish([load_f[m]])
+
+        def row_of(row):
+            if row < 2 or row >= sz.lat - 2:
+                at = row % 2 * width
+                return rim[0 if row < 2 else 1, :, at : at + width]
+            return preds[m, :, row * width : (row + 1) * width]
+
         for prow in range(sz.prows):
             for group in range(sz.groups):
                 first = prow * 8 + group * sz.parts
-                rows = [
-                    preds[:, (first + i) * width : (first + i + 1) * width]
-                    for i in range(sz.parts)
-                ]
+                rows = [row_of(first + k) for k in range(sz.parts)]
                 for q, out in enumerate(swap_blocks(rows)):
                     ps[q, pl.ds(group * sz.ch, sz.ch), :] = out
             for q in range(sz.parts):
@@ -282,19 +331,19 @@
         x = preact[0, at, :].astype(F32)
         twice = 1.0 + lax.erf(x * SQRT_HALF)
         bell = jnp.exp2(x * x * (-0.5 * LOG2_E)) * (2.0 * INV_ROOT_TWO_PI)
-        slope[0, at, :] = twice + x * bell
+        slope[0, at, :] = (twice + x * bell).astype(BF16)
         return carry
 
     lax.fori_loop(0, preact.shape[1] // rows, one, 0)
 
 
-def pair_kernel(sz, count, match, place, preds, truth, grads_out, grads, vals, tsc, sums, scale, inv, sems):
+def pair_kernel(sz, count, match, preds, truth, grads_out, grads, vals, tsc, sums, scale, inv, sems):
     norm = 1.0 / (32.0 * sz.ch)
     members = sz.members
     folds = sz.subpad // 8
     copies = Copies(sems)
     vals[...] = preds[...].reshape(members, sz.subpad, LANES).astype(F32)
-    tsc[...] = truth[place[0]].astype(F32)
+    tsc[...] = truth[lax.axis_index("pair") * 2 + lax.axis_index("core")].astype(F32)
 
     def squares(diff):
         return jnp.sum((diff * diff).reshape(folds, 8, LANES), axis=0)
@@ -397,27 +446,29 @@
 
 
 def sibling_kernel(
-    sz, place, back, slope_in, hid_in, ext, w_proj, wt3_in, gp, gpre, hid, edge_up, edge_dn, sib,
-    slope, hid_sib, wt3, rows_f, wpt, sems,
+    sz, back_in, slope_in, hid_in, ext, w_proj, gp, gpre, hid, sib,
+    back, slope, hid_sib, rows_f, wpt, sems,
 ):
     width = sz.lon
     copies = Copies(sems)
+    load_b = copies.start(back_in, back)
     quarter = sz.pos // 4
     load_s = []
     for m in range(sz.mem):
         for part in range(4):
             at = slice(part * quarter, (part + 1) * quarter)
             load_s.append(copies.start(slope_in.at[m, :, at], slope.at[m, :, at]))
-    load_w = copies.start(wt3_in, wt3)
     block = sz.hid // sz.devs
+    mine = lax.axis_index("core")
     load_h = []
-    for half, core in ((hid_sib, 1 - place[2]), (hid, place[2])):
+    for half, core in ((hid_sib, 1 - mine), (hid, mine)):
         for m in range(sz.mem):
             for z in range(sz.devs // 2):
                 at = pl.ds(pl.multiple_of((2 * z + core) * block, block), block)
                 to = slice(z * block, (z + 1) * block)
                 load_h.append(copies.start(hid_in.at[m, at, :], half.at[m, to, :]))
     wpt[...] = (w_proj[...].astype(F32) * 0.5).T.astype(BF16)
+    copies.finish([load_b])
     for m in range(sz.mem):
         for prow in range(sz.prows):
             for q in range(sz.parts):
@@ -434,43 +485,60 @@
             if here.start % quarter == 0:
                 copies.finish([load_s[m * 4 + here.start // quarter]])
             dhid = jnp.dot(wpt[...], gp[m, :, here], preferred_element_type=F32)
-            gpre[m, :, here] = (dhid * slope[m, :, here]).astype(BF16)
+            gpre[m, :, here] = (dhid * slope[m, :, here].astype(F32)).astype(BF16)
+    def store(at, term):
+        sib[:, at : at + term.shape[1]] = term.astype(BF16)
+
+    copies.finish(load_h[: len(load_h) // 2])
+    weight_sums(sz, 1 - mine, gpre, hid_sib, ext, gp, store)
+    copies.finish()
+
+
+def own_kernel(sz, gpre, hid, ext, gp, own):
+    def store(at, term):
+        own[:, at : at + term.shape[1]] = term
+
+    weight_sums(sz, lax.axis_index("core"), gpre, hid, ext, gp, store)
+
+
+def merge_kernel(own, other, out):
+    out[...] = (own[...] + other[...].astype(F32)).astype(BF16)
+
+
+def edge_terms_kernel(sz, gpre, wt3_in, edge_up, edge_dn, gv, wt3, sems):
+    width = sz.lon
+    copies = Copies(sems)
+    for side in range(2):
+        at = slice(0, width) if side == 0 else slice(sz.pos - width, sz.pos)
+        copies.start(wt3_in.at[2 * side], wt3.at[side])
+        copies.start(gpre.at[:, :, at], gv.at[side])
+    copies.finish()
+    for side, edge in enumerate((edge_up, edge_dn)):
+        for m in range(sz.mem):
+            part = jnp.dot(wt3[side], gv[side, m], preferred_element_type=F32)
+            edge[m] = fold_taps(part, sz.ch)
+
+
+def data_kernel(sz, gpre_in, gp_in, wt3_in, ov, ev, gpre, gp, wt3, gs, sems):
+    width = sz.lon
+    copies = Copies(sems)
+    load_w = copies.start(wt3_in, wt3)
+    half = sz.pos // 2
+    loads, load_p = [], []
+    for m in range(sz.mem):
+        for part in range(2):
+            at = slice(part * half, (part + 1) * half)
+            loads.append(copies.start(gpre_in.at[m, :, at], gpre.at[m, :, at]))
+            if part == 0:
+                load_p.append(copies.start(gp_in.at[m], gp.at[m]))
+    zero = jnp.zeros((sz.hid, width), BF16)
     copies.finish([load_w])
     for m in range(sz.mem):
-        for side, edge in enumerate((edge_up, edge_dn)):
-            at = 0 if side == 0 else sz.pos - width
-            part = jnp.dot(
-                wt3[2 * side], gpre[m, :, at : at + width], preferred_element_type=F32
-            )
-            edge[m] = fold_taps(part, sz.ch)
-
-    def store(at, term):
-        sib[:, at : at + term.shape[1]] = term.astype(BF16)
-
-    copies.finish(load_h[: len(load_h) // 2])
-    weight_sums(sz, 1 - place[2], gpre, hid_sib, ext, gp, store)
-    copies.finish()
-
-
-def own_kernel(sz, place, gpre, hid, ext, gp, own):
-    def store(at, term):
-        own[:, at : at + term.shape[1]] = term
-
-    weight_sums(sz, place[2], gpre, hid, ext, gp, store)
-
-
-def merge_kernel(own, other, out):
-    out[...] = (own[...] + other[...].astype(F32)).astype(BF16)
-
-
-def data_kernel(sz, gpre, gp, wt3, ov, ev, gs):
-    width = sz.lon
-    for m in range(sz.mem):
+        copies.finish([loads[2 * m], load_p[m]])
 
         def two_rows(first):
             low, high = max(first, 0), min(first + 2, sz.lat)
             cols = [gpre[m, :, low * width : high * width]]
-            zero = jnp.zeros((sz.hid, width), BF16)
             if first < 0:
                 cols.insert(0, zero)
             if first + 2 > sz.lat:
@@ -478,6 +546,8 @@
             return cols[0] if len(cols) == 1 else jnp.concatenate(cols, axis=1)
 
         for pair in range(sz.lat // 2):
+            if (pair * 2 + 3) * width > half:
+                copies.finish([loads[2 * m + 1]])
             part = None
             for ro in range(3):
                 term = jnp.dot(wt3[ro], two_rows(pair * 2 + 1 - ro), preferred_element_type=F32)
@@ -528,18 +598,12 @@
     count = matchings.shape[0]
     down = [(i, i + 1) for i in range(band_count - 1)]
     up = [(i + 1, i) for i in range(band_count - 1)]
-    band = lax.axis_index("band").astype(jnp.int32)
-    core = lax.axis_index("core").astype(jnp.int32)
-    member = lax.axis_index("pair").astype(jnp.int32) * lax.axis_size("core") + core
-    place = jnp.stack([member, band, core])
-
     ext_shape = (mem, TAPS, pos + 2 * lon)
     part_shape = (sz.devs, mem, sz.subpad, LANES)
     flat = pltpu.VMEM((ch * lat, lon), F32)
     taps_row = pltpu.VMEM((TAPS, lon), F32)
     regroup_rows = pltpu.VMEM((sz.parts, sz.subpad, LANES), F32)
     wide_bf = pltpu.VMEM((mem, hid, pos), BF16)
-    rows_bf = pltpu.VMEM((mem, ch, pos), BF16)
     halo_shape = (band_count, mem * ch, lon)
 
     both_bf = pltpu.VMEM((mem, ch, lat, lon), BF16)
@@ -558,58 +622,72 @@
         ],
         1_000_000,
         3_000_000,
-        (place, states, noise_field),
-        smem=(0,),
+        (states, noise_field),
     )
     halos = lax.all_to_all(send, "band", 0, 0, tiled=True)
-    x_in, e_in, w3, wt3 = call(
-        functools.partial(prep_kernel, sz),
-        "prep",
-        [((mem, ch, pos), BF16), (ext_shape, BF16), ((hid, 3 * TAPS), BF16), ((3, TAPS, hid), BF16)],
+    conv_flops = 2 * mem * pos * hid * 3 * TAPS
+    wide = (mem, hid, pos)
+    pair_shape = (hid, 2 * lon)
+    preact, hidden, ext, fields, w3, wt3 = call(
+        functools.partial(front_kernel, sz),
+        "front",
+        [
+            (wide, BF16),
+            (wide, BF16),
+            (ext_shape, BF16),
+            ((mem, ch, pos), F32),
+            ((hid, 3 * TAPS), BF16),
+            ((3, TAPS, hid), BF16),
+        ],
         [
             both_bf,
             both_f,
             pltpu.VMEM((9 * ch, hid), BF16),
-            rows_bf,
-            pltpu.VMEM((mem, TAPS, pos), BF16),
+            pltpu.VMEM((ch, pos), F32),
+            pltpu.VMEM((2,) + pair_shape, F32),
+            wide_bf,
+            wide_bf,
+            pltpu.VMEM(ext_shape, BF16),
+            pltpu.VMEM((mem, ch, pos), F32),
             pltpu.VMEM((hid, 3 * TAPS), BF16),
             pltpu.VMEM((3, TAPS, hid), BF16),
             flat,
             taps_row,
-            dma(4 * mem + 3),
-        ],
-        10_000_000,
-        8_000_000,
-        (states, noise_field, w_conv.T),
-    )
-
-    conv_flops = 2 * mem * pos * hid * 3 * TAPS
+            dma(3 + 4 * mem + mem * lat // 2),
+        ],
+        conv_flops,
+        9_000_000,
+        (states, noise_field, w_conv.T, w_proj),
+        vmem=(3,),
+        limit=55,
+    )
+    units = 2 * mem
     preact, hidden, ext, snd = call(
-        functools.partial(forward_kernel, sz),
-        "forward",
-        [((mem, hid, pos), BF16), ((mem, hid, pos), BF16), (ext_shape, BF16), (part_shape, BF16)],
-        [
-            pltpu.VMEM(ext_shape, BF16),
-            rows_bf,
+        functools.partial(rim_kernel, sz),
+        "rim",
+        [(wide, BF16), (wide, BF16), (ext_shape, BF16), (part_shape, BF16)],
+        [
+            pltpu.VMEM((2,) + pair_shape, F32),
+            pltpu.VMEM((units,) + pair_shape, BF16),
+            pltpu.VMEM((units,) + pair_shape, BF16),
+            pltpu.VMEM((mem, sz.devs, sz.subpad, LANES), BF16),
             pltpu.VMEM(halo_shape, BF16),
+            pltpu.VMEM((2, mem, TAPS, 4 * lon), BF16),
+            pltpu.VMEM((mem, ch, pos), F32),
             pltpu.VMEM((hid, 3 * TAPS), BF16),
             pltpu.VMEM(w_proj.shape, BF16),
-            pltpu.VMEM((2, hid, 2 * lon), F32),
-            wide_bf,
-            wide_bf,
-            pltpu.VMEM((mem, sz.devs, sz.subpad, LANES), BF16),
+            pltpu.VMEM((TAPS, 2 * lon), F32),
+            pltpu.VMEM((2, ch, 2 * lon), F32),
             taps_row,
             regroup_rows,
-            pltpu.VMEM((ch, pos), F32),
             pltpu.VMEM((mem * ch, lon), F32),
-            pltpu.VMEM((2, mem, TAPS, lon), BF16),
-            dma(5 + 3 * mem + mem * lat // 2),
-        ],
-        conv_flops,
+            dma(7 + 2 * units + 2 * mem),
+        ],
+        conv_flops // 4,
         9_000_000,
-        (place, e_in, x_in, halos, w3, w_proj),
-        smem=(0,),
-        aliases={1: 2},
+        (halos, preact, hidden, ext, fields, w3, w_proj),
+        limit=53,
+        aliases={1: 0, 2: 1, 3: 2},
     )
 
     preds = lax.all_to_all(snd, MEMBER, 0, 0, tiled=True)
@@ -632,8 +710,8 @@
         grid=(mem, 4),
         in_specs=[block],
         out_specs=block,
-        out_shape=jax.ShapeDtypeStruct((mem, hid, pos), F32),
-        compiler_params=pltpu.CompilerParams(vmem_limit_bytes=16 * 1024 * 1024),
+        out_shape=jax.ShapeDtypeStruct((mem, hid, pos), BF16),
+        compiler_params=pltpu.CompilerParams(vmem_limit_bytes=40 * 1024 * 1024),
         cost_estimate=pl.CostEstimate(
             flops=10 * mem * hid * pos, bytes_accessed=8 * mem * hid * pos, transcendentals=0
         ),
@@ -656,40 +734,37 @@
         ],
         sz.members * 30 * sz.subpad * LANES,
         2_000_000,
-        (matchings, place, preds, truth),
-        smem=(0, 1),
-        vmem=(2, 3),
+        (matchings, preds, truth),
+        smem=(0,),
+        vmem=(1, 2),
         limit=16,
     )
     back = lax.all_to_all(grads, MEMBER, 0, 0, tiled=True)
 
     half = (hid // 2, sz.cols)
     edge_shape = (mem, ch, lon)
-    grad_pred, grad_pre, hid_own, edge_up, edge_dn, sibling = call(
+    grad_pred, grad_pre, hid_own, sibling = call(
         functools.partial(sibling_kernel, sz),
         "sibling",
         [
             ((mem, ch, pos), BF16),
             ((mem, hid, pos), BF16),
             ((mem, hid // 2, pos), BF16),
-            (edge_shape, F32),
-            (edge_shape, F32),
             (half, BF16),
         ],
         [
-            pltpu.VMEM((mem, hid, pos), F32),
+            pltpu.VMEM(part_shape, BF16),
+            pltpu.VMEM((mem, hid, pos), BF16),
             pltpu.VMEM((mem, hid // 2, pos), BF16),
-            pltpu.VMEM((3, TAPS, hid), BF16),
             regroup_rows,
             pltpu.VMEM((hid, ch), BF16),
             dma(1 + 4 * mem + mem * sz.devs),
         ],
         conv_flops,
         9_000_000,
-        (place, back, slope, hidden, ext, w_proj, wt3),
-        smem=(0,),
-        vmem=(1, 4, 5),
-        vmem_outs=range(6),
+        (back, slope, hidden, ext, w_proj),
+        vmem=(0, 3, 4),
+        vmem_outs=range(4),
         limit=40,
     )
     swapped = lax.ppermute(sibling, "core", [(0, 1), (1, 0)])
@@ -700,9 +775,8 @@
         [],
         conv_flops // 2,
         9_000_000,
-        (place, grad_pre, hid_own, ext, grad_pred),
-        smem=(0,),
-        vmem=range(1, 5),
+        (grad_pre, hid_own, ext, grad_pred),
+        vmem=range(4),
         vmem_outs=(0,),
         limit=16,
     )
@@ -723,7 +797,22 @@
     terms = lax.all_to_all(
         partial.reshape(shards // 2, each, sz.cols), ("pair", "band"), 0, 0, tiled=True
     )
-    edge_up, edge_dn, _ = lax.optimization_barrier((edge_up, edge_dn, partial))
+    late_wt3, _ = lax.optimization_barrier((wt3, partial))
+    edge_up, edge_dn = call(
+        functools.partial(edge_terms_kernel, sz),
+        "edge_terms",
+        [(edge_shape, F32), (edge_shape, F32)],
+        [
+            pltpu.VMEM((2, mem, hid, lon), BF16),
+            pltpu.VMEM((2, TAPS, hid), BF16),
+            dma(4),
+        ],
+        200_000_000,
+        1_500_000,
+        (grad_pre, late_wt3),
+        vmem_outs=(0, 1),
+        limit=60,
+    )
     from_dn = lax.ppermute(edge_up, "band", up)
     from_up = lax.ppermute(edge_dn, "band", down)
 
@@ -731,13 +820,18 @@
         functools.partial(data_kernel, sz),
         "data",
         [((mem, ch, lat, lon), BF16), ((2,) + edge_shape, F32)],
-        [flat],
+        [
+            wide_bf,
+            pltpu.VMEM((mem, ch, pos), BF16),
+            pltpu.VMEM((3, TAPS, hid), BF16),
+            flat,
+            dma(1 + 3 * mem),
+        ],
         conv_flops,
         8_000_000,
-        (grad_pre, grad_pred, wt3),
-        vmem=range(3),
+        (grad_pre, grad_pred, late_wt3),
         vmem_outs=(0, 1),
-        limit=16,
+        limit=50,
     )
     (grad_states,) = call(
         functools.partial(border_kernel, sz),

time: 108 us -> 107 us (level)
  local copies, waits for them, and re-layouts: 10.6 us -> 6.09 us
  Pallas kernels: 42 us -> 45 us
    unnamed x28 -> x20, local copies, waits for them, and re-layouts: 10.6 us -> 6.09 us
    pallas_call x11 -> x12, Pallas kernels: 39 us -> 41.7 us  [call(): pl.pallas_call(kernel, in_specs=[specs[kind(i)] for i in range(len(args))...]
    all_to_all x1, waiting for transfers between devices: 10 us -> 11.2 us  [on_device(): back = lax.all_to_all(grads, MEMBER, 0, 0, tiled=True)]
  transfers between devices with their start and end apart: 7 -> 7, of which waited for: 4 -> 3; matrix products, arithmetic and copies ran while one was open for 0% -> 0% of each run, Pallas kernels for 15% -> 24%
where the time goes in v6:
time: 107 us; the launch traced here: 106 us
  Pallas kernels  45 us (42%)
  waiting for transfers between devices  29.8 us (28%)
  starting transfers between devices  24.1 us (23%)
  local copies, waits for them, and re-layouts  6.09 us (6%)
    pallas_call x12, Pallas kernels, call(): pl.pallas_call(kernel, in_specs=[specs[kind(i)] for i in range(len(args))...  41.7 us
    all_to_all x1, waiting for transfers between devices, on_device(): preds = lax.all_to_all(snd, MEMBER, 0, 0, tiled=True)  18.1 us
    all_to_all x1, waiting for transfers between devices, on_device(): back = lax.all_to_all(grads, MEMBER, 0, 0, tiled=True)  11.2 us
    unnamed x20, local copies, waits for them, and re-layouts  6.09 us
    all_to_all x1, starting transfers between devices, on_device(): halos = lax.all_to_all(send, 'band', 0, 0, tiled=True)  5.2 us
    all_to_all x1, starting transfers between devices, on_device(): lax.all_to_all(partial.reshape(shards // 2, each, sz.cols), ('pair', 'ban...  5.05 us
    all_to_all x1, starting transfers between devices, on_device(): preds = lax.all_to_all(snd, MEMBER, 0, 0, tiled=True)  4.89 us
    ppermute x1, starting transfers between devices, on_device(): from_up = lax.ppermute(edge_dn, 'band', down)  3.83 us
  transfers between devices with their start and end apart: 7, of which 3 were waited for; matrix products, arithmetic and copies ran while one was open for 0% of the time, Pallas kernels for 24%

profile of v6, /device:TPU:0, one launch (start us, length us, event | category | flops | bytes accessed | tf_op | source)
XLA Modules:
  0.0 105.8 jit_solution(14034928105041732264)
XLA Ops:
  0.6 2.4 %edges.1 = bf16[4,168,128]{2,1,0:T(8,128)(2,1)} custom-call(bf16[2,84,16,128]{3,2,1,0:T(8,128)(2,1)} %states.3, f32[2,84,16,128]{3,2,1,0:T(8,128)} %noise.3), custom_call_target="tpu_custom_call" | custom-call | flops 1000000 | bytes 3000000 | tf_op jit(solution)/shard_map/edges/pallas_call | solution.py:29
  3.0 5.2 %all-to-all-start = ((bf16[4,168,128]{2,1,0:T(8,128)(2,1)}), bf16[4,168,128]{2,1,0:T(8,128)(2,1)S(1)}, u32[]{:S(2)}, u32[]{:S(2)}) async-start(bf16[4,168,128]{2,1,0:T(8,128)(2,1)} %edges.1), calls=%async_computation | async-start | bytes 344064 | tf_op jit(solution)/shard_map/all_to_all | solution.py:627
  8.2 0.0 copy-start.8
  8.2 8.6 %front.1 = (bf16[2,512,2048]{2,1,0:T(8,128)(2,1)}, bf16[2,512,2048]{2,1,0:T(8,128)(2,1)}, bf16[2,256,2304]{2,1,0:T(8,128)(2,1)}, f32[2,84,2048]{2,1,0:T(8,128)},...) custom-call(bf16[2,84,16,128]{3,2,1,0:T(8,128)(2,1)} %states.3, f32[2,84,16,128]{3,2,1,0:T(8,128)} %noise.3, ...), custom_call_target="tpu_custom_call" | custom-call | flops 3221225472 | bytes 9000000 | tf_op jit(solution)/shard_map/front/pallas_call | solution.py:29
  16.9 0.0 all-to-all-done.halos_in
  16.9 0.0 copy-done.8
  16.9 0.0 copy-start.7
  16.9 0.0 copy-start.9
  16.9 5.5 %rim.1 = (bf16[2,512,2048]{2,1,0:T(8,128)(2,1)}, bf16[2,512,2048]{2,1,0:T(8,128)(2,1)}, bf16[2,256,2304]{2,1,0:T(8,128)(2,1)}, bf16[8,2,168,128]{3,2,1,0:T(8,128)(2,1)}) custom-call(bf16[4,168,128]{2,1,0:T(8,128)(2,1)S(1)} %all-to-all-done.halos_in, ...), custom_call_target="tpu_custom_call", output_to_operand_aliasing={{0}: (1, {}), {1}: (2, {}), {2}: (3, {})} | custom-call | flops 805306368 | bytes 9000000 | tf_op jit(solution)/shard_map/rim/pallas_call | solution.py:29
  22.5 4.9 %all-to-all-start.1 = ((bf16[8,2,168,128]{3,2,1,0:T(8,128)(2,1)}), bf16[8,2,168,128]{3,2,1,0:T(8,128)(2,1)S(1)}, u32[]{:S(2)}, u32[]{:S(2)}) async-start(bf16[8,2,168,128]{3,2,1,0:T(8,128)(2,1)} %get-tuple-element.30), calls=%async_computation.1 | async-start | bytes 1376256 | tf_op jit(solution)/shard_map/all_to_all | solution.py:693
  27.4 0.0 copy-done.7
  27.4 0.7 truth.1
  28.1 18.1 %all-to-all-done.1.preds = bf16[8,2,168,128]{3,2,1,0:T(8,128)(2,1)S(1)} async-done(((bf16[8,2,168,128]{3,2,1,0:T(8,128)(2,1)}), bf16[8,2,168,128]{3,2,1,0:T(8,128)(2,1)S(1)}, u32[]{:S(2)}, u32[]{:S(2)}) %all-to-all-start.1) | async-done | bytes 688160 | tf_op jit(solution)/shard_map/all_to_all | solution.py:693
  46.2 0.0 copy-done.9
  46.2 4.0 %pairs.1 = bf16[8,2,168,128]{3,2,1,0:T(8,128)(2,1)} custom-call(s32[4,16]{1,0:T(4,128)S(1)} %copy-done.9, bf16[8,2,168,128]{3,2,1,0:T(8,128)(2,1)S(1)} %all-to-all-done.1.preds, bf16[8,168,128]{2,1,0:T(8,128)(2,1)S(1)} %truth.1), custom_call_target="tpu_custom_call" | custom-call | flops 10321920 | bytes 2000000 | tf_op jit(solution)/shard_map/pairs/pallas_call | solution.py:29
  50.2 3.7 %all-to-all-start.2 = ((bf16[8,2,168,128]{3,2,1,0:T(8,128)(2,1)}), bf16[8,2,168,128]{3,2,1,0:T(8,128)(2,1)S(1)}, u32[]{:S(2)}, u32[]{:S(2)}) async-start(bf16[8,2,168,128]{3,2,1,0:T(8,128)(2,1)} %pairs.1), calls=%async_computation.2 | async-start | bytes 1376256 | tf_op jit(solution)/shard_map/all_to_all | solution.py:742
  53.9 0.0 copy-start
  54.0 2.2 %copy-done = bf16[2,512,2048]{2,1,0:T(8,128)(2,1)S(1)} copy-done((bf16[2,512,2048]{2,1,0:T(8,128)(2,1)S(1)}, bf16[2,512,2048]{2,1,0:T(8,128)(2,1)}, u32[]{:S(2)}) %copy-start) | copy-done | bytes 4194328
  56.1 0.0 copy-start.2
  56.1 3.3 %slope.1.slope_in = bf16[2,512,2048]{2,1,0:T(8,128)(2,1)S(1)} custom-call(bf16[2,512,2048]{2,1,0:T(8,128)(2,1)S(1)} %copy-done), custom_call_target="tpu_custom_call" | custom-call | flops 20971520 | bytes 16777216 | tf_op jit(solution)/shard_map/slope/pallas_call | solution.py:708
  59.4 0.0 copy-start.3
  59.4 1.9 %copy-done.3 = bf16[2,512,2048]{2,1,0:T(8,128)(2,1)} copy-done((bf16[2,512,2048]{2,1,0:T(8,128)(2,1)}, bf16[2,512,2048]{2,1,0:T(8,128)(2,1)S(1)}, u32[]{:S(2)}) %copy-start.3) | copy-done | bytes 4194328
  61.3 11.2 %all-to-all-done.2.back_in = bf16[8,2,168,128]{3,2,1,0:T(8,128)(2,1)S(1)} async-done(((bf16[8,2,168,128]{3,2,1,0:T(8,128)(2,1)}), bf16[8,2,168,128]{3,2,1,0:T(8,128)(2,1)S(1)}, u32[]{:S(2)}, u32[]{:S(2)}) %all-to-all-start.2) | async-done | bytes 688160 | tf_op jit(solution)/shard_map/all_to_all | solution.py:742
  72.5 0.0 copy-start.5
  72.5 0.8 copy-done.5
  73.4 0.0 copy-done.2
  73.4 0.0 copy-start.6
  73.4 1.1 %copy-done.6 = bf16[8,2,168,128]{3,2,1,0:T(8,128)(2,1)S(1)} copy-done((bf16[8,2,168,128]{3,2,1,0:T(8,128)(2,1)S(1)}, bf16[8,2,168,128]{3,2,1,0:T(8,128)(2,1)}, u32[]{:S(2)}) %copy-start.6) | copy-done | bytes 688152
  74.5 6.4 %sibling.1 = (bf16[2,84,2048]{2,1,0:T(8,128)(2,1)S(1)}, bf16[2,512,2048]{2,1,0:T(8,128)(2,1)S(1)}, bf16[2,256,2048]{2,1,0:T(8,128)(2,1)S(1)}, bf16[256,896]{1,0:T(8,128)(2,1)S(1)}) custom-call(bf16[8,2,168,128]{3,2,1,0:T(8,128)(2,1)S(1)} %copy-done.6, bf16[2,512,2048]{2,1,0:T(8,128)(2,1)} %copy-done.3, bf16[2,512,2048]{2,1,0:T(8,128)(2,1)} %get-tuple-element.33.hid_in, ...), custom_call_target="tpu_custom_call" | custom-call | flops 3221225472 | bytes 9000000 | tf_op jit(solution)/shard_map/sibling/pallas_call | solution.py:29
  80.9 0.0 copy-start.1
  80.9 0.1 collective-permute-start
  81.0 2.4 %own.1 = f32[256,896]{1,0:T(8,128)S(1)} custom-call(bf16[2,512,2048]{2,1,0:T(8,128)(2,1)S(1)} %get-tuple-element.35.gpre.gpre_in, bf16[2,256,2048]{2,1,0:T(8,128)(2,1)S(1)} %get-tuple-element.38.hid, bf16[2,256,2304]{2,1,0:T(8,128)(2,1)S(1)} %copy-done.2, bf16[2,84,2048]{2,1,0:T(8,128)(2,1)S(1)} %get-tuple-element.36.gp.gp_in), custom_call_target="tpu_custom_call" | custom-call | flops 1610612736 | bytes 9000000 | tf_op jit(solution)/shard_map/own/pallas_call | solution.py:29
  83.3 0.0 copy-done.1
  83.4 0.0 copy-start.4
  83.4 0.0 collective-permute-done.other
  83.4 0.9 merge.1
  84.2 5.1 %all-to-all-start.3 = ((bf16[16,16,896]{2,1,0:T(8,128)(2,1)}), bf16[16,16,896]{2,1,0:T(8,128)(2,1)S(1)}, u32[]{:S(2)}, u32[]{:S(2)}) async-start(bf16[16,16,896]{2,1,0:T(8,128)(2,1)} %bitcast.1), calls=%async_computation.3 | async-start | bytes 917504 | tf_op jit(solution)/shard_map/all_to_all | solution.py:797
  89.3 2.4 %edge_terms.1 = (f32[2,84,128]{2,1,0:T(8,128)}, f32[2,84,128]{2,1,0:T(8,128)}) custom-call(bf16[2,512,2048]{2,1,0:T(8,128)(2,1)} %copy-done.1, bf16[3,256,512]{2,1,0:T(8,128)(2,1)} %get-tuple-element.40.wt3_in), custom_call_target="tpu_custom_call" | custom-call | flops 200000000 | bytes 1500000 | tf_op jit(solution)/shard_map/edge_terms/pallas_call | solution.py:29
  91.7 3.8 %collective-permute-start.1 = (f32[2,84,128]{2,1,0:T(8,128)}, f32[2,84,128]{2,1,0:T(8,128)S(1)}, u32[]{:S(2)}, u32[]{:S(2)}) collective-permute-start(f32[2,84,128]{2,1,0:T(8,128)} %get-tuple-element.43), channel_id=1, source_target_pairs={{0,1},{1,2},{2,3},{4,5},{5,6},{6,7},{8,9},{9,10},{10,11},{12,13},{... | collective-permute-start | bytes 258056 | tf_op jit(solution)/shard_map/ppermute | solution.py:817
  95.5 1.3 %collective-permute-start.2 = (f32[2,84,128]{2,1,0:T(8,128)}, f32[2,84,128]{2,1,0:T(8,128)S(1)}, u32[]{:S(2)}, u32[]{:S(2)}) collective-permute-start(f32[2,84,128]{2,1,0:T(8,128)} %get-tuple-element.44), channel_id=1, source_target_pairs={{1,0},{2,1},{3,2},{5,4},{6,5},{7,6},{9,8},{10,9},{11,10},{13,12},{... | collective-permute-start | bytes 258056 | tf_op jit(solution)/shard_map/ppermute | solution.py:816
  96.8 0.0 copy-done.4
  96.8 6.7 %data.1 = (bf16[2,84,16,128]{3,2,1,0:T(8,128)(2,1)S(1)}, f32[2,2,84,128]{3,2,1,0:T(8,128)S(1)}) custom-call(bf16[2,512,2048]{2,1,0:T(8,128)(2,1)} %copy-done.1, bf16[2,84,2048]{2,1,0:T(8,128)(2,1)S(1)} %get-tuple-element.36.gp.gp_in, bf16[3,256,512]{2,1,0:T(8,128)(2,1)S(1)} %copy-done.4), custom_call_target="tpu_custom_call" | custom-call | flops 3221225472 | bytes 8000000 | tf_op jit(solution)/shard_map/data/pallas_call | solution.py:29
  103.5 0.0 collective-permute-done.1.uv
  103.6 0.5 collective-permute-done.2.dv
  104.1 1.0 border.1
  105.1 0.0 all-to-all-done.3.terms
  105.1 0.7 final.1
Async XLA Ops:
  3.0 13.9 %all-to-all-start = ((bf16[4,168,128]{2,1,0:T(8,128)(2,1)}), bf16[4,168,128]{2,1,0:T(8,128)(2,1)S(1)}, u32[]{:S(2)}, u32[]{:S(2)}) async-start(bf16[4,168,128]{2,1,0:T(8,128)(2,1)} %edges.1), calls=%async_computation | async-start | bytes 344064 | tf_op jit(solution)/shard_map/all_to_all | solution.py:627
  8.2 8.7 %copy-start.8 = (bf16[84,512]{1,0:T(8,128)(2,1)S(1)}, bf16[84,512]{1,0:T(8,128)(2,1)}, u32[]{:S(2)}) copy-start(bf16[84,512]{1,0:T(8,128)(2,1)} %w_proj.3) | copy-start | bytes 258052
  16.9 10.5 %copy-start.7 = (bf16[84,16,128]{2,1,0:T(8,128)(2,1)S(1)}, bf16[84,16,128]{2,1,0:T(8,128)(2,1)}, u32[]{:S(2)}) copy-start(bf16[84,16,128]{2,1,0:T(8,128)(2,1)} %target) | copy-start | bytes 1032196
  16.9 29.3 %copy-start.9 = (s32[4,16]{1,0:T(4,128)S(1)}, s32[4,16]{1,0:T(4,128)}, u32[]{:S(2)}) copy-start(s32[4,16]{1,0:T(4,128)} %match.1) | copy-start | bytes 772
  22.5 23.7 %all-to-all-start.1 = ((bf16[8,2,168,128]{3,2,1,0:T(8,128)(2,1)}), bf16[8,2,168,128]{3,2,1,0:T(8,128)(2,1)S(1)}, u32[]{:S(2)}, u32[]{:S(2)}) async-start(bf16[8,2,168,128]{3,2,1,0:T(8,128)(2,1)} %get-tuple-element.30), calls=%async_computation.1 | async-start | bytes 1376256 | tf_op jit(solution)/shard_map/all_to_all | solution.py:693
  50.2 22.3 %all-to-all-start.2 = ((bf16[8,2,168,128]{3,2,1,0:T(8,128)(2,1)}), bf16[8,2,168,128]{3,2,1,0:T(8,128)(2,1)S(1)}, u32[]{:S(2)}, u32[]{:S(2)}) async-start(bf16[8,2,168,128]{3,2,1,0:T(8,128)(2,1)} %pairs.1), calls=%async_computation.2 | async-start | bytes 1376256 | tf_op jit(solution)/shard_map/all_to_all | solution.py:742
  53.9 2.2 %copy-start = (bf16[2,512,2048]{2,1,0:T(8,128)(2,1)S(1)}, bf16[2,512,2048]{2,1,0:T(8,128)(2,1)}, u32[]{:S(2)}) copy-start(bf16[2,512,2048]{2,1,0:T(8,128)(2,1)} %get-tuple-element.32.preact) | copy-start | bytes 12582916
  56.1 17.2 %copy-start.2 = (bf16[2,256,2304]{2,1,0:T(8,128)(2,1)S(1)}, bf16[2,256,2304]{2,1,0:T(8,128)(2,1)}, u32[]{:S(2)}) copy-start(bf16[2,256,2304]{2,1,0:T(8,128)(2,1)} %get-tuple-element.34.ext) | copy-start | bytes 7077892
  59.4 1.9 %copy-start.3 = (bf16[2,512,2048]{2,1,0:T(8,128)(2,1)}, bf16[2,512,2048]{2,1,0:T(8,128)(2,1)S(1)}, u32[]{:S(2)}) copy-start(bf16[2,512,2048]{2,1,0:T(8,128)(2,1)S(1)} %slope.1.slope_in) | copy-start | bytes 12582916
  72.5 0.8 copy-start.5
  73.4 1.1 %copy-start.6 = (bf16[8,2,168,128]{3,2,1,0:T(8,128)(2,1)S(1)}, bf16[8,2,168,128]{3,2,1,0:T(8,128)(2,1)}, u32[]{:S(2)}) copy-start(bf16[8,2,168,128]{3,2,1,0:T(8,128)(2,1)} %copy-done.5) | copy-start | bytes 2064388
  80.9 2.5 %copy-start.1 = (bf16[2,512,2048]{2,1,0:T(8,128)(2,1)}, bf16[2,512,2048]{2,1,0:T(8,128)(2,1)S(1)}, u32[]{:S(2)}) copy-start(bf16[2,512,2048]{2,1,0:T(8,128)(2,1)S(1)} %get-tuple-element.35.gpre.gpre_in) | copy-start | bytes 12582916
  80.9 2.5 %collective-permute-start = (bf16[256,896]{1,0:T(8,128)(2,1)S(1)}, bf16[256,896]{1,0:T(8,128)(2,1)S(1)}, u32[]{:S(2)}, u32[]{:S(2)}) collective-permute-start(bf16[256,896]{1,0:T(8,128)(2,1)S(1)} %get-tuple-element.39), channel_id=1, source_target_pairs={{0,4},{4,0},{1,5},{5,1},{2,6},{6,2},{3,7},{7,3},{8,12},{12,8},{9,1... | collective-permute-start | bytes 1376264 | tf_op jit(solution)/shard_map/ppermute | solution.py:770
  83.4 13.5 %copy-start.4 = (bf16[3,256,512]{2,1,0:T(8,128)(2,1)S(1)}, bf16[3,256,512]{2,1,0:T(8,128)(2,1)}, u32[]{:S(2)}) copy-start(bf16[3,256,512]{2,1,0:T(8,128)(2,1)} %get-tuple-element.40.wt3_in) | copy-start | bytes 2359300
  84.2 20.8 %all-to-all-start.3 = ((bf16[16,16,896]{2,1,0:T(8,128)(2,1)}), bf16[16,16,896]{2,1,0:T(8,128)(2,1)S(1)}, u32[]{:S(2)}, u32[]{:S(2)}) async-start(bf16[16,16,896]{2,1,0:T(8,128)(2,1)} %bitcast.1), calls=%async_computation.3 | async-start | bytes 917504 | tf_op jit(solution)/shard_map/all_to_all | solution.py:797
  91.7 11.9 %collective-permute-start.1 = (f32[2,84,128]{2,1,0:T(8,128)}, f32[2,84,128]{2,1,0:T(8,128)S(1)}, u32[]{:S(2)}, u32[]{:S(2)}) collective-permute-start(f32[2,84,128]{2,1,0:T(8,128)} %get-tuple-element.43), channel_id=1, source_target_pairs={{0,1},{1,2},{2,3},{4,5},{5,6},{6,7},{8,9},{9,10},{10,11},{12,13},{... | collective-permute-start | bytes 258056 | tf_op jit(solution)/shard_map/ppermute | solution.py:817
  95.5 8.6 %collective-permute-start.2 = (f32[2,84,128]{2,1,0:T(8,128)}, f32[2,84,128]{2,1,0:T(8,128)S(1)}, u32[]{:S(2)}, u32[]{:S(2)}) collective-permute-start(f32[2,84,128]{2,1,0:T(8,128)} %get-tuple-element.44), channel_id=1, source_target_pairs={{1,0},{2,1},{3,2},{5,4},{6,5},{7,6},{9,8},{10,9},{11,10},{13,12},{... | collective-permute-start | bytes 258056 | tf_op jit(solution)/shard_map/ppermute | solution.py:816

commit v7 on v6

--- a/solution.py
+++ b/solution.py
@@ -173,16 +173,19 @@
     es[...] = jnp.zeros_like(es)
     taps = 3 * sz.ch
     last = sz.lat // 2 - 1
-
-    def expand(m):
+    stops = (last // 2,)
+
+    def load(m):
         copies.finish(loads[m])
-        xs[...] = (st[m].astype(F32) + ns[m]).astype(BF16).astype(F32).reshape(
+        xs[m] = (st[m].astype(F32) + ns[m]).astype(BF16).astype(F32).reshape(
             sz.ch * sz.lat, sz.lon
         )
-        for row in range(sz.lat):
-            vals = xs[pl.ds(row, sz.ch, stride=sz.lat), :]
-            xv[:, row * width : (row + 1) * width] = vals
-            ext[m, :, (row + 1) * width : (row + 2) * width] = expand_row(vals, es)
+
+    def expand(m, rows):
+        for row in rows:
+            vals = xs[m, pl.ds(row, sz.ch, stride=sz.lat), :]
+            xv[m, :, row * width : (row + 1) * width] = vals
+            ext[m, :, (row + 1) * width : (row + 2) * width] = expand_row(vals, es.at[row % 4])
 
     def rest(m, pair):
         here = slice(pair * 2 * width, (pair + 1) * 2 * width)
@@ -190,10 +193,11 @@
         preb[m, :, here] = preact.astype(BF16)
         hidden = hidden_pair(preact)
         hid[m, :, here] = hidden
-        preds[m, :, here] = project_pair(xv[:, here], w_proj, hidden)
+        preds[m, :, here] = project_pair(xv[m, :, here], w_proj, hidden)
 
     for m in range(sz.mem):
-        expand(m)
+        load(m)
+        expand(m, range(5))
         if m == 0:
             copies.finish([w_load])
             for ro in range(3):
@@ -208,20 +212,23 @@
                 w3[:, ro * TAPS : (ro + 1) * TAPS] = piece.T
             copies.start(w3, w3_out)
             copies.start(wt3v, wt3_out)
-        inner = slice(width, width + sz.pos)
-        copies.start(ext.at[m, :, inner], ext_out.at[m, :, inner])
         pre[1] = conv_pair(sz, ext, w3, m, 1)
         for pair in range(1, last):
+            expand(m, range(pair * 2 + 3, min(pair * 2 + 5, sz.lat)) if pair > 1 else ())
             if pair + 1 < last:
+                if pair == 1:
+                    expand(m, range(5, 7))
                 pre[(pair + 1) % 2] = conv_pair(sz, ext, w3, m, pair + 1)
             rest(m, pair)
-            if pair % 2 == 0 or pair + 1 == last:
-                first = pair if pair % 2 else pair - 1
+            if pair == stops[0] or pair + 1 == last:
+                first = 1 if pair == stops[0] else stops[0] + 1
                 here = slice(first * 2 * width, (pair + 1) * 2 * width)
                 copies.start(preb.at[m, :, here], pre_out.at[m, :, here])
                 copies.start(hid.at[m, :, here], hid_out.at[m, :, here])
         here = slice(2 * width, sz.pos - 2 * width)
         copies.start(preds.at[m, :, here], preds_out.at[m, :, here])
+        inner = slice(width, width + sz.pos)
+        copies.start(ext.at[m, :, inner], ext_out.at[m, :, inner])
     copies.finish()
 
 
@@ -274,9 +281,11 @@
     copies.finish([load_h])
     for side in range(2):
         at = 0 if side == 0 else 3 * width
-        hr[...] = halo_rows(sz, halos, side)
+        hr[side] = halo_rows(sz, halos, side)
         for m in range(sz.mem):
-            ends[side, m, :, at : at + width] = expand_row(hr[pl.ds(m * sz.ch, sz.ch), :], es)
+            ends[side, m, :, at : at + width] = expand_row(
+                hr[side, pl.ds(m * sz.ch, sz.ch), :], es.at[side * sz.mem + m]
+            )
         to = 0 if side == 0 else width + sz.pos
         copies.start(ends.at[side, :, :, at : at + width], ext_out.at[:, :, to : to + width])
     copies.finish([load_w] + load_e)
@@ -285,30 +294,22 @@
 
     def conv(i):
         m, side = units[i]
-        pre[i % 2] = conv_pair(sz, ends.at[side], w3, m, 0)
-
-    conv(0)
-    copies.finish([load_p])
-    for i, (m, side) in enumerate(units):
-        if i + 1 < len(units):
-            conv(i + 1)
-        here = slice(side * last * 2 * width, (side * last + 1) * 2 * width)
-        preact = pre[i % 2]
+        pre[i] = conv_pair(sz, ends.at[side], w3, m, 0)
+
+    def rest(i):
+        m, side = units[i]
+        preact = pre[i]
         preb[i] = preact.astype(BF16)
         hidden = hidden_pair(preact)
         hid[i] = hidden
-        copies.start(preb.at[i], pre_out.at[m, :, here])
-        copies.start(hid.at[i], hid_out.at[m, :, here])
-        xf[...] = ends[side, m, :, width : 3 * width].astype(F32)
-        rim[side] = project_pair(xf[pl.ds(sz.ch, sz.ch), :], w_proj, hidden)
-        if side == 0:
-            continue
-        copies.finish([load_f[m]])
-
+        xf[i] = ends[side, m, :, width : 3 * width].astype(F32)
+        rim[i] = project_pair(xf[i, pl.ds(sz.ch, sz.ch), :], w_proj, hidden)
+
+    def patches(m):
         def row_of(row):
             if row < 2 or row >= sz.lat - 2:
                 at = row % 2 * width
-                return rim[0 if row < 2 else 1, :, at : at + width]
+                return rim[2 * m if row < 2 else 2 * m + 1, :, at : at + width]
             return preds[m, :, row * width : (row + 1) * width]
 
         for prow in range(sz.prows):
@@ -316,10 +317,24 @@
                 first = prow * 8 + group * sz.parts
                 rows = [row_of(first + k) for k in range(sz.parts)]
                 for q, out in enumerate(swap_blocks(rows)):
-                    ps[q, pl.ds(group * sz.ch, sz.ch), :] = out
-            for q in range(sz.parts):
-                snd[m, prow * sz.parts + q] = ps[q].astype(BF16)
+                    ps[m, prow * sz.parts + q, pl.ds(group * sz.ch, sz.ch), :] = out
+            for q in range(prow * sz.parts, (prow + 1) * sz.parts):
+                snd[m, q] = ps[m, q].astype(BF16)
+
+    copies.finish([load_p] + load_f)
+    conv(0)
+    for i, (m, side) in enumerate(units):
+        if i + 1 < len(units):
+            conv(i + 1)
+        rest(i)
+        if side == 1:
+            patches(m)
+    for m in range(sz.mem):
         copies.start(snd.at[m], snd_out.at[:, m])
+    for i, (m, side) in enumerate(units):
+        here = slice(side * last * 2 * width, (side * last + 1) * 2 * width)
+        copies.start(preb.at[i], pre_out.at[m, :, here])
+        copies.start(hid.at[i], hid_out.at[m, :, here])
     copies.finish()
 
 
@@ -358,7 +373,7 @@
             sums[pl.ds(at, 8), :] = squares(own - vals[other])
         return carry
 
-    lax.fori_loop(0, members, first, 0)
+    lax.fori_loop(0, members, first, 0, unroll=2)
     rows = (count + 1) * members
     total = sums[pl.ds(0, rows, stride=8), :]
     for j in range(1, 8):
@@ -397,7 +412,7 @@
             grads[m // sz.mem, m % sz.mem] = second(m)
             return carry
 
-        lax.fori_loop(0, members // 4, several, 0)
+        lax.fori_loop(0, members // 4, several, 0, unroll=2)
         at = slice(part * quarter, (part + 1) * quarter)
         copies.start(grads.at[at], grads_out.at[at])
     copies.finish()
@@ -452,12 +467,7 @@
     width = sz.lon
     copies = Copies(sems)
     load_b = copies.start(back_in, back)
-    quarter = sz.pos // 4
-    load_s = []
-    for m in range(sz.mem):
-        for part in range(4):
-            at = slice(part * quarter, (part + 1) * quarter)
-            load_s.append(copies.start(slope_in.at[m, :, at], slope.at[m, :, at]))
+    load_s = [copies.start(slope_in.at[m], slope.at[m]) for m in range(sz.mem)]
     block = sz.hid // sz.devs
     mine = lax.axis_index("core")
     load_h = []
@@ -471,19 +481,18 @@
     copies.finish([load_b])
     for m in range(sz.mem):
         for prow in range(sz.prows):
-            for q in range(sz.parts):
-                rows_f[q] = back[prow * sz.parts + q, m].astype(F32)
+            parts = range(prow * sz.parts, (prow + 1) * sz.parts)
+            for q in parts:
+                rows_f[m, q] = back[q, m].astype(F32)
             for group in range(sz.groups):
-                outs = swap_blocks(
-                    [rows_f[q, pl.ds(group * sz.ch, sz.ch), :] for q in range(sz.parts)]
-                )
+                outs = swap_blocks([rows_f[m, q, pl.ds(group * sz.ch, sz.ch), :] for q in parts])
                 for i, out in enumerate(outs):
                     row = prow * 8 + group * sz.parts + i
                     gp[m, :, row * width : (row + 1) * width] = out.astype(BF16)
         for pair in range(sz.lat // 2):
             here = slice(pair * 2 * width, (pair + 1) * 2 * width)
-            if here.start % quarter == 0:
-                copies.finish([load_s[m * 4 + here.start // quarter]])
+            if pair == 0:
+                copies.finish([load_s[m]])
             dhid = jnp.dot(wpt[...], gp[m, :, here], preferred_element_type=F32)
             gpre[m, :, here] = (dhid * slope[m, :, here].astype(F32)).astype(BF16)
     def store(at, term):
@@ -494,29 +503,23 @@
     copies.finish()
 
 
-def own_kernel(sz, gpre, hid, ext, gp, own):
+def own_kernel(sz, gpre, hid, ext, gp, wt3, own, edge_up, edge_dn):
     def store(at, term):
         own[:, at : at + term.shape[1]] = term
 
     weight_sums(sz, lax.axis_index("core"), gpre, hid, ext, gp, store)
+    for side, edge in enumerate((edge_up, edge_dn)):
+        at = 0 if side == 0 else sz.pos - sz.lon
+        cols = [gpre[m, :, at : at + sz.lon] for m in range(sz.mem)]
+        part = jnp.dot(
+            wt3[2 * side], jnp.concatenate(cols, axis=1), preferred_element_type=F32
+        )
+        for m in range(sz.mem):
+            edge[m] = fold_taps(part[:, m * sz.lon : (m + 1) * sz.lon], sz.ch)
 
 
 def merge_kernel(own, other, out):
     out[...] = (own[...] + other[...].astype(F32)).astype(BF16)
-
-
-def edge_terms_kernel(sz, gpre, wt3_in, edge_up, edge_dn, gv, wt3, sems):
-    width = sz.lon
-    copies = Copies(sems)
-    for side in range(2):
-        at = slice(0, width) if side == 0 else slice(sz.pos - width, sz.pos)
-        copies.start(wt3_in.at[2 * side], wt3.at[side])
-        copies.start(gpre.at[:, :, at], gv.at[side])
-    copies.finish()
-    for side, edge in enumerate((edge_up, edge_dn)):
-        for m in range(sz.mem):
-            part = jnp.dot(wt3[side], gv[side, m], preferred_element_type=F32)
-            edge[m] = fold_taps(part, sz.ch)
 
 
 def data_kernel(sz, gpre_in, gp_in, wt3_in, ov, ev, gpre, gp, wt3, gs, sems):
@@ -534,7 +537,7 @@
     zero = jnp.zeros((sz.hid, width), BF16)
     copies.finish([load_w])
     for m in range(sz.mem):
-        copies.finish([loads[2 * m], load_p[m]])
+        copies.finish(loads[2 * m : 2 * m + 2] + [load_p[m]])
 
         def two_rows(first):
             low, high = max(first, 0), min(first + 2, sz.lat)
@@ -546,8 +549,6 @@
             return cols[0] if len(cols) == 1 else jnp.concatenate(cols, axis=1)
 
         for pair in range(sz.lat // 2):
-            if (pair * 2 + 3) * width > half:
-                copies.finish([loads[2 * m + 1]])
             part = None
             for ro in range(3):
                 term = jnp.dot(wt3[ro], two_rows(pair * 2 + 1 - ro), preferred_element_type=F32)
@@ -643,7 +644,7 @@
             both_bf,
             both_f,
             pltpu.VMEM((9 * ch, hid), BF16),
-            pltpu.VMEM((ch, pos), F32),
+            pltpu.VMEM((mem, ch, pos), F32),
             pltpu.VMEM((2,) + pair_shape, F32),
             wide_bf,
             wide_bf,
@@ -651,8 +652,8 @@
             pltpu.VMEM((mem, ch, pos), F32),
             pltpu.VMEM((hid, 3 * TAPS), BF16),
             pltpu.VMEM((3, TAPS, hid), BF16),
-            flat,
-            taps_row,
+            pltpu.VMEM((mem, ch * lat, lon), F32),
+            pltpu.VMEM((4, TAPS, lon), F32),
             dma(3 + 4 * mem + mem * lat // 2),
         ],
         conv_flops,
@@ -667,7 +668,7 @@
         "rim",
         [(wide, BF16), (wide, BF16), (ext_shape, BF16), (part_shape, BF16)],
         [
-            pltpu.VMEM((2,) + pair_shape, F32),
+            pltpu.VMEM((units,) + pair_shape, F32),
             pltpu.VMEM((units,) + pair_shape, BF16),
             pltpu.VMEM((units,) + pair_shape, BF16),
             pltpu.VMEM((mem, sz.devs, sz.subpad, LANES), BF16),
@@ -676,11 +677,11 @@
             pltpu.VMEM((mem, ch, pos), F32),
             pltpu.VMEM((hid, 3 * TAPS), BF16),
             pltpu.VMEM(w_proj.shape, BF16),
-            pltpu.VMEM((TAPS, 2 * lon), F32),
-            pltpu.VMEM((2, ch, 2 * lon), F32),
-            taps_row,
-            regroup_rows,
-            pltpu.VMEM((mem * ch, lon), F32),
+            pltpu.VMEM((units, TAPS, 2 * lon), F32),
+            pltpu.VMEM((units, ch, 2 * lon), F32),
+            pltpu.VMEM((units, TAPS, lon), F32),
+            pltpu.VMEM((mem, sz.devs, sz.subpad, LANES), F32),
+            pltpu.VMEM((2, mem * ch, lon), F32),
             dma(7 + 2 * units + 2 * mem),
         ],
         conv_flops // 4,
@@ -756,9 +757,9 @@
             pltpu.VMEM(part_shape, BF16),
             pltpu.VMEM((mem, hid, pos), BF16),
             pltpu.VMEM((mem, hid // 2, pos), BF16),
-            regroup_rows,
+            pltpu.VMEM((mem, sz.devs, sz.subpad, LANES), F32),
             pltpu.VMEM((hid, ch), BF16),
-            dma(1 + 4 * mem + mem * sz.devs),
+            dma(1 + mem + mem * sz.devs),
         ],
         conv_flops,
         9_000_000,
@@ -768,16 +769,16 @@
         limit=40,
     )
     swapped = lax.ppermute(sibling, "core", [(0, 1), (1, 0)])
-    (own,) = call(
+    own, edge_up, edge_dn = call(
         functools.partial(own_kernel, sz),
         "own",
-        [(half, F32)],
+        [(half, F32), (edge_shape, F32), (edge_shape, F32)],
         [],
         conv_flops // 2,
         9_000_000,
-        (grad_pre, hid_own, ext, grad_pred),
-        vmem=range(4),
-        vmem_outs=(0,),
+        (grad_pre, hid_own, ext, grad_pred, wt3),
+        vmem=range(5),
+        vmem_outs=range(3),
         limit=16,
     )
     (partial,) = call(
@@ -797,22 +798,7 @@
     terms = lax.all_to_all(
         partial.reshape(shards // 2, each, sz.cols), ("pair", "band"), 0, 0, tiled=True
     )
-    late_wt3, _ = lax.optimization_barrier((wt3, partial))
-    edge_up, edge_dn = call(
-        functools.partial(edge_terms_kernel, sz),
-        "edge_terms",
-        [(edge_shape, F32), (edge_shape, F32)],
-        [
-            pltpu.VMEM((2, mem, hid, lon), BF16),
-            pltpu.VMEM((2, TAPS, hid), BF16),
-            dma(4),
-        ],
-        200_000_000,
-        1_500_000,
-        (grad_pre, late_wt3),
-        vmem_outs=(0, 1),
-        limit=60,
-    )
+    edge_up, edge_dn, late_wt3, _ = lax.optimization_barrier((edge_up, edge_dn, wt3, partial))
     from_dn = lax.ppermute(edge_up, "band", up)
     from_up = lax.ppermute(edge_dn, "band", down)
 

time: 107 us -> 105 us (0.981)
  Pallas kernels: 45 us -> 41.1 us
  local copies, waits for them, and re-layouts: 6.09 us -> 7.2 us
    pallas_call x12 -> x11, Pallas kernels: 41.7 us -> 37.9 us  [call(): pl.pallas_call(kernel, in_specs=[specs[kind(i)] for i in range(len(args))...]
    unnamed x20 -> x24, local copies, waits for them, and re-layouts: 6.09 us -> 7.2 us
  transfers between devices with their start and end apart: 7 -> 7, of which waited for: 3 -> 4; matrix products, arithmetic and copies ran while one was open for 0% -> 0% of each run, Pallas kernels for 24% -> 21%
where the time goes in v7:
time: 105 us; the launch traced here: 104 us
  Pallas kernels  41.1 us (39%)
  waiting for transfers between devices  30.5 us (29%)
  starting transfers between devices  24.1 us (23%)
  local copies, waits for them, and re-layouts  7.2 us (7%)
    pallas_call x11, Pallas kernels, call(): pl.pallas_call(kernel, in_specs=[specs[kind(i)] for i in range(len(args))...  37.9 us
    all_to_all x1, waiting for transfers between devices, on_device(): preds = lax.all_to_all(snd, MEMBER, 0, 0, tiled=True)  18.1 us
    all_to_all x1, waiting for transfers between devices, on_device(): back = lax.all_to_all(grads, MEMBER, 0, 0, tiled=True)  11.2 us
    unnamed x24, local copies, waits for them, and re-layouts  7.2 us
    all_to_all x1, starting transfers between devices, on_device(): halos = lax.all_to_all(send, 'band', 0, 0, tiled=True)  5.2 us
    all_to_all x1, starting transfers between devices, on_device(): lax.all_to_all(partial.reshape(shards // 2, each, sz.cols), ('pair', 'ban...  5.05 us
    all_to_all x1, starting transfers between devices, on_device(): preds = lax.all_to_all(snd, MEMBER, 0, 0, tiled=True)  4.89 us
    ppermute x1, starting transfers between devices, on_device(): from_up = lax.ppermute(edge_dn, 'band', down)  3.82 us
  transfers between devices with their start and end apart: 7, of which 4 were waited for; matrix products, arithmetic and copies ran while one was open for 0% of the time, Pallas kernels for 21%

profile of v7, /device:TPU:0, one launch (start us, length us, event | category | flops | bytes accessed | tf_op | source)
XLA Modules:
  0.0 103.8 jit_solution(10758528789689137845)
XLA Ops:
  0.6 2.4 %edges.1 = bf16[4,168,128]{2,1,0:T(8,128)(2,1)} custom-call(bf16[2,84,16,128]{3,2,1,0:T(8,128)(2,1)} %states.3, f32[2,84,16,128]{3,2,1,0:T(8,128)} %noise.3), custom_call_target="tpu_custom_call" | custom-call | flops 1000000 | bytes 3000000 | tf_op jit(solution)/shard_map/edges/pallas_call | solution.py:29
  3.0 5.2 %all-to-all-start = ((bf16[4,168,128]{2,1,0:T(8,128)(2,1)}), bf16[4,168,128]{2,1,0:T(8,128)(2,1)S(1)}, u32[]{:S(2)}, u32[]{:S(2)}) async-start(bf16[4,168,128]{2,1,0:T(8,128)(2,1)} %edges.1), calls=%async_computation | async-start | bytes 344064 | tf_op jit(solution)/shard_map/all_to_all | solution.py:628
  8.2 0.0 copy-start.10
  8.2 8.6 %front.1 = (bf16[2,512,2048]{2,1,0:T(8,128)(2,1)}, bf16[2,512,2048]{2,1,0:T(8,128)(2,1)}, bf16[2,256,2304]{2,1,0:T(8,128)(2,1)}, f32[2,84,2048]{2,1,0:T(8,128)},...) custom-call(bf16[2,84,16,128]{3,2,1,0:T(8,128)(2,1)} %states.3, f32[2,84,16,128]{3,2,1,0:T(8,128)} %noise.3, ...), custom_call_target="tpu_custom_call" | custom-call | flops 3221225472 | bytes 9000000 | tf_op jit(solution)/shard_map/front/pallas_call | solution.py:29
  16.9 0.0 all-to-all-done.halos_in
  16.9 0.0 copy-done.10
  16.9 0.0 copy-start.9
  16.9 0.0 copy-start.11
  16.9 5.5 %rim.1 = (bf16[2,512,2048]{2,1,0:T(8,128)(2,1)}, bf16[2,512,2048]{2,1,0:T(8,128)(2,1)}, bf16[2,256,2304]{2,1,0:T(8,128)(2,1)}, bf16[8,2,168,128]{3,2,1,0:T(8,128)(2,1)}) custom-call(bf16[4,168,128]{2,1,0:T(8,128)(2,1)S(1)} %all-to-all-done.halos_in, ...), custom_call_target="tpu_custom_call", output_to_operand_aliasing={{0}: (1, {}), {1}: (2, {}), {2}: (3, {})} | custom-call | flops 805306368 | bytes 9000000 | tf_op jit(solution)/shard_map/rim/pallas_call | solution.py:29
  22.4 4.9 %all-to-all-start.1 = ((bf16[8,2,168,128]{3,2,1,0:T(8,128)(2,1)}), bf16[8,2,168,128]{3,2,1,0:T(8,128)(2,1)S(1)}, u32[]{:S(2)}, u32[]{:S(2)}) async-start(bf16[8,2,168,128]{3,2,1,0:T(8,128)(2,1)} %get-tuple-element.33), calls=%async_computation.1 | async-start | bytes 1376256 | tf_op jit(solution)/shard_map/all_to_all | solution.py:694
  27.3 0.0 copy-done.9
  27.3 0.7 truth.1
  28.0 18.1 %all-to-all-done.1.preds = bf16[8,2,168,128]{3,2,1,0:T(8,128)(2,1)S(1)} async-done(((bf16[8,2,168,128]{3,2,1,0:T(8,128)(2,1)}), bf16[8,2,168,128]{3,2,1,0:T(8,128)(2,1)S(1)}, u32[]{:S(2)}, u32[]{:S(2)}) %all-to-all-start.1) | async-done | bytes 688160 | tf_op jit(solution)/shard_map/all_to_all | solution.py:694
  46.1 0.0 copy-done.11
  46.1 3.8 %pairs.1 = bf16[8,2,168,128]{3,2,1,0:T(8,128)(2,1)} custom-call(s32[4,16]{1,0:T(4,128)S(1)} %copy-done.11, bf16[8,2,168,128]{3,2,1,0:T(8,128)(2,1)S(1)} %all-to-all-done.1.preds, bf16[8,168,128]{2,1,0:T(8,128)(2,1)S(1)} %truth.1), custom_call_target="tpu_custom_call" | custom-call | flops 10321920 | bytes 2000000 | tf_op jit(solution)/shard_map/pairs/pallas_call | solution.py:29
  49.9 3.7 %all-to-all-start.2 = ((bf16[8,2,168,128]{3,2,1,0:T(8,128)(2,1)}), bf16[8,2,168,128]{3,2,1,0:T(8,128)(2,1)S(1)}, u32[]{:S(2)}, u32[]{:S(2)}) async-start(bf16[8,2,168,128]{3,2,1,0:T(8,128)(2,1)} %pairs.1), calls=%async_computation.2 | async-start | bytes 1376256 | tf_op jit(solution)/shard_map/all_to_all | solution.py:743
  53.7 0.0 copy-start
  53.7 2.2 %copy-done = bf16[2,512,2048]{2,1,0:T(8,128)(2,1)S(1)} copy-done((bf16[2,512,2048]{2,1,0:T(8,128)(2,1)S(1)}, bf16[2,512,2048]{2,1,0:T(8,128)(2,1)}, u32[]{:S(2)}) %copy-start) | copy-done | bytes 4194328
  55.8 0.0 copy-start.1
  55.8 3.3 %slope.1.slope_in = bf16[2,512,2048]{2,1,0:T(8,128)(2,1)S(1)} custom-call(bf16[2,512,2048]{2,1,0:T(8,128)(2,1)S(1)} %copy-done), custom_call_target="tpu_custom_call" | custom-call | flops 20971520 | bytes 16777216 | tf_op jit(solution)/shard_map/slope/pallas_call | solution.py:709
  59.1 0.0 copy-start.3
  59.1 1.9 %copy-done.3 = bf16[2,512,2048]{2,1,0:T(8,128)(2,1)} copy-done((bf16[2,512,2048]{2,1,0:T(8,128)(2,1)}, bf16[2,512,2048]{2,1,0:T(8,128)(2,1)S(1)}, u32[]{:S(2)}) %copy-start.3) | copy-done | bytes 4194328
  61.1 11.2 %all-to-all-done.2.back_in = bf16[8,2,168,128]{3,2,1,0:T(8,128)(2,1)S(1)} async-done(((bf16[8,2,168,128]{3,2,1,0:T(8,128)(2,1)}), bf16[8,2,168,128]{3,2,1,0:T(8,128)(2,1)S(1)}, u32[]{:S(2)}, u32[]{:S(2)}) %all-to-all-start.2) | async-done | bytes 688160 | tf_op jit(solution)/shard_map/all_to_all | solution.py:743
  72.2 0.0 copy-start.7
  72.2 0.8 copy-done.7
  73.1 0.0 copy-done.1
  73.1 0.0 copy-start.8
  73.1 1.1 %copy-done.8 = bf16[8,2,168,128]{3,2,1,0:T(8,128)(2,1)S(1)} copy-done((bf16[8,2,168,128]{3,2,1,0:T(8,128)(2,1)S(1)}, bf16[8,2,168,128]{3,2,1,0:T(8,128)(2,1)}, u32[]{:S(2)}) %copy-start.8) | copy-done | bytes 688152
  74.2 0.0 copy-start.4
  74.2 5.8 %sibling.1 = (bf16[2,84,2048]{2,1,0:T(8,128)(2,1)S(1)}, bf16[2,512,2048]{2,1,0:T(8,128)(2,1)S(1)}, bf16[2,256,2048]{2,1,0:T(8,128)(2,1)S(1)}, bf16[256,896]{1,0:T(8,128)(2,1)S(1)}) custom-call(bf16[8,2,168,128]{3,2,1,0:T(8,128)(2,1)S(1)} %copy-done.8, bf16[2,512,2048]{2,1,0:T(8,128)(2,1)} %copy-done.3, bf16[2,512,2048]{2,1,0:T(8,128)(2,1)} %get-tuple-element.36.hid_in, ...), custom_call_target="tpu_custom_call" | custom-call | flops 3221225472 | bytes 9000000 | tf_op jit(solution)/shard_map/sibling/pallas_call | solution.py:29
  80.0 0.0 copy-start.2
  80.0 0.0 copy-start.5
  80.0 0.1 collective-permute-start
  80.1 0.0 copy-done.4
  80.1 2.6 %own.1 = (f32[256,896]{1,0:T(8,128)S(1)}, f32[2,84,128]{2,1,0:T(8,128)S(1)}, f32[2,84,128]{2,1,0:T(8,128)S(1)}) custom-call(bf16[2,512,2048]{2,1,0:T(8,128)(2,1)S(1)} %get-tuple-element.38.gpre.gpre_in, bf16[2,256,2048]{2,1,0:T(8,128)(2,1)S(1)} %get-tuple-element.40.hid, bf16[2,256,2304]{2,1,0:T(8,128)(2,1)S(1)} %copy-done.1, ...), custom_call_target="tpu_custom_call" | custom-call | flops 1610612736 | bytes 9000000 | tf_op jit(solution)/shard_map/own/pallas_call | solution.py:29
  82.7 0.0 copy-done.2
  82.7 0.0 copy-done.5
  82.7 0.0 collective-permute-done.other
  82.8 0.9 merge.1
  83.6 5.1 %all-to-all-start.3 = ((bf16[16,16,896]{2,1,0:T(8,128)(2,1)}), bf16[16,16,896]{2,1,0:T(8,128)(2,1)S(1)}, u32[]{:S(2)}, u32[]{:S(2)}) async-start(bf16[16,16,896]{2,1,0:T(8,128)(2,1)} %bitcast.1), calls=%async_computation.3 | async-start | bytes 917504 | tf_op jit(solution)/shard_map/all_to_all | solution.py:798
  88.7 3.8 %collective-permute-start.1 = (f32[2,84,128]{2,1,0:T(8,128)S(1)}, f32[2,84,128]{2,1,0:T(8,128)S(1)}, u32[]{:S(2)}, u32[]{:S(2)}) collective-permute-start(f32[2,84,128]{2,1,0:T(8,128)S(1)} %get-tuple-element.49), channel_id=1, source_target_pairs={{0,1},{1,2},{2,3},{4,5},{5,6},{6,7},{8,9},{9,10},{10,11},{12,13},{... | collective-permute-start | bytes 258056 | tf_op jit(solution)/shard_map/ppermute | solution.py:803
  92.5 1.3 %collective-permute-start.2 = (f32[2,84,128]{2,1,0:T(8,128)S(1)}, f32[2,84,128]{2,1,0:T(8,128)S(1)}, u32[]{:S(2)}, u32[]{:S(2)}) collective-permute-start(f32[2,84,128]{2,1,0:T(8,128)S(1)} %get-tuple-element.50), channel_id=1, source_target_pairs={{1,0},{2,1},{3,2},{5,4},{6,5},{7,6},{9,8},{10,9},{11,10},{13,12},{... | collective-permute-start | bytes 258056 | tf_op jit(solution)/shard_map/ppermute | solution.py:802
  93.8 0.0 copy-start.6
  93.8 1.1 %copy-done.6 = bf16[2,84,2048]{2,1,0:T(8,128)(2,1)S(1)} copy-done((bf16[2,84,2048]{2,1,0:T(8,128)(2,1)S(1)}, bf16[2,84,2048]{2,1,0:T(8,128)(2,1)}, u32[]{:S(2)}) %copy-start.6) | copy-done | bytes 688152
  94.9 5.9 %data.1 = (bf16[2,84,16,128]{3,2,1,0:T(8,128)(2,1)S(1)}, f32[2,2,84,128]{3,2,1,0:T(8,128)S(1)}) custom-call(bf16[2,512,2048]{2,1,0:T(8,128)(2,1)} %copy-done.2, bf16[2,84,2048]{2,1,0:T(8,128)(2,1)S(1)} %copy-done.6, bf16[3,256,512]{2,1,0:T(8,128)(2,1)S(1)} %copy-done.4), custom_call_target="tpu_custom_call" | custom-call | flops 3221225472 | bytes 8000000 | tf_op jit(solution)/shard_map/data/pallas_call | solution.py:29
  100.8 0.0 collective-permute-done.1.uv
  100.8 0.4 collective-permute-done.2.dv
  101.2 1.0 border.1
  102.2 0.8 all-to-all-done.3.terms
  103.0 0.7 final.1
Async XLA Ops:
  3.0 13.8 %all-to-all-start = ((bf16[4,168,128]{2,1,0:T(8,128)(2,1)}), bf16[4,168,128]{2,1,0:T(8,128)(2,1)S(1)}, u32[]{:S(2)}, u32[]{:S(2)}) async-start(bf16[4,168,128]{2,1,0:T(8,128)(2,1)} %edges.1), calls=%async_computation | async-start | bytes 344064 | tf_op jit(solution)/shard_map/all_to_all | solution.py:628
  8.2 8.7 %copy-start.10 = (bf16[84,512]{1,0:T(8,128)(2,1)S(1)}, bf16[84,512]{1,0:T(8,128)(2,1)}, u32[]{:S(2)}) copy-start(bf16[84,512]{1,0:T(8,128)(2,1)} %w_proj.3) | copy-start | bytes 258052
  16.9 10.4 %copy-start.9 = (bf16[84,16,128]{2,1,0:T(8,128)(2,1)S(1)}, bf16[84,16,128]{2,1,0:T(8,128)(2,1)}, u32[]{:S(2)}) copy-start(bf16[84,16,128]{2,1,0:T(8,128)(2,1)} %target) | copy-start | bytes 1032196
  16.9 29.2 %copy-start.11 = (s32[4,16]{1,0:T(4,128)S(1)}, s32[4,16]{1,0:T(4,128)}, u32[]{:S(2)}) copy-start(s32[4,16]{1,0:T(4,128)} %match.1) | copy-start | bytes 772
  22.4 23.7 %all-to-all-start.1 = ((bf16[8,2,168,128]{3,2,1,0:T(8,128)(2,1)}), bf16[8,2,168,128]{3,2,1,0:T(8,128)(2,1)S(1)}, u32[]{:S(2)}, u32[]{:S(2)}) async-start(bf16[8,2,168,128]{3,2,1,0:T(8,128)(2,1)} %get-tuple-element.33), calls=%async_computation.1 | async-start | bytes 1376256 | tf_op jit(solution)/shard_map/all_to_all | solution.py:694
  49.9 22.3 %all-to-all-start.2 = ((bf16[8,2,168,128]{3,2,1,0:T(8,128)(2,1)}), bf16[8,2,168,128]{3,2,1,0:T(8,128)(2,1)S(1)}, u32[]{:S(2)}, u32[]{:S(2)}) async-start(bf16[8,2,168,128]{3,2,1,0:T(8,128)(2,1)} %pairs.1), calls=%async_computation.2 | async-start | bytes 1376256 | tf_op jit(solution)/shard_map/all_to_all | solution.py:743
  53.7 2.2 %copy-start = (bf16[2,512,2048]{2,1,0:T(8,128)(2,1)S(1)}, bf16[2,512,2048]{2,1,0:T(8,128)(2,1)}, u32[]{:S(2)}) copy-start(bf16[2,512,2048]{2,1,0:T(8,128)(2,1)} %get-tuple-element.35.preact) | copy-start | bytes 12582916
  55.8 17.2 %copy-start.1 = (bf16[2,256,2304]{2,1,0:T(8,128)(2,1)S(1)}, bf16[2,256,2304]{2,1,0:T(8,128)(2,1)}, u32[]{:S(2)}) copy-start(bf16[2,256,2304]{2,1,0:T(8,128)(2,1)} %get-tuple-element.37.ext) | copy-start | bytes 7077892
  59.1 1.9 %copy-start.3 = (bf16[2,512,2048]{2,1,0:T(8,128)(2,1)}, bf16[2,512,2048]{2,1,0:T(8,128)(2,1)S(1)}, u32[]{:S(2)}) copy-start(bf16[2,512,2048]{2,1,0:T(8,128)(2,1)S(1)} %slope.1.slope_in) | copy-start | bytes 12582916
  72.2 0.8 copy-start.7
  73.1 1.1 %copy-start.8 = (bf16[8,2,168,128]{3,2,1,0:T(8,128)(2,1)S(1)}, bf16[8,2,168,128]{3,2,1,0:T(8,128)(2,1)}, u32[]{:S(2)}) copy-start(bf16[8,2,168,128]{3,2,1,0:T(8,128)(2,1)} %copy-done.7) | copy-start | bytes 2064388
  74.2 5.9 %copy-start.4 = (bf16[3,256,512]{2,1,0:T(8,128)(2,1)S(1)}, bf16[3,256,512]{2,1,0:T(8,128)(2,1)}, u32[]{:S(2)}) copy-start(bf16[3,256,512]{2,1,0:T(8,128)(2,1)} %get-tuple-element.46.wt3.wt3_in) | copy-start | bytes 2359300
  80.0 2.7 %copy-start.2 = (bf16[2,512,2048]{2,1,0:T(8,128)(2,1)}, bf16[2,512,2048]{2,1,0:T(8,128)(2,1)S(1)}, u32[]{:S(2)}) copy-start(bf16[2,512,2048]{2,1,0:T(8,128)(2,1)S(1)} %get-tuple-element.38.gpre.gpre_in) | copy-start | bytes 12582916
  80.0 2.7 %copy-start.5 = (bf16[2,84,2048]{2,1,0:T(8,128)(2,1)}, bf16[2,84,2048]{2,1,0:T(8,128)(2,1)S(1)}, u32[]{:S(2)}) copy-start(bf16[2,84,2048]{2,1,0:T(8,128)(2,1)S(1)} %get-tuple-element.39.gp.gp_in) | copy-start | bytes 2064388
  80.0 2.7 %collective-permute-start = (bf16[256,896]{1,0:T(8,128)(2,1)S(1)}, bf16[256,896]{1,0:T(8,128)(2,1)S(1)}, u32[]{:S(2)}, u32[]{:S(2)}) collective-permute-start(bf16[256,896]{1,0:T(8,128)(2,1)S(1)} %get-tuple-element.45), channel_id=1, source_target_pairs={{0,4},{4,0},{1,5},{5,1},{2,6},{6,2},{3,7},{7,3},{8,12},{12,8},{9,1... | collective-permute-start | bytes 1376264 | tf_op jit(solution)/shard_map/ppermute | solution.py:771
  83.6 19.4 %all-to-all-start.3 = ((bf16[16,16,896]{2,1,0:T(8,128)(2,1)}), bf16[16,16,896]{2,1,0:T(8,128)(2,1)S(1)}, u32[]{:S(2)}, u32[]{:S(2)}) async-start(bf16[16,16,896]{2,1,0:T(8,128)(2,1)} %bitcast.1), calls=%async_computation.3 | async-start | bytes 917504 | tf_op jit(solution)/shard_map/all_to_all | solution.py:798
  88.7 12.1 %collective-permute-start.1 = (f32[2,84,128]{2,1,0:T(8,128)S(1)}, f32[2,84,128]{2,1,0:T(8,128)S(1)}, u32[]{:S(2)}, u32[]{:S(2)}) collective-permute-start(f32[2,84,128]{2,1,0:T(8,128)S(1)} %get-tuple-element.49), channel_id=1, source_target_pairs={{0,1},{1,2},{2,3},{4,5},{5,6},{6,7},{8,9},{9,10},{10,11},{12,13},{... | collective-permute-start | bytes 258056 | tf_op jit(solution)/shard_map/ppermute | solution.py:803
  92.5 8.7 %collective-permute-start.2 = (f32[2,84,128]{2,1,0:T(8,128)S(1)}, f32[2,84,128]{2,1,0:T(8,128)S(1)}, u32[]{:S(2)}, u32[]{:S(2)}) collective-permute-start(f32[2,84,128]{2,1,0:T(8,128)S(1)} %get-tuple-element.50), channel_id=1, source_target_pairs={{1,0},{2,1},{3,2},{5,4},{6,5},{7,6},{9,8},{10,9},{11,10},{13,12},{... | collective-permute-start | bytes 258056 | tf_op jit(solution)/shard_map/ppermute | solution.py:802
  93.8 1.1 %copy-start.6 = (bf16[2,84,2048]{2,1,0:T(8,128)(2,1)S(1)}, bf16[2,84,2048]{2,1,0:T(8,128)(2,1)}, u32[]{:S(2)}) copy-start(bf16[2,84,2048]{2,1,0:T(8,128)(2,1)} %copy-done.5) | copy-start | bytes 2064388
